TPU v7x, 256 devices: a whole 4x4x8 slice. The times are simulated.
256 devices in a mesh: chan: 64 (over z, y, x_hi), grp: 4 (over x_lo, core).
Axes of the slice: x: 4 (x_hi: 2, x_lo: 2; x = x_hi * 2 + x_lo), y: 4, z: 8, core: 2. Of those that a mesh axis runs over, the one named last changes fastest.
Arguments:
- gate_up: bfloat16 [4096, 2, 28672], P('grp', None, 'chan'), may hold values from -6 to 6
- counts: int32 [4], P('grp'), may hold values from 512 to 1024
- panels: int32 [2, 512], replicated, may hold values from 0 to 28671, as said below
- inverses: float32 [2, 512, 512], replicated
- down_weight: bfloat16 [28672, 8192], P('chan', 'grp'), may hold values from -6 to 6
Outputs:
- pruned_weight: bfloat16 [28672, 8192], P('chan', 'grp')
Inputs may be any that keep to these rules, and one draw needn't show every extreme that they name: `panels`: the entries 512 // 64 * s to 512 // 64 * (s + 1) - 1 of each panel lie in channels s * (28672 // 64) to (s + 1) * (28672 // 64) - 1; all 1024 indices are different.
All inputs are finite; a program needn't handle non-finite values.
Results may differ from a plain program's by a relative error of at most 0.0051.
Values may be sent and summed in bfloat16 or wider, within the bound.
No kernel may reach another device: no remote copies, remote signals or barrier semaphores. Data moves between devices by JAX's collectives and lax.ppermute only.
A program may use at most 64 MiB of HBM per device.

v0:
```python
import jax
import jax.numpy as jnp
from jax import lax
from jax.sharding import Mesh, PartitionSpec as P


BF16 = jnp.bfloat16
F32 = jnp.float32
NT = (((1,), (1,)), ((), ()))


def shift(x, axis, by):
    n = lax.axis_size(axis)
    return lax.ppermute(x, axis, [(i, (i + by) % n) for i in range(n)])


def to_all(x, axes):
    n = lax.axis_size(axes)
    return lax.all_to_all(jnp.broadcast_to(x, (n, *x.shape)), axes, split_axis=0, concat_axis=0, tiled=True)


def place(pieces, axis, dim):
    n, me = lax.axis_size(axis), lax.axis_index(axis)
    shape = list(pieces[0][1].shape)
    shape.insert(dim, n)
    out = jnp.zeros(tuple(shape), pieces[0][1].dtype)
    for back, piece in pieces:
        at = [0] * len(shape)
        at[dim] = (me - back) % n
        out = lax.dynamic_update_slice(out, jnp.expand_dims(piece, dim), at)
    return out


def gather_rows(rows):
    other = shift(rows, "xh", 1)
    both = place([(0, rows), (1, other)], "xh", 1)
    others = [(k, shift(both, "y", k)) for k in (1, 3, 2)]
    around = place([(0, both)] + others, "y", 1)
    return around.reshape(2, 64, rows.shape[-1])


def ring_z(block):
    pieces = [(0, block)]
    ahead, behind = block, block
    for step in (1, 2, 3):
        ahead, behind = shift(ahead, "z", 1), shift(behind, "z", -1)
        pieces += [(step, ahead), (8 - step, behind)]
    half = block.shape[-1] // 2
    ahead, behind = ahead[..., :half], behind[..., half:]
    ahead, behind = shift(ahead, "z", 1), shift(behind, "z", -1)
    far = jnp.concatenate([ahead, behind], axis=-1)
    pieces.append((4, far))
    return place(pieces, "z", 1).reshape(2, 512, block.shape[-1])


def compute(gate_up, counts, panels, inverses, down_weight):
    tokens, _, local = gate_up.shape
    panel = panels.shape[1]
    columns = down_weight.shape[1]
    share = panel // 64
    shard = lax.axis_index("z") * 8 + lax.axis_index("y") * 2 + lax.axis_index("xh")
    zero = lax.axis_index("co") == 0
    mine = lax.dynamic_slice(panels, (0, shard * share), (2, share)).reshape(-1) - shard * local
    onehot = mine[:, None] == jnp.arange(local, dtype=jnp.int32)[None, :]
    select = onehot.astype(BF16)

    rows = jnp.dot(select, down_weight, preferred_element_type=F32).astype(BF16)

    slot = jnp.arange(tokens, dtype=jnp.int32)
    valid = (slot < counts[0]).astype(F32)
    gate = gate_up[:, 0, :].astype(F32)
    up = gate_up[:, 1, :].astype(F32)
    hidden = (jax.nn.silu(gate) * up * valid[:, None]).astype(BF16)
    acts = lax.dot_general(select, hidden, NT, preferred_element_type=F32).astype(BF16)

    acts = to_all(acts, "z").reshape(128, tokens)
    near = gather_rows(rows.reshape(2, share, columns))
    acts = to_all(acts, ("y", "xh"))
    acts = acts.reshape(8, 8, 2, share, tokens).transpose(2, 1, 0, 3, 4).reshape(2, panel, tokens)
    rows_all = ring_z(near).reshape(2 * panel, columns)

    tens = jnp.arange(8, dtype=jnp.int32)[:, None] == 0
    count = jnp.where(tens, counts[0] // 32, counts[0] % 32).astype(F32)
    count = jnp.broadcast_to(count, (8, panel))

    left = jnp.concatenate([hidden.T, acts[1]], axis=0)
    first = lax.dot_general(left, acts[0], NT, preferred_element_type=F32)
    second = lax.dot_general(left[:local], acts[1], NT, preferred_element_type=F32)
    half, cross_half = local // 2, panel // 2

    def part(k):
        return jnp.concatenate(
            [
                first[k * half : (k + 1) * half],
                second[k * half : (k + 1) * half],
                first[local + k * cross_half : local + (k + 1) * cross_half],
                count,
            ],
            axis=0,
        )

    keep = jnp.where(zero, part(0), part(1))
    give = jnp.where(zero, part(1), part(0)).astype(BF16)
    given = shift(give, "co", 1)
    keep = keep + given.astype(F32)
    give = keep.astype(BF16)
    given = shift(give, "xl", 1)
    keep = keep + given.astype(F32)
    rows_in_half = 2 * half + cross_half
    scale = 1.0 / (32.0 * keep[rows_in_half, 0] + keep[rows_in_half + 1, 0])
    keep = keep[:rows_in_half] * scale
    give = keep.astype(BF16)
    given = shift(give, "co", 1)
    other = given.astype(F32)
    low, top = jnp.where(zero, keep, other), jnp.where(zero, other, keep)
    first_hess = jnp.concatenate([low[:half], top[:half]], axis=0)
    second_hess = jnp.concatenate([low[half : 2 * half], top[half : 2 * half]], axis=0)
    cross = jnp.concatenate([low[2 * half :], top[2 * half :]], axis=0)

    mid = lax.Precision.HIGH
    second_gain = jnp.dot(second_hess, inverses[1], precision=mid)
    first_gain = jnp.dot(first_hess - jnp.dot(second_gain, cross, precision=mid), inverses[0], precision=mid)
    gain = jnp.concatenate([first_gain, second_gain], axis=1).astype(BF16)

    gone = jnp.any(onehot, axis=0)[:, None]
    new = down_weight.astype(F32) - jnp.dot(gain, rows_all, preferred_element_type=F32)
    return jnp.where(gone, 0.0, new).astype(BF16)


def solution(mesh):
    fine = Mesh(mesh.devices.reshape(8, 4, 2, 2, 2), ("z", "y", "xh", "xl", "co"))
    chan, grp = ("z", "y", "xh"), ("xl", "co")
    in_specs = (P(grp, None, chan), P(grp), P(), P(), P(chan, grp))
    return jax.shard_map(compute, mesh=fine, in_specs=in_specs, out_specs=P(chan, grp), check_vma=False)
```

profile of v0, /device:TPU:1, one launch (start us, length us, event | category | flops | bytes accessed | tf_op | source)
XLA Modules:
  0.0 103.8 jit_solution(6374631010941737170)
XLA Ops:
  1.0 1.9 %bitcast_dynamic-update-slice_fusion.10 = (bf16[2,2,8,2048]{3,2,1,0:T(8,128)(2,1)S(1)}, bf16[16,2048]{1,0:T(8,128)(2,1)S(1)}) fusion(bf16[2,2,8,2048]{3,2,1,0:T(8,128)(2,1)S(1)} %broadcast_in_dim.90, s32[]{:T(128)S(6)} %select_n.160, bf16[448,2048]{1,0:T(8,128)(2,1)} %param.9, s32[16]{0:T(128)S(1)} %sub.58), kind=kOutput, calls=%fused_computation.70 | convolution fusion | flops 29400064 | bytes 1966596 | tf_op jit(solution)/shard_map/dot_general | solution.py:67
  2.9 3.6 %collective-permute-start.3 = (bf16[2,8,2048]{2,1,0:T(8,128)(2,1)S(1)}, bf16[2,8,2048]{2,1,0:T(8,128)(2,1)S(1)}, u32[]{:S(2)}, u32[]{:S(2)}) collective-permute-start(bf16[2,8,2048]{2,1,0:T(8,128)(2,1)S(1)} %bitcast.131), channel_id=1, source_target_pairs={{0,4},{4,0},{1,5},{5,1},{2,6},{6,2},{3,7},{7,3},{8,12},{12,8},{9,1... | collective-permute-start | bytes 196616 | tf_op jit(solution)/shard_map/ppermute | solution.py:14
  8.6 8.2 %all-to-all-start = ((bf16[8,16,1024]{2,1,0:T(8,128)(2,1)}), bf16[8,16,1024]{2,1,0:T(8,128)(2,1)S(1)}, u32[]{:S(2)}, u32[]{:S(2)}) async-start(bf16[8,16,1024]{2,1,0:T(8,128)(2,1)} %broadcast_in_dim.83), calls=%async_computation | async-start | bytes 524288 | tf_op jit(solution)/shard_map/all_to_all | solution.py:19
  17.0 1.4 %collective-permute-start.4 = (bf16[2,2,8,2048]{3,2,1,0:T(8,128)(2,1)S(1)}, bf16[2,2,8,2048]{3,2,1,0:T(8,128)(2,1)S(1)}, u32[]{:S(2)}, u32[]{:S(2)}) collective-permute-start(bf16[2,2,8,2048]{3,2,1,0:T(8,128)(2,1)S(1)} %bitcast_dynamic-update-slice_fusion.11), channel_id=1, source_target_pairs={{0,8},{8,16},{16,24},{24,0},{1,9},{9,17},{17,25},{25,1},{2,10},{10... | collective-permute-start | bytes 393224 | tf_op jit(solution)/shard_map/ppermute | solution.py:14
  18.4 1.5 %collective-permute-start.5 = (bf16[2,2,8,2048]{3,2,1,0:T(8,128)(2,1)S(1)}, bf16[2,2,8,2048]{3,2,1,0:T(8,128)(2,1)S(1)}, u32[]{:S(2)}, u32[]{:S(2)}) collective-permute-start(bf16[2,2,8,2048]{3,2,1,0:T(8,128)(2,1)S(1)} %bitcast_dynamic-update-slice_fusion.11), channel_id=1, source_target_pairs={{0,24},{8,0},{16,8},{24,16},{1,25},{9,1},{17,9},{25,17},{2,26},{10... | collective-permute-start | bytes 393224 | tf_op jit(solution)/shard_map/ppermute | solution.py:14
  19.9 1.6 %collective-permute-start.6 = (bf16[2,2,8,2048]{3,2,1,0:T(8,128)(2,1)S(1)}, bf16[2,2,8,2048]{3,2,1,0:T(8,128)(2,1)S(1)}, u32[]{:S(2)}, u32[]{:S(2)}) collective-permute-start(bf16[2,2,8,2048]{3,2,1,0:T(8,128)(2,1)S(1)} %bitcast_dynamic-update-slice_fusion.11), channel_id=1, source_target_pairs={{0,16},{8,24},{16,0},{24,8},{1,17},{9,25},{17,1},{25,9},{2,18},{10... | collective-permute-start | bytes 393224 | tf_op jit(solution)/shard_map/ppermute | solution.py:14
  21.5 5.5 %all-to-all-done = bf16[8,16,1024]{2,1,0:T(8,128)(2,1)S(1)} async-done(((bf16[8,16,1024]{2,1,0:T(8,128)(2,1)}), bf16[8,16,1024]{2,1,0:T(8,128)(2,1)S(1)}, u32[]{:S(2)}, u32[]{:S(2)}) %all-to-all-start) | async-done | bytes 262176 | tf_op jit(solution)/shard_map/all_to_all | solution.py:19
  27.0 1.6 %broadcast_in_dim.84 = bf16[8,128,1024]{2,1,0:T(8,128)(2,1)} broadcast(bf16[128,1024]{1,0:T(8,128)(2,1)S(1)} %bitcast.127), dimensions={1,2} | broadcast | bytes 2359296 | tf_op jit(solution)/shard_map/broadcast_in_dim | solution.py:19
  28.7 4.2 %all-to-all-start.1 = ((bf16[8,128,1024]{2,1,0:T(8,128)(2,1)}), bf16[8,128,1024]{2,1,0:T(8,128)(2,1)S(1)}, u32[]{:S(2)}, u32[]{:S(2)}) async-start(bf16[8,128,1024]{2,1,0:T(8,128)(2,1)} %broadcast_in_dim.84), calls=%async_computation.1 | async-start | bytes 4194304 | tf_op jit(solution)/shard_map/all_to_all | solution.py:19
  33.0 2.7 %collective-permute-start.8 = (bf16[2,64,2048]{2,1,0:T(8,128)(2,1)S(1)}, bf16[2,64,2048]{2,1,0:T(8,128)(2,1)}, u32[]{:S(2)}, u32[]{:S(2)}) collective-permute-start(bf16[2,64,2048]{2,1,0:T(8,128)(2,1)S(1)} %bitcast.125), channel_id=1, source_target_pairs={{0,224},{32,0},{64,32},{96,64},{128,96},{160,128},{192,160},{224,1... | collective-permute-start | bytes 1572872 | tf_op jit(solution)/shard_map/ppermute | solution.py:14
  35.7 2.1 %fusion.69 = bf16[448,1024]{1,0:T(8,128)(2,1)S(1)} fusion(f32[1024]{0:T(1024)S(1)} %fusion.45, bf16[1024,2,448]{0,2,1:T(8,128)(2,1)} %param.5), kind=kLoop, calls=%fused_computation.98 | loop fusion | flops 4128768 | bytes 2756608 | tf_op jit(solution)/shard_map/transpose | solution.py:86
  38.4 6.6 %collective-permute-done.7 = bf16[2,64,2048]{2,1,0:T(8,128)(2,1)} collective-permute-done((bf16[2,64,2048]{2,1,0:T(8,128)(2,1)S(1)}, bf16[2,64,2048]{2,1,0:T(8,128)(2,1)}, u32[]{:S(2)}, u32[]{:S(2)}) %collective-permute-start.7) | collective-permute-done | bytes 524320 | tf_op jit(solution)/shard_map/ppermute | solution.py:14
  45.0 2.7 %collective-permute-start.10 = (bf16[2,64,2048]{2,1,0:T(8,128)(2,1)}, bf16[2,64,2048]{2,1,0:T(8,128)(2,1)S(1)}, u32[]{:S(2)}, u32[]{:S(2)}) collective-permute-start(bf16[2,64,2048]{2,1,0:T(8,128)(2,1)} %collective-permute-done.8), channel_id=1, source_target_pairs={{0,224},{32,0},{64,32},{96,64},{128,96},{160,128},{192,160},{224,1... | collective-permute-start | bytes 1572872 | tf_op jit(solution)/shard_map/ppermute | solution.py:14
  47.6 10.6 %all-to-all-done.1 = bf16[8,128,1024]{2,1,0:T(8,128)(2,1)S(1)} async-done(((bf16[8,128,1024]{2,1,0:T(8,128)(2,1)}), bf16[8,128,1024]{2,1,0:T(8,128)(2,1)S(1)}, u32[]{:S(2)}, u32[]{:S(2)}) %all-to-all-start.1) | async-done | bytes 2097184 | tf_op jit(solution)/shard_map/all_to_all | solution.py:19
  58.6 1.3 %copy-done.5 = bf16[1024,2,448]{0,2,1:T(8,128)(2,1)S(1)} copy-done((bf16[1024,2,448]{0,2,1:T(8,128)(2,1)S(1)}, bf16[1024,2,448]{0,2,1:T(8,128)(2,1)}, u32[]{:S(2)}) %copy-start.5) | copy-done | bytes 1835032
  60.8 1.2 %fusion.2 = f32[960,512]{1,0:T(8,128)S(1)} fusion(bf16[512,1024]{1,0:T(8,128)(2,1)S(1)} %bitcast.128, bf16[512,1024]{1,0:T(8,128)(2,1)S(1)} %bitcast.130, bf16[448,1024]{1,0:T(8,128)(2,1)S(1)} %fusion.69), kind=kOutput, calls=%fused_computation.9 | convolution fusion | flops 1010565120 | bytes 4980736 | tf_op jit(solution)/shard_map/dot_general | solution.py:87
  62.5 4.1 %collective-permute-start = (bf16[712,512]{1,0:T(8,128)(2,1)S(1)}, bf16[712,512]{1,0:T(8,128)(2,1)S(1)}, u32[]{:S(2)}, u32[]{:S(2)}) collective-permute-start(bf16[712,512]{1,0:T(8,128)(2,1)S(1)} %select_convert_fusion.1), channel_id=1, source_target_pairs={{0,1},{1,0},{2,3},{3,2},{4,5},{5,4},{6,7},{7,6},{8,9},{9,8},{10,11... | collective-permute-start | bytes 2187272 | tf_op jit(solution)/shard_map/ppermute | solution.py:14
  66.6 1.1 %bitcast_dynamic-update-slice_fusion.5 = bf16[2,8,64,2048]{3,2,1,0:T(8,128)(2,1)S(1)} fusion(bf16[2,8,64,2048]{3,2,1,0:T(8,128)(2,1)S(1)} %copy-done.1, s32[]{:T(128)S(6)} %select_n.174, bf16[2,64,2048]{2,1,0:T(8,128)(2,1)} %collective-permute-done.7), kind=kLoop, calls=%fused_computation.65 | loop fusion | bytes 1048580 | tf_op jit(solution)/shard_map/dynamic_update_slice | solution.py:30
  67.7 1.1 %bitcast_dynamic-update-slice_fusion.4 = bf16[2,8,64,2048]{3,2,1,0:T(8,128)(2,1)S(1)} fusion(bf16[2,8,64,2048]{3,2,1,0:T(8,128)(2,1)S(1)} %bitcast_dynamic-update-slice_fusion.5, s32[]{:T(128)S(6)} %select_n.176, bf16[2,64,2048]{2,1,0:T(8,128)(2,1)} %collective-permute-done.8), kind=kLoop, calls=%fused_computation.64 | loop fusion | bytes 1048580 | tf_op jit(solution)/shard_map/dynamic_update_slice | solution.py:30
  69.1 2.7 %collective-permute-start.12 = (bf16[2,64,2048]{2,1,0:T(8,128)(2,1)S(1)}, bf16[2,64,2048]{2,1,0:T(8,128)(2,1)S(1)}, u32[]{:S(2)}, u32[]{:S(2)}) collective-permute-start(bf16[2,64,2048]{2,1,0:T(8,128)(2,1)S(1)} %collective-permute-done.10), channel_id=1, source_target_pairs={{0,224},{32,0},{64,32},{96,64},{128,96},{160,128},{192,160},{224,1... | collective-permute-start | bytes 1572872 | tf_op jit(solution)/shard_map/ppermute | solution.py:14
  72.1 1.2 %collective-permute-start.1 = (bf16[712,512]{1,0:T(8,128)(2,1)S(1)}, bf16[712,512]{1,0:T(8,128)(2,1)S(1)}, u32[]{:S(2)}, u32[]{:S(2)}) collective-permute-start(bf16[712,512]{1,0:T(8,128)(2,1)S(1)} %get-tuple-element.5), channel_id=1, source_target_pairs={{0,2},{2,0},{1,3},{3,1},{4,6},{6,4},{5,7},{7,5},{8,10},{10,8},{9,1... | collective-permute-start | bytes 2187272 | tf_op jit(solution)/shard_map/ppermute | solution.py:14
  73.3 1.1 %bitcast_dynamic-update-slice_fusion.3 = bf16[2,8,64,2048]{3,2,1,0:T(8,128)(2,1)S(1)} fusion(bf16[2,8,64,2048]{3,2,1,0:T(8,128)(2,1)S(1)} %bitcast_dynamic-update-slice_fusion.4, s32[]{:T(128)S(6)} %select_n.178, bf16[2,64,2048]{2,1,0:T(8,128)(2,1)} %collective-permute-done.9), kind=kLoop, calls=%fused_computation.63 | loop fusion | bytes 1048580 | tf_op jit(solution)/shard_map/dynamic_update_slice | solution.py:30
  74.5 6.6 %collective-permute-done.12 = bf16[2,64,2048]{2,1,0:T(8,128)(2,1)S(1)} collective-permute-done((bf16[2,64,2048]{2,1,0:T(8,128)(2,1)S(1)}, bf16[2,64,2048]{2,1,0:T(8,128)(2,1)S(1)}, u32[]{:S(2)}, u32[]{:S(2)}) %collective-permute-start.12) | collective-permute-done | bytes 524320 | tf_op jit(solution)/shard_map/ppermute | solution.py:14
  81.0 3.5 %collective-permute-start.14 = (bf16[2,64,1024]{2,1,0:T(8,128)(2,1)S(1)}, bf16[2,64,1024]{2,1,0:T(8,128)(2,1)S(1)}, u32[]{:S(2)}, u32[]{:S(2)}) collective-permute-start(bf16[2,64,1024]{2,1,0:T(8,128)(2,1)S(1)} %slice.119), channel_id=1, source_target_pairs={{0,224},{32,0},{64,32},{96,64},{128,96},{160,128},{192,160},{224,1... | collective-permute-start | bytes 786440 | tf_op jit(solution)/shard_map/ppermute | solution.py:14
  84.7 3.1 %collective-permute-done.1 = bf16[712,512]{1,0:T(8,128)(2,1)S(1)} collective-permute-done((bf16[712,512]{1,0:T(8,128)(2,1)S(1)}, bf16[712,512]{1,0:T(8,128)(2,1)S(1)}, u32[]{:S(2)}, u32[]{:S(2)}) %collective-permute-start.1) | collective-permute-done | bytes 729120 | tf_op jit(solution)/shard_map/ppermute | solution.py:14
  90.0 3.2 %collective-permute-start.2 = (bf16[704,512]{1,0:T(8,128)(2,1)S(1)}, bf16[704,512]{1,0:T(8,128)(2,1)S(1)}, u32[]{:S(2)}, u32[]{:S(2)}) collective-permute-start(bf16[704,512]{1,0:T(8,128)(2,1)S(1)} %fusion.17), channel_id=1, source_target_pairs={{0,1},{1,0},{2,3},{3,2},{4,5},{5,4},{6,7},{7,6},{8,9},{9,8},{10,11... | collective-permute-start | bytes 2162696 | tf_op jit(solution)/shard_map/ppermute | solution.py:14
  93.4 1.6 %collective-permute-done.2 = bf16[704,512]{1,0:T(8,128)(2,1)S(1)} collective-permute-done((bf16[704,512]{1,0:T(8,128)(2,1)S(1)}, bf16[704,512]{1,0:T(8,128)(2,1)S(1)}, u32[]{:S(2)}, u32[]{:S(2)}) %collective-permute-start.2) | collective-permute-done | bytes 720928 | tf_op jit(solution)/shard_map/ppermute | solution.py:14
  95.6 1.4 %copy-done.2 = f32[2,512,512]{2,1,0:T(8,128)S(1)} copy-done((f32[2,512,512]{2,1,0:T(8,128)S(1)}, f32[2,512,512]{2,1,0:T(8,128)}, u32[]{:S(2)}) %copy-start.2) | copy-done | bytes 2097176
  97.1 0.9 fusion.62
  98.0 0.9 fusion.18
  99.0 1.0 convolution_convert_fusion.1
  100.4 3.3 %select_convert_fusion = bf16[448,2048]{1,0:T(8,128)(2,1)} fusion(bf16[448,2048]{1,0:T(8,128)(2,1)S(1)} %copy-done.3, bf16[1024,2048]{1,0:T(8,128)(2,1)S(1)} %bitcast.123, pred[448]{0:T(512)(128)(4,1)S(1)} %fusion.42, bf16[448,512]{1,0:T(8,128)(2,1)S(1)} %get-tuple-element.25, bf16[448,512]{1,0:T(8,128)(2,1)S(1)} %convolution_convert_fusion.1), kind=kOutput, calls=%fused_computation | convolution fusion | flops 1884553216 | bytes 8782272 | tf_op jit(solution)/shard_map/dot_general | solution.py:126
  (64 shorter events, 8.0 us)
Async XLA Ops:
  0.0 7.1 %copy-start.4 = (bf16[1024,2,448]{0,2,1:T(8,128)(2,1)S(1)}, bf16[1024,2,448]{0,2,1:T(8,128)(2,1)}, u32[]{:S(2)}) copy-start(bf16[1024,2,448]{0,2,1:T(8,128)(2,1)} %param.5) | copy-start | bytes 5505028
  2.9 14.1 %collective-permute-start.3 = (bf16[2,8,2048]{2,1,0:T(8,128)(2,1)S(1)}, bf16[2,8,2048]{2,1,0:T(8,128)(2,1)S(1)}, u32[]{:S(2)}, u32[]{:S(2)}) collective-permute-start(bf16[2,8,2048]{2,1,0:T(8,128)(2,1)S(1)} %bitcast.131), channel_id=1, source_target_pairs={{0,4},{4,0},{1,5},{5,1},{2,6},{6,2},{3,7},{7,3},{8,12},{12,8},{9,1... | collective-permute-start | bytes 196616 | tf_op jit(solution)/shard_map/ppermute | solution.py:14
  8.6 18.4 %all-to-all-start = ((bf16[8,16,1024]{2,1,0:T(8,128)(2,1)}), bf16[8,16,1024]{2,1,0:T(8,128)(2,1)S(1)}, u32[]{:S(2)}, u32[]{:S(2)}) async-start(bf16[8,16,1024]{2,1,0:T(8,128)(2,1)} %broadcast_in_dim.83), calls=%async_computation | async-start | bytes 524288 | tf_op jit(solution)/shard_map/all_to_all | solution.py:19
  17.0 15.9 %collective-permute-start.4 = (bf16[2,2,8,2048]{3,2,1,0:T(8,128)(2,1)S(1)}, bf16[2,2,8,2048]{3,2,1,0:T(8,128)(2,1)S(1)}, u32[]{:S(2)}, u32[]{:S(2)}) collective-permute-start(bf16[2,2,8,2048]{3,2,1,0:T(8,128)(2,1)S(1)} %bitcast_dynamic-update-slice_fusion.11), channel_id=1, source_target_pairs={{0,8},{8,16},{16,24},{24,0},{1,9},{9,17},{17,25},{25,1},{2,10},{10... | collective-permute-start | bytes 393224 | tf_op jit(solution)/shard_map/ppermute | solution.py:14
  18.4 14.5 %collective-permute-start.5 = (bf16[2,2,8,2048]{3,2,1,0:T(8,128)(2,1)S(1)}, bf16[2,2,8,2048]{3,2,1,0:T(8,128)(2,1)S(1)}, u32[]{:S(2)}, u32[]{:S(2)}) collective-permute-start(bf16[2,2,8,2048]{3,2,1,0:T(8,128)(2,1)S(1)} %bitcast_dynamic-update-slice_fusion.11), channel_id=1, source_target_pairs={{0,24},{8,0},{16,8},{24,16},{1,25},{9,1},{17,9},{25,17},{2,26},{10... | collective-permute-start | bytes 393224 | tf_op jit(solution)/shard_map/ppermute | solution.py:14
  19.9 13.0 %collective-permute-start.6 = (bf16[2,2,8,2048]{3,2,1,0:T(8,128)(2,1)S(1)}, bf16[2,2,8,2048]{3,2,1,0:T(8,128)(2,1)S(1)}, u32[]{:S(2)}, u32[]{:S(2)}) collective-permute-start(bf16[2,2,8,2048]{3,2,1,0:T(8,128)(2,1)S(1)} %bitcast_dynamic-update-slice_fusion.11), channel_id=1, source_target_pairs={{0,16},{8,24},{16,0},{24,8},{1,17},{9,25},{17,1},{25,9},{2,18},{10... | collective-permute-start | bytes 393224 | tf_op jit(solution)/shard_map/ppermute | solution.py:14
  28.7 29.6 %all-to-all-start.1 = ((bf16[8,128,1024]{2,1,0:T(8,128)(2,1)}), bf16[8,128,1024]{2,1,0:T(8,128)(2,1)S(1)}, u32[]{:S(2)}, u32[]{:S(2)}) async-start(bf16[8,128,1024]{2,1,0:T(8,128)(2,1)} %broadcast_in_dim.84), calls=%async_computation.1 | async-start | bytes 4194304 | tf_op jit(solution)/shard_map/all_to_all | solution.py:19
  32.9 12.0 %collective-permute-start.7 = (bf16[2,64,2048]{2,1,0:T(8,128)(2,1)S(1)}, bf16[2,64,2048]{2,1,0:T(8,128)(2,1)}, u32[]{:S(2)}, u32[]{:S(2)}) collective-permute-start(bf16[2,64,2048]{2,1,0:T(8,128)(2,1)S(1)} %bitcast.124), channel_id=1, source_target_pairs={{0,32},{32,64},{64,96},{96,128},{128,160},{160,192},{192,224},{224... | collective-permute-start | bytes 1572872 | tf_op jit(solution)/shard_map/ppermute | solution.py:14
  33.0 11.9 %collective-permute-start.8 = (bf16[2,64,2048]{2,1,0:T(8,128)(2,1)S(1)}, bf16[2,64,2048]{2,1,0:T(8,128)(2,1)}, u32[]{:S(2)}, u32[]{:S(2)}) collective-permute-start(bf16[2,64,2048]{2,1,0:T(8,128)(2,1)S(1)} %bitcast.125), channel_id=1, source_target_pairs={{0,224},{32,0},{64,32},{96,64},{128,96},{160,128},{192,160},{224,1... | collective-permute-start | bytes 1572872 | tf_op jit(solution)/shard_map/ppermute | solution.py:14
  38.4 6.6 %copy-start = (bf16[2,8,64,2048]{3,2,1,0:T(8,128)(2,1)}, bf16[2,8,64,2048]{3,2,1,0:T(8,128)(2,1)S(1)}, u32[]{:S(2)}) copy-start(bf16[2,8,64,2048]{3,2,1,0:T(8,128)(2,1)S(1)} %constant_dynamic-update-slice_fusion) | copy-start | bytes 12582916
  45.0 23.8 %collective-permute-start.9 = (bf16[2,64,2048]{2,1,0:T(8,128)(2,1)}, bf16[2,64,2048]{2,1,0:T(8,128)(2,1)}, u32[]{:S(2)}, u32[]{:S(2)}) collective-permute-start(bf16[2,64,2048]{2,1,0:T(8,128)(2,1)} %collective-permute-done.7), channel_id=1, source_target_pairs={{0,32},{32,64},{64,96},{96,128},{128,160},{160,192},{192,224},{224... | collective-permute-start | bytes 1572872 | tf_op jit(solution)/shard_map/ppermute | solution.py:14
  45.0 24.1 %collective-permute-start.10 = (bf16[2,64,2048]{2,1,0:T(8,128)(2,1)}, bf16[2,64,2048]{2,1,0:T(8,128)(2,1)S(1)}, u32[]{:S(2)}, u32[]{:S(2)}) collective-permute-start(bf16[2,64,2048]{2,1,0:T(8,128)(2,1)} %collective-permute-done.8), channel_id=1, source_target_pairs={{0,224},{32,0},{64,32},{96,64},{128,96},{160,128},{192,160},{224,1... | collective-permute-start | bytes 1572872 | tf_op jit(solution)/shard_map/ppermute | solution.py:14
  58.4 1.5 %copy-start.5 = (bf16[1024,2,448]{0,2,1:T(8,128)(2,1)S(1)}, bf16[1024,2,448]{0,2,1:T(8,128)(2,1)}, u32[]{:S(2)}) copy-start(bf16[1024,2,448]{0,2,1:T(8,128)(2,1)} %param.5) | copy-start | bytes 5505028
  62.1 4.5 %copy-start.1 = (bf16[2,8,64,2048]{3,2,1,0:T(8,128)(2,1)S(1)}, bf16[2,8,64,2048]{3,2,1,0:T(8,128)(2,1)}, u32[]{:S(2)}) copy-start(bf16[2,8,64,2048]{3,2,1,0:T(8,128)(2,1)} %copy-done) | copy-start | bytes 12582916
  62.5 9.2 %collective-permute-start = (bf16[712,512]{1,0:T(8,128)(2,1)S(1)}, bf16[712,512]{1,0:T(8,128)(2,1)S(1)}, u32[]{:S(2)}, u32[]{:S(2)}) collective-permute-start(bf16[712,512]{1,0:T(8,128)(2,1)S(1)} %select_convert_fusion.1), channel_id=1, source_target_pairs={{0,1},{1,0},{2,3},{3,2},{4,5},{5,4},{6,7},{7,6},{8,9},{9,8},{10,11... | collective-permute-start | bytes 2187272 | tf_op jit(solution)/shard_map/ppermute | solution.py:14
  68.8 15.8 %collective-permute-start.11 = (bf16[2,64,2048]{2,1,0:T(8,128)(2,1)}, bf16[2,64,2048]{2,1,0:T(8,128)(2,1)S(1)}, u32[]{:S(2)}, u32[]{:S(2)}) collective-permute-start(bf16[2,64,2048]{2,1,0:T(8,128)(2,1)} %collective-permute-done.9), channel_id=1, source_target_pairs={{0,32},{32,64},{64,96},{96,128},{128,160},{160,192},{192,224},{224... | collective-permute-start | bytes 1572872 | tf_op jit(solution)/shard_map/ppermute | solution.py:14
  69.1 12.0 %collective-permute-start.12 = (bf16[2,64,2048]{2,1,0:T(8,128)(2,1)S(1)}, bf16[2,64,2048]{2,1,0:T(8,128)(2,1)S(1)}, u32[]{:S(2)}, u32[]{:S(2)}) collective-permute-start(bf16[2,64,2048]{2,1,0:T(8,128)(2,1)S(1)} %collective-permute-done.10), channel_id=1, source_target_pairs={{0,224},{32,0},{64,32},{96,64},{128,96},{160,128},{192,160},{224,1... | collective-permute-start | bytes 1572872 | tf_op jit(solution)/shard_map/ppermute | solution.py:14
  72.1 15.7 %collective-permute-start.1 = (bf16[712,512]{1,0:T(8,128)(2,1)S(1)}, bf16[712,512]{1,0:T(8,128)(2,1)S(1)}, u32[]{:S(2)}, u32[]{:S(2)}) collective-permute-start(bf16[712,512]{1,0:T(8,128)(2,1)S(1)} %get-tuple-element.5), channel_id=1, source_target_pairs={{0,2},{2,0},{1,3},{3,1},{4,6},{6,4},{5,7},{7,5},{8,10},{10,8},{9,1... | collective-permute-start | bytes 2187272 | tf_op jit(solution)/shard_map/ppermute | solution.py:14
  81.0 12.2 %collective-permute-start.14 = (bf16[2,64,1024]{2,1,0:T(8,128)(2,1)S(1)}, bf16[2,64,1024]{2,1,0:T(8,128)(2,1)S(1)}, u32[]{:S(2)}, u32[]{:S(2)}) collective-permute-start(bf16[2,64,1024]{2,1,0:T(8,128)(2,1)S(1)} %slice.119), channel_id=1, source_target_pairs={{0,224},{32,0},{64,32},{96,64},{128,96},{160,128},{192,160},{224,1... | collective-permute-start | bytes 786440 | tf_op jit(solution)/shard_map/ppermute | solution.py:14
  84.6 8.7 %collective-permute-start.13 = (bf16[2,64,1024]{2,1,0:T(8,128)(2,1)S(1)}, bf16[2,64,1024]{2,1,0:T(8,128)(2,1)S(1)}, u32[]{:S(2)}, u32[]{:S(2)}) collective-permute-start(bf16[2,64,1024]{2,1,0:T(8,128)(2,1)S(1)} %slice.118), channel_id=1, source_target_pairs={{0,32},{32,64},{64,96},{96,128},{128,160},{160,192},{192,224},{224... | collective-permute-start | bytes 786440 | tf_op jit(solution)/shard_map/ppermute | solution.py:14
  90.0 5.0 %collective-permute-start.2 = (bf16[704,512]{1,0:T(8,128)(2,1)S(1)}, bf16[704,512]{1,0:T(8,128)(2,1)S(1)}, u32[]{:S(2)}, u32[]{:S(2)}) collective-permute-start(bf16[704,512]{1,0:T(8,128)(2,1)S(1)} %fusion.17), channel_id=1, source_target_pairs={{0,1},{1,0},{2,3},{3,2},{4,5},{5,4},{6,7},{7,6},{8,9},{9,8},{10,11... | collective-permute-start | bytes 2162696 | tf_op jit(solution)/shard_map/ppermute | solution.py:14
  95.5 1.6 %copy-start.2 = (f32[2,512,512]{2,1,0:T(8,128)S(1)}, f32[2,512,512]{2,1,0:T(8,128)}, u32[]{:S(2)}) copy-start(f32[2,512,512]{2,1,0:T(8,128)} %param.8) | copy-start | bytes 6291460
  98.9 1.5 %copy-start.3 = (bf16[448,2048]{1,0:T(8,128)(2,1)S(1)}, bf16[448,2048]{1,0:T(8,128)(2,1)}, u32[]{:S(2)}) copy-start(bf16[448,2048]{1,0:T(8,128)(2,1)} %param.9) | copy-start | bytes 5505028
where the time goes:
time: 104 us
  starting transfers between devices  40.9 us (39%)
  waiting for transfers between devices  34 us (33%)
  local copies, waits for them, and re-layouts  11.2 us (11%)
  matrix products  10.9 us (10%)
  other arithmetic  4.49 us (4%)
  between operations  2.34 us (2%)
    ppermute x15, starting transfers between devices, shift(): return lax.ppermute(x, axis, [(i, (i + by) % n) for i in range(n)])  28.5 us
    ppermute x15, waiting for transfers between devices, shift(): return lax.ppermute(x, axis, [(i, (i + by) % n) for i in range(n)])  17.9 us
    all_to_all x2, waiting for transfers between devices, to_all(): lax.all_to_all(jnp.broadcast_to(x, (n, *x.shape)), axes, split_axis=0, co...  16.1 us
    all_to_all x2, starting transfers between devices, to_all(): lax.all_to_all(jnp.broadcast_to(x, (n, *x.shape)), axes, split_axis=0, co...  12.4 us
    dynamic_update_slice x12, local copies, waits for them, and re-layouts, place(): out = lax.dynamic_update_slice(out, jnp.expand_dims(piece, dim), at)  3.52 us
    dot_general x1, matrix products, compute(): jnp.dot(gain, rows_all, preferred_element_type=F32)  3.34 us
    unnamed x12, local copies, waits for them, and re-layouts  3.28 us
    broadcast_in_dim x2, local copies, waits for them, and re-layouts, to_all(): jnp.broadcast_to(x, (n, *x.shape))  2.36 us
  transfers between devices with their start and end apart: 17, of which 6 were waited for; matrix products, arithmetic and copies ran while one was open for 13% of the time, Pallas kernels for 0%

commit v1 on v0

v1 whole, which is shorter than its diff:
```python
import functools

import jax
import jax.numpy as jnp
from jax import lax
from jax.experimental import pallas as pl
from jax.experimental.pallas import tpu as pltpu
from jax.sharding import Mesh, PartitionSpec as P


BF16 = jnp.bfloat16
F32 = jnp.float32
NT = (((1,), (1,)), ((), ()))
VMEM = pl.BlockSpec(memory_space=pltpu.VMEM)
SMEM = pl.BlockSpec(memory_space=pltpu.SMEM)
HBM = pl.BlockSpec(memory_space=pltpu.HBM)


def shift(x, axis, by):
    n = lax.axis_size(axis)
    return lax.ppermute(x, axis, [(i, (i + by) % n) for i in range(n)])


def to_all(x, axes):
    n = lax.axis_size(axes)
    return lax.all_to_all(jnp.broadcast_to(x, (n, *x.shape)), axes, split_axis=0, concat_axis=0, tiled=True)


def place(pieces, axis, dim):
    n, me = lax.axis_size(axis), lax.axis_index(axis)
    shape = list(pieces[0][1].shape)
    shape.insert(dim, n)
    out = jnp.zeros(tuple(shape), pieces[0][1].dtype)
    for back, piece in pieces:
        at = [0] * len(shape)
        at[dim] = (me - back) % n
        out = lax.dynamic_update_slice(out, jnp.expand_dims(piece, dim), at)
    return out


def gather_rows(rows):
    other = shift(rows, "xh", 1)
    both = place([(0, rows), (1, other)], "xh", 1)
    others = [(k, shift(both, "y", k)) for k in (1, 3, 2)]
    around = place([(0, both)] + others, "y", 1)
    return around.reshape(2, 64, rows.shape[-1])


def ring_z(block):
    pieces = [(0, block)]
    ahead, behind = block, block
    for step in (1, 2, 3):
        ahead, behind = shift(ahead, "z", 1), shift(behind, "z", -1)
        pieces += [(step, ahead), (8 - step, behind)]
    half = block.shape[-1] // 2
    ahead, behind = ahead[..., :half], behind[..., half:]
    ahead, behind = shift(ahead, "z", 1), shift(behind, "z", -1)
    return pieces + [(4, ahead), (4, behind)]


def far(x):
    return pltpu.with_memory_space_constraint(x, pltpu.HBM)


def dot(a, b):
    return jnp.dot(a, b, preferred_element_type=F32)


def dot_nt(a, b):
    return lax.dot_general(a, b, NT, preferred_element_type=F32)


def partial_kernel(core_ref, count_ref, hidden_ref, acts_ref, keep_ref, give_ref):
    half, cross = hidden_ref.shape[0] // 2, acts_ref.shape[1] // 2
    core = core_ref[0]
    count = count_ref[0]
    high = lax.broadcasted_iota(jnp.int32, (8, acts_ref.shape[1]), 0) == 0
    counts = jnp.where(high, count // 32, count % 32).astype(F32)
    for mine, ref in ((core, keep_ref), (1 - core, give_ref)):
        hidden = hidden_ref[pl.ds(pl.multiple_of(mine * half, 32), half), :]
        second = acts_ref[1, pl.ds(pl.multiple_of(mine * cross, 32), cross), :]
        ref[pl.ds(0, half), :] = dot_nt(hidden, acts_ref[0]).astype(ref.dtype)
        ref[pl.ds(half, half), :] = dot_nt(hidden, acts_ref[1]).astype(ref.dtype)
        ref[pl.ds(2 * half, cross), :] = dot_nt(second, acts_ref[0]).astype(ref.dtype)
        ref[pl.ds(2 * half + cross, 8), :] = counts.astype(ref.dtype)


def join_kernel(keep_ref, given_ref, out_ref, give_ref):
    rows = out_ref.shape[0]
    counts = keep_ref[pl.ds(rows, 8), :] + given_ref[pl.ds(rows, 8), :].astype(F32)
    scale = 1.0 / (32.0 * counts[0:1, :] + counts[1:2, :])
    joined = (keep_ref[pl.ds(0, rows), :] + given_ref[pl.ds(0, rows), :].astype(F32)) * scale
    out_ref[...] = joined
    give_ref[...] = joined.astype(BF16)


def split(x):
    high = x.astype(BF16)
    return high, (x - high.astype(F32)).astype(BF16)


def dot3(a, b):
    return dot(a[0], b[0]) + (dot(a[0], b[1]) + dot(a[1], b[0]))


def tail_kernel(
    backs, at_ref, keep_ref, given_ref, inv_ref, stay_ref, *refs
):
    pieces, (old_ref, out_ref, inv_buf, rows_ref, old_buf, new_buf, gain_ref, inv_sems, sems, old_sem, new_sems) = (
        refs[: len(backs)], refs[len(backs):]
    )
    zero, z = at_ref[0] == 0, at_ref[1]
    depth, columns = pieces[0].shape[1:]
    panel = inv_ref.shape[1]
    copies = []
    for i, (back, piece) in enumerate(zip(backs, pieces)):
        width = piece.shape[2]
        left = columns - width if i == len(backs) - 1 else 0
        row = pl.multiple_of(lax.rem(z + 8 - back, 8) * depth, depth)
        for p in range(2):
            copies.append(
                pltpu.make_async_copy(
                    piece.at[p],
                    rows_ref.at[p, pl.ds(row, depth), pl.ds(left, width)],
                    sems.at[i, p],
                )
            )
    old_copy = pltpu.make_async_copy(old_ref, old_buf, old_sem)
    inv_copies = [pltpu.make_async_copy(inv_ref.at[p], inv_buf.at[p], inv_sems.at[p]) for p in (1, 0)]
    for copy in inv_copies:
        copy.start()
    for copy in copies:
        copy.start()
    old_copy.start()

    keep, given = keep_ref[...], given_ref[...].astype(F32)
    low, top = jnp.where(zero, keep, given), jnp.where(zero, given, keep)
    half = old_ref.shape[0] // 2
    for copy in inv_copies:
        copy.wait()
    first_inv, second_inv = split(inv_buf[0]), split(inv_buf[1])
    cross = split(jnp.concatenate([low[2 * half :], top[2 * half :]], axis=0))
    for k, part in enumerate((low, top)):
        second = dot3(split(part[half : 2 * half]), second_inv)
        first = dot3(split(part[:half] - dot3(split(second), cross)), first_inv)
        gain_ref[pl.ds(k * half, half), pl.ds(0, panel)] = first.astype(BF16)
        gain_ref[pl.ds(k * half, half), pl.ds(panel, panel)] = second.astype(BF16)

    for copy in copies:
        copy.wait()
    old_copy.wait()
    stay = stay_ref[...] > 0.0
    gain = gain_ref[...]
    chunks = new_sems.shape[0]
    width = columns // chunks
    outs = []
    for c in range(chunks):
        at = pl.ds(c * width, width)
        change = dot(gain[:, :panel], rows_ref[0, :, at]) + dot(gain[:, panel:], rows_ref[1, :, at])
        new = jnp.where(stay, old_buf[:, at].astype(F32) - change, 0.0)
        new_buf[:, at] = new.astype(BF16)
        outs.append(pltpu.make_async_copy(new_buf.at[:, at], out_ref.at[:, at], new_sems.at[c]))
        outs[-1].start()
    for copy in outs:
        copy.wait()


def compute(gate_up, counts, panels, inverses, down_weight):
    tokens, _, local = gate_up.shape
    panel = panels.shape[1]
    columns = down_weight.shape[1]
    share = panel // 64
    shard = lax.axis_index("z") * 8 + lax.axis_index("y") * 2 + lax.axis_index("xh")
    core = lax.axis_index("co").astype(jnp.int32)
    mine = lax.dynamic_slice(panels, (0, shard * share), (2, share)).reshape(-1) - shard * local
    onehot = mine[:, None] == jnp.arange(local, dtype=jnp.int32)[None, :]
    select = onehot.astype(BF16)

    rows = jnp.dot(select, down_weight, preferred_element_type=F32).astype(BF16)

    slot = jnp.arange(tokens, dtype=jnp.int32)
    valid = (slot < counts[0]).astype(F32)
    gate = gate_up[:, 0, :].astype(F32)
    up = gate_up[:, 1, :].astype(F32)
    hidden = (jax.nn.silu(gate) * up * valid[:, None]).astype(BF16)
    acts = lax.dot_general(select, hidden, NT, preferred_element_type=F32).astype(BF16)

    acts = to_all(acts, "z").reshape(128, tokens)
    near = gather_rows(rows.reshape(2, share, columns))
    acts = to_all(acts, ("y", "xh"))
    acts = acts.reshape(8, 8, 2, share, tokens).transpose(2, 1, 0, 3, 4).reshape(2, panel, tokens)
    pieces = ring_z(near)

    half, cross_half = local // 2, panel // 2
    rows_in_half = 2 * half + cross_half
    keep, give = pl.pallas_call(
        partial_kernel,
        out_shape=(
            jax.ShapeDtypeStruct((rows_in_half + 8, panel), F32),
            jax.ShapeDtypeStruct((rows_in_half + 8, panel), BF16),
        ),
        in_specs=[SMEM, SMEM, VMEM, VMEM],
        out_specs=(VMEM, VMEM),
        compiler_params=pltpu.CompilerParams(vmem_limit_bytes=12 * 1024 * 1024),
        name="partial",
    )(core[None], counts, hidden.T, acts)
    given = shift(give, "co", 1)
    keep = keep + given.astype(F32)
    give = keep.astype(BF16)
    given = shift(give, "xl", 1)
    keep, give = pl.pallas_call(
        join_kernel,
        out_shape=(
            jax.ShapeDtypeStruct((rows_in_half, panel), F32),
            jax.ShapeDtypeStruct((rows_in_half, panel), BF16),
        ),
        in_specs=[VMEM, VMEM],
        out_specs=(VMEM, VMEM),
        compiler_params=pltpu.CompilerParams(vmem_limit_bytes=12 * 1024 * 1024),
        name="join",
    )(keep, given)
    given = shift(give, "co", 1)

    stay = jnp.where(jnp.any(onehot, axis=0), 0.0, 1.0).astype(F32)[:, None]
    at = jnp.stack([core, lax.axis_index("z").astype(jnp.int32)])
    backs = [back for back, _ in pieces]
    return pl.pallas_call(
        functools.partial(tail_kernel, backs),
        out_shape=jax.ShapeDtypeStruct((local, columns), BF16),
        in_specs=[SMEM, VMEM, VMEM, HBM, VMEM] + [HBM] * (len(backs) + 1),
        out_specs=HBM,
        scratch_shapes=[
            pltpu.VMEM((2, panel, panel), F32),
            pltpu.VMEM((2, panel, columns), BF16),
            pltpu.VMEM((local, columns), BF16),
            pltpu.VMEM((local, columns), BF16),
            pltpu.VMEM((local, 2 * panel), BF16),
            pltpu.SemaphoreType.DMA((2,)),
            pltpu.SemaphoreType.DMA((len(backs), 2)),
            pltpu.SemaphoreType.DMA(()),
            pltpu.SemaphoreType.DMA((4,)),
        ],
        compiler_params=pltpu.CompilerParams(vmem_limit_bytes=20 * 1024 * 1024),
        name="tail",
    )(at, keep, given, far(inverses), stay, *[far(piece) for _, piece in pieces], far(down_weight))


def solution(mesh):
    fine = Mesh(mesh.devices.reshape(8, 4, 2, 2, 2), ("z", "y", "xh", "xl", "co"))
    chan, grp = ("z", "y", "xh"), ("xl", "co")
    in_specs = (P(grp, None, chan), P(grp), P(), P(), P(chan, grp))
    return jax.shard_map(compute, mesh=fine, in_specs=in_specs, out_specs=P(chan, grp), check_vma=False)
```

time: 104 us -> 133 us (1.28)
  the two profiles are of different devices: /device:TPU:1 before, /device:TPU:8 now
where the time goes in v1:
time: 133 us; the launch traced here: 132 us
  waiting for transfers between devices  67.9 us (51%)
  starting transfers between devices  36.7 us (28%)
  Pallas kernels  11.3 us (8%)
  local copies, waits for them, and re-layouts  8.69 us (7%)
  matrix products  4.68 us (4%)
  other arithmetic  1.83 us (1%)
    ppermute x15, waiting for transfers between devices, shift(): return lax.ppermute(x, axis, [(i, (i + by) % n) for i in range(n)])  56 us
    ppermute x15, starting transfers between devices, shift(): return lax.ppermute(x, axis, [(i, (i + by) % n) for i in range(n)])  20.9 us
    all_to_all x2, starting transfers between devices, to_all(): lax.all_to_all(jnp.broadcast_to(x, (n, *x.shape)), axes, split_axis=0, co...  15.8 us
    all_to_all x2, waiting for transfers between devices, to_all(): lax.all_to_all(jnp.broadcast_to(x, (n, *x.shape)), axes, split_axis=0, co...  11.9 us
    pallas_call x1, Pallas kernels, compute(): pl.pallas_call(functools.partial(tail_kernel, backs), out_shape=jax.Shape...  9.11 us
    dynamic_update_slice x5, local copies, waits for them, and re-layouts, place(): out = lax.dynamic_update_slice(out, jnp.expand_dims(piece, dim), at)  3.42 us
  transfers between devices with their start and end apart: 17, of which 8 were waited for; matrix products, arithmetic and copies ran while one was open for 7% of the time, Pallas kernels for 2%

profile of v1, /device:TPU:8, one launch (start us, length us, event | category | flops | bytes accessed | tf_op | source)
XLA Modules:
  0.0 132.3 jit_solution(12097712338396076738)
XLA Ops:
  0.0 0.8 fusion.10
  1.5 2.2 %convolution_convert_fusion.1 = bf16[16,1024]{1,0:T(8,128)(2,1)S(1)} fusion(s32[16]{0:T(128)S(1)} %sub.27, f32[1024]{0:T(1024)S(1)} %fusion.9, bf16[1024,2,448]{0,2,1:T(8,128)(2,1)} %param.5), kind=kOutput, calls=%fused_computation.10 | convolution fusion | flops 18832384 | bytes 1871936 | tf_op jit(solution)/shard_map/dot_general | solution.py:186
  3.7 0.7 broadcast_in_dim.40
  4.4 8.5 %all-to-all-start = ((bf16[8,16,1024]{2,1,0:T(8,128)(2,1)}), bf16[8,16,1024]{2,1,0:T(8,128)(2,1)S(1)}, u32[]{:S(2)}, u32[]{:S(2)}) async-start(bf16[8,16,1024]{2,1,0:T(8,128)(2,1)} %broadcast_in_dim.40), calls=%async_computation | async-start | bytes 524288 | tf_op jit(solution)/shard_map/all_to_all | solution.py:26
  12.9 11.9 %all-to-all-done = bf16[8,16,1024]{2,1,0:T(8,128)(2,1)S(1)} async-done(((bf16[8,16,1024]{2,1,0:T(8,128)(2,1)}), bf16[8,16,1024]{2,1,0:T(8,128)(2,1)S(1)}, u32[]{:S(2)}, u32[]{:S(2)}) %all-to-all-start) | async-done | bytes 262176 | tf_op jit(solution)/shard_map/all_to_all | solution.py:26
  24.7 1.6 %broadcast_in_dim.41 = bf16[8,128,1024]{2,1,0:T(8,128)(2,1)} broadcast(bf16[128,1024]{1,0:T(8,128)(2,1)S(1)} %bitcast.57), dimensions={1,2} | broadcast | bytes 2359296 | tf_op jit(solution)/shard_map/broadcast_in_dim | solution.py:26
  26.3 7.4 %all-to-all-start.1 = ((bf16[8,128,1024]{2,1,0:T(8,128)(2,1)}), bf16[8,128,1024]{2,1,0:T(8,128)(2,1)S(1)}, u32[]{:S(2)}, u32[]{:S(2)}) async-start(bf16[8,128,1024]{2,1,0:T(8,128)(2,1)} %broadcast_in_dim.41), calls=%async_computation.1 | async-start | bytes 4194304 | tf_op jit(solution)/shard_map/all_to_all | solution.py:26
  33.7 0.7 broadcast_in_dim.45
  34.4 2.5 %bitcast_dynamic-update-slice_fusion.4 = (bf16[2,2,8,2048]{3,2,1,0:T(8,128)(2,1)}, bf16[16,2048]{1,0:T(8,128)(2,1)S(1)}) fusion(bf16[2,2,8,2048]{3,2,1,0:T(8,128)(2,1)} %broadcast_in_dim.45, s32[]{:T(128)S(6)} %select_n.66, bf16[448,2048]{1,0:T(8,128)(2,1)} %refs_9_.1, s32[16]{0:T(128)S(1)} %sub.27), kind=kOutput, calls=%fused_computation.15 | convolution fusion | flops 29400064 | bytes 1966148 | tf_op jit(solution)/shard_map/dot_general | solution.py:179
  36.9 3.0 %collective-permute-start.3 = (bf16[2,8,2048]{2,1,0:T(8,128)(2,1)S(1)}, bf16[2,8,2048]{2,1,0:T(8,128)(2,1)S(1)}, u32[]{:S(2)}, u32[]{:S(2)}) collective-permute-start(bf16[2,8,2048]{2,1,0:T(8,128)(2,1)S(1)} %bitcast.58), channel_id=1, source_target_pairs={{0,4},{4,0},{1,5},{5,1},{2,6},{6,2},{3,7},{7,3},{8,12},{12,8},{9,1... | collective-permute-start | bytes 196616 | tf_op jit(solution)/shard_map/ppermute | solution.py:21
  39.9 0.6 fusion.14.hidden_ref
  40.6 18.6 %collective-permute-done.3 = bf16[2,8,2048]{2,1,0:T(8,128)(2,1)S(1)} collective-permute-done((bf16[2,8,2048]{2,1,0:T(8,128)(2,1)S(1)}, bf16[2,8,2048]{2,1,0:T(8,128)(2,1)S(1)}, u32[]{:S(2)}, u32[]{:S(2)}) %collective-permute-start.3) | collective-permute-done | bytes 65568 | tf_op jit(solution)/shard_map/ppermute | solution.py:21
  59.2 0.6 bitcast_dynamic-update-slice_fusion.5
  59.9 1.5 %collective-permute-start.4 = (bf16[2,2,8,2048]{3,2,1,0:T(8,128)(2,1)}, bf16[2,2,8,2048]{3,2,1,0:T(8,128)(2,1)S(1)}, u32[]{:S(2)}, u32[]{:S(2)}) collective-permute-start(bf16[2,2,8,2048]{3,2,1,0:T(8,128)(2,1)} %bitcast_dynamic-update-slice_fusion.5), channel_id=1, source_target_pairs={{0,8},{8,16},{16,24},{24,0},{1,9},{9,17},{17,25},{25,1},{2,10},{10... | collective-permute-start | bytes 393224 | tf_op jit(solution)/shard_map/ppermute | solution.py:21
  61.3 0.6 collective-permute-start.5
  61.9 2.1 %collective-permute-start.6 = (bf16[2,2,8,2048]{3,2,1,0:T(8,128)(2,1)}, bf16[2,2,8,2048]{3,2,1,0:T(8,128)(2,1)}, u32[]{:S(2)}, u32[]{:S(2)}) collective-permute-start(bf16[2,2,8,2048]{3,2,1,0:T(8,128)(2,1)} %bitcast_dynamic-update-slice_fusion.5), channel_id=1, source_target_pairs={{0,16},{8,24},{16,0},{24,8},{1,17},{9,25},{17,1},{25,9},{2,18},{10... | collective-permute-start | bytes 393224 | tf_op jit(solution)/shard_map/ppermute | solution.py:21
  64.0 0.9 bitcast_dynamic-update-slice_fusion.2
  65.7 2.0 %partial.1 = (f32[712,512]{1,0:T(8,128)S(1)}, bf16[712,512]{1,0:T(8,128)(2,1)S(1)}) custom-call(s32[1]{0:T(128)} %bitcast.core_ref, s32[1]{0:T(128)} %copy.28.count_ref, bf16[448,1024]{1,0:T(8,128)(2,1)S(1)} %fusion.14.hidden_ref, bf16[2,512,1024]{2,1,0:T(8,128)(2,1)S(1)} %bitcast.52), custom_call_target="tpu_custom_call" | custom-call | tf_op jit(solution)/shard_map/partial/pallas_call | solution.py:196
  67.8 0.9 bitcast_dynamic-update-slice_fusion
  68.7 0.9 bitcast_dynamic-update-slice_fusion.3
  69.7 3.2 %collective-permute-start.8 = (bf16[2,64,2048]{2,1,0:T(8,128)(2,1)S(1)}, bf16[2,64,2048]{2,1,0:T(8,128)(2,1)S(1)}, u32[]{:S(2)}, u32[]{:S(2)}) collective-permute-start(bf16[2,64,2048]{2,1,0:T(8,128)(2,1)S(1)} %bitcast.55), channel_id=1, source_target_pairs={{0,224},{32,0},{64,32},{96,64},{128,96},{160,128},{192,160},{224,1... | collective-permute-start | bytes 1572872 | tf_op jit(solution)/shard_map/ppermute | solution.py:21
  73.2 0.7 collective-permute-start.1
  73.9 11.3 %collective-permute-done.7.refs_1_ = bf16[2,64,2048]{2,1,0:T(8,128)(2,1)S(1)} collective-permute-done((bf16[2,64,2048]{2,1,0:T(8,128)(2,1)S(1)}, bf16[2,64,2048]{2,1,0:T(8,128)(2,1)S(1)}, u32[]{:S(2)}, u32[]{:S(2)}) %collective-permute-start.7) | collective-permute-done | bytes 524320 | tf_op jit(solution)/shard_map/ppermute | solution.py:21
  85.3 3.2 %collective-permute-start.10 = (bf16[2,64,2048]{2,1,0:T(8,128)(2,1)S(1)}, bf16[2,64,2048]{2,1,0:T(8,128)(2,1)S(1)}, u32[]{:S(2)}, u32[]{:S(2)}) collective-permute-start(bf16[2,64,2048]{2,1,0:T(8,128)(2,1)S(1)} %collective-permute-done.8.refs_2_), channel_id=1, source_target_pairs={{0,224},{32,0},{64,32},{96,64},{128,96},{160,128},{192,160},{224,1... | collective-permute-start | bytes 1572872 | tf_op jit(solution)/shard_map/ppermute | solution.py:21
  88.5 11.4 %collective-permute-done.9.refs_3_ = bf16[2,64,2048]{2,1,0:T(8,128)(2,1)S(1)} collective-permute-done((bf16[2,64,2048]{2,1,0:T(8,128)(2,1)S(1)}, bf16[2,64,2048]{2,1,0:T(8,128)(2,1)S(1)}, u32[]{:S(2)}, u32[]{:S(2)}) %collective-permute-start.9) | collective-permute-done | bytes 524320 | tf_op jit(solution)/shard_map/ppermute | solution.py:21
  99.9 3.2 %collective-permute-start.12 = (bf16[2,64,2048]{2,1,0:T(8,128)(2,1)S(1)}, bf16[2,64,2048]{2,1,0:T(8,128)(2,1)S(1)}, u32[]{:S(2)}, u32[]{:S(2)}) collective-permute-start(bf16[2,64,2048]{2,1,0:T(8,128)(2,1)S(1)} %collective-permute-done.10.refs_4_), channel_id=1, source_target_pairs={{0,224},{32,0},{64,32},{96,64},{128,96},{160,128},{192,160},{224,1... | collective-permute-start | bytes 1572872 | tf_op jit(solution)/shard_map/ppermute | solution.py:21
  103.6 10.1 %collective-permute-done.11.refs_5_ = bf16[2,64,2048]{2,1,0:T(8,128)(2,1)S(1)} collective-permute-done((bf16[2,64,2048]{2,1,0:T(8,128)(2,1)S(1)}, bf16[2,64,2048]{2,1,0:T(8,128)(2,1)S(1)}, u32[]{:S(2)}, u32[]{:S(2)}) %collective-permute-start.11) | collective-permute-done | bytes 524320 | tf_op jit(solution)/shard_map/ppermute | solution.py:21
  113.7 0.8 slice.16
  114.5 0.8 slice.17
  115.3 3.2 %collective-permute-start.14 = (bf16[2,64,1024]{2,1,0:T(8,128)(2,1)}, bf16[2,64,1024]{2,1,0:T(8,128)(2,1)}, u32[]{:S(2)}, u32[]{:S(2)}) collective-permute-start(bf16[2,64,1024]{2,1,0:T(8,128)(2,1)} %slice.17), channel_id=1, source_target_pairs={{0,224},{32,0},{64,32},{96,64},{128,96},{160,128},{192,160},{224,1... | collective-permute-start | bytes 786440 | tf_op jit(solution)/shard_map/ppermute | solution.py:21
  118.8 3.5 %collective-permute-done.13.refs_7_ = bf16[2,64,1024]{2,1,0:T(8,128)(2,1)S(1)} collective-permute-done((bf16[2,64,1024]{2,1,0:T(8,128)(2,1)}, bf16[2,64,1024]{2,1,0:T(8,128)(2,1)S(1)}, u32[]{:S(2)}, u32[]{:S(2)}) %collective-permute-start.13) | collective-permute-done | bytes 262176 | tf_op jit(solution)/shard_map/ppermute | solution.py:21
  123.0 9.1 %tail.1 = bf16[448,2048]{1,0:T(8,128)(2,1)} custom-call(s32[2]{0:T(128)S(1)} %pad_add_fusion.at_ref, f32[704,512]{1,0:T(8,128)S(1)} %get-tuple-element.11.keep_ref, bf16[704,512]{1,0:T(8,128)(2,1)S(1)} %collective-permute-done.2.given_ref, f32[2,512,512]{2,1,0:T(8,128)} %inv_ref.1, f32[448,1]{1,0:T(8,128)S(1)} %copy.21.stay_ref, ...), custom_call_target="tpu_custom_call" | custom-call | tf_op jit(solution)/shard_map/tail/pallas_call | solution.py:227
  (46 shorter events, 2.7 us)
Async XLA Ops:
  4.4 20.3 %all-to-all-start = ((bf16[8,16,1024]{2,1,0:T(8,128)(2,1)}), bf16[8,16,1024]{2,1,0:T(8,128)(2,1)S(1)}, u32[]{:S(2)}, u32[]{:S(2)}) async-start(bf16[8,16,1024]{2,1,0:T(8,128)(2,1)} %broadcast_in_dim.40), calls=%async_computation | async-start | bytes 524288 | tf_op jit(solution)/shard_map/all_to_all | solution.py:26
  26.3 39.2 %all-to-all-start.1 = ((bf16[8,128,1024]{2,1,0:T(8,128)(2,1)}), bf16[8,128,1024]{2,1,0:T(8,128)(2,1)S(1)}, u32[]{:S(2)}, u32[]{:S(2)}) async-start(bf16[8,128,1024]{2,1,0:T(8,128)(2,1)} %broadcast_in_dim.41), calls=%async_computation.1 | async-start | bytes 4194304 | tf_op jit(solution)/shard_map/all_to_all | solution.py:26
  33.7 6.2 %copy-start.1 = (bf16[1024,2,448]{0,2,1:T(8,128)(2,1)S(1)}, bf16[1024,2,448]{0,2,1:T(8,128)(2,1)}, u32[]{:S(2)}) copy-start(bf16[1024,2,448]{0,2,1:T(8,128)(2,1)} %param.5) | copy-start | bytes 5505028
  36.9 22.3 %collective-permute-start.3 = (bf16[2,8,2048]{2,1,0:T(8,128)(2,1)S(1)}, bf16[2,8,2048]{2,1,0:T(8,128)(2,1)S(1)}, u32[]{:S(2)}, u32[]{:S(2)}) collective-permute-start(bf16[2,8,2048]{2,1,0:T(8,128)(2,1)S(1)} %bitcast.58), channel_id=1, source_target_pairs={{0,4},{4,0},{1,5},{5,1},{2,6},{6,2},{3,7},{7,3},{8,12},{12,8},{9,1... | collective-permute-start | bytes 196616 | tf_op jit(solution)/shard_map/ppermute | solution.py:21
  59.9 5.6 %collective-permute-start.4 = (bf16[2,2,8,2048]{3,2,1,0:T(8,128)(2,1)}, bf16[2,2,8,2048]{3,2,1,0:T(8,128)(2,1)S(1)}, u32[]{:S(2)}, u32[]{:S(2)}) collective-permute-start(bf16[2,2,8,2048]{3,2,1,0:T(8,128)(2,1)} %bitcast_dynamic-update-slice_fusion.5), channel_id=1, source_target_pairs={{0,8},{8,16},{16,24},{24,0},{1,9},{9,17},{17,25},{25,1},{2,10},{10... | collective-permute-start | bytes 393224 | tf_op jit(solution)/shard_map/ppermute | solution.py:21
  61.3 6.4 %collective-permute-start.5 = (bf16[2,2,8,2048]{3,2,1,0:T(8,128)(2,1)}, bf16[2,2,8,2048]{3,2,1,0:T(8,128)(2,1)}, u32[]{:S(2)}, u32[]{:S(2)}) collective-permute-start(bf16[2,2,8,2048]{3,2,1,0:T(8,128)(2,1)} %bitcast_dynamic-update-slice_fusion.5), channel_id=1, source_target_pairs={{0,24},{8,0},{16,8},{24,16},{1,25},{9,1},{17,9},{25,17},{2,26},{10... | collective-permute-start | bytes 393224 | tf_op jit(solution)/shard_map/ppermute | solution.py:21
  61.9 6.8 %collective-permute-start.6 = (bf16[2,2,8,2048]{3,2,1,0:T(8,128)(2,1)}, bf16[2,2,8,2048]{3,2,1,0:T(8,128)(2,1)}, u32[]{:S(2)}, u32[]{:S(2)}) collective-permute-start(bf16[2,2,8,2048]{3,2,1,0:T(8,128)(2,1)} %bitcast_dynamic-update-slice_fusion.5), channel_id=1, source_target_pairs={{0,16},{8,24},{16,0},{24,8},{1,17},{9,25},{17,1},{25,9},{2,18},{10... | collective-permute-start | bytes 393224 | tf_op jit(solution)/shard_map/ppermute | solution.py:21
  67.7 5.3 %collective-permute-start = (bf16[712,512]{1,0:T(8,128)(2,1)S(1)}, bf16[712,512]{1,0:T(8,128)(2,1)S(1)}, u32[]{:S(2)}, u32[]{:S(2)}) collective-permute-start(bf16[712,512]{1,0:T(8,128)(2,1)S(1)} %get-tuple-element.10), channel_id=1, source_target_pairs={{0,1},{1,0},{2,3},{3,2},{4,5},{5,4},{6,7},{7,6},{8,9},{9,8},{10,11... | collective-permute-start | bytes 2187272 | tf_op jit(solution)/shard_map/ppermute | solution.py:21
  69.6 3.6 %copy-start = (bf16[2,4,2,8,2048]{4,3,2,1,0:T(8,128)(2,1)}, bf16[2,4,2,8,2048]{4,3,2,1,0:T(8,128)(2,1)S(1)}, u32[]{:S(2)}) copy-start(bf16[2,4,2,8,2048]{4,3,2,1,0:T(8,128)(2,1)S(1)} %bitcast_dynamic-update-slice_fusion.3) | copy-start | bytes 1572868
  69.6 15.6 %collective-permute-start.7 = (bf16[2,64,2048]{2,1,0:T(8,128)(2,1)S(1)}, bf16[2,64,2048]{2,1,0:T(8,128)(2,1)S(1)}, u32[]{:S(2)}, u32[]{:S(2)}) collective-permute-start(bf16[2,64,2048]{2,1,0:T(8,128)(2,1)S(1)} %bitcast.54), channel_id=1, source_target_pairs={{0,32},{32,64},{64,96},{96,128},{128,160},{160,192},{192,224},{224... | collective-permute-start | bytes 1572872 | tf_op jit(solution)/shard_map/ppermute | solution.py:21
  69.7 15.5 %collective-permute-start.8 = (bf16[2,64,2048]{2,1,0:T(8,128)(2,1)S(1)}, bf16[2,64,2048]{2,1,0:T(8,128)(2,1)S(1)}, u32[]{:S(2)}, u32[]{:S(2)}) collective-permute-start(bf16[2,64,2048]{2,1,0:T(8,128)(2,1)S(1)} %bitcast.55), channel_id=1, source_target_pairs={{0,224},{32,0},{64,32},{96,64},{128,96},{160,128},{192,160},{224,1... | collective-permute-start | bytes 1572872 | tf_op jit(solution)/shard_map/ppermute | solution.py:21
  73.2 29.9 %collective-permute-start.1 = (bf16[712,512]{1,0:T(8,128)(2,1)S(1)}, bf16[712,512]{1,0:T(8,128)(2,1)S(1)}, u32[]{:S(2)}, u32[]{:S(2)}) collective-permute-start(bf16[712,512]{1,0:T(8,128)(2,1)S(1)} %get-tuple-element.13), channel_id=1, source_target_pairs={{0,2},{2,0},{1,3},{3,1},{4,6},{6,4},{5,7},{7,5},{8,10},{10,8},{9,1... | collective-permute-start | bytes 2187272 | tf_op jit(solution)/shard_map/ppermute | solution.py:21
  85.2 33.2 %copy-start.4 = (bf16[2,64,2048]{2,1,0:T(8,128)(2,1)}, bf16[2,64,2048]{2,1,0:T(8,128)(2,1)S(1)}, u32[]{:S(2)}) copy-start(bf16[2,64,2048]{2,1,0:T(8,128)(2,1)S(1)} %collective-permute-done.7.refs_1_) | copy-start | bytes 1572868
  85.2 14.7 %collective-permute-start.9 = (bf16[2,64,2048]{2,1,0:T(8,128)(2,1)S(1)}, bf16[2,64,2048]{2,1,0:T(8,128)(2,1)S(1)}, u32[]{:S(2)}, u32[]{:S(2)}) collective-permute-start(bf16[2,64,2048]{2,1,0:T(8,128)(2,1)S(1)} %collective-permute-done.7.refs_1_), channel_id=1, source_target_pairs={{0,32},{32,64},{64,96},{96,128},{128,160},{160,192},{192,224},{224... | collective-permute-start | bytes 1572872 | tf_op jit(solution)/shard_map/ppermute | solution.py:21
  85.3 33.2 %copy-start.5 = (bf16[2,64,2048]{2,1,0:T(8,128)(2,1)}, bf16[2,64,2048]{2,1,0:T(8,128)(2,1)S(1)}, u32[]{:S(2)}) copy-start(bf16[2,64,2048]{2,1,0:T(8,128)(2,1)S(1)} %collective-permute-done.8.refs_2_) | copy-start | bytes 1572868
  85.3 14.7 %collective-permute-start.10 = (bf16[2,64,2048]{2,1,0:T(8,128)(2,1)S(1)}, bf16[2,64,2048]{2,1,0:T(8,128)(2,1)S(1)}, u32[]{:S(2)}, u32[]{:S(2)}) collective-permute-start(bf16[2,64,2048]{2,1,0:T(8,128)(2,1)S(1)} %collective-permute-done.8.refs_2_), channel_id=1, source_target_pairs={{0,224},{32,0},{64,32},{96,64},{128,96},{160,128},{192,160},{224,1... | collective-permute-start | bytes 1572872 | tf_op jit(solution)/shard_map/ppermute | solution.py:21
  99.9 18.6 %copy-start.6 = (bf16[2,64,2048]{2,1,0:T(8,128)(2,1)}, bf16[2,64,2048]{2,1,0:T(8,128)(2,1)S(1)}, u32[]{:S(2)}) copy-start(bf16[2,64,2048]{2,1,0:T(8,128)(2,1)S(1)} %collective-permute-done.9.refs_3_) | copy-start | bytes 1572868
  99.9 13.8 %collective-permute-start.11 = (bf16[2,64,2048]{2,1,0:T(8,128)(2,1)S(1)}, bf16[2,64,2048]{2,1,0:T(8,128)(2,1)S(1)}, u32[]{:S(2)}, u32[]{:S(2)}) collective-permute-start(bf16[2,64,2048]{2,1,0:T(8,128)(2,1)S(1)} %collective-permute-done.9.refs_3_), channel_id=1, source_target_pairs={{0,32},{32,64},{64,96},{96,128},{128,160},{160,192},{192,224},{224... | collective-permute-start | bytes 1572872 | tf_op jit(solution)/shard_map/ppermute | solution.py:21
  99.9 18.6 %copy-start.7 = (bf16[2,64,2048]{2,1,0:T(8,128)(2,1)}, bf16[2,64,2048]{2,1,0:T(8,128)(2,1)S(1)}, u32[]{:S(2)}) copy-start(bf16[2,64,2048]{2,1,0:T(8,128)(2,1)S(1)} %collective-permute-done.10.refs_4_) | copy-start | bytes 1572868
  99.9 14.6 %collective-permute-start.12 = (bf16[2,64,2048]{2,1,0:T(8,128)(2,1)S(1)}, bf16[2,64,2048]{2,1,0:T(8,128)(2,1)S(1)}, u32[]{:S(2)}, u32[]{:S(2)}) collective-permute-start(bf16[2,64,2048]{2,1,0:T(8,128)(2,1)S(1)} %collective-permute-done.10.refs_4_), channel_id=1, source_target_pairs={{0,224},{32,0},{64,32},{96,64},{128,96},{160,128},{192,160},{224,1... | collective-permute-start | bytes 1572872 | tf_op jit(solution)/shard_map/ppermute | solution.py:21
  103.4 19.3 %collective-permute-start.2 = (bf16[704,512]{1,0:T(8,128)(2,1)S(1)}, bf16[704,512]{1,0:T(8,128)(2,1)S(1)}, u32[]{:S(2)}, u32[]{:S(2)}) collective-permute-start(bf16[704,512]{1,0:T(8,128)(2,1)S(1)} %get-tuple-element.12), channel_id=1, source_target_pairs={{0,1},{1,0},{2,3},{3,2},{4,5},{5,4},{6,7},{7,6},{8,9},{9,8},{10,11... | collective-permute-start | bytes 2162696 | tf_op jit(solution)/shard_map/ppermute | solution.py:21
  113.7 4.8 %copy-start.2 = (bf16[2,64,2048]{2,1,0:T(8,128)(2,1)}, bf16[2,64,2048]{2,1,0:T(8,128)(2,1)S(1)}, u32[]{:S(2)}) copy-start(bf16[2,64,2048]{2,1,0:T(8,128)(2,1)S(1)} %collective-permute-done.11.refs_5_) | copy-start | bytes 1572868
  114.5 7.8 %collective-permute-start.13 = (bf16[2,64,1024]{2,1,0:T(8,128)(2,1)}, bf16[2,64,1024]{2,1,0:T(8,128)(2,1)S(1)}, u32[]{:S(2)}, u32[]{:S(2)}) collective-permute-start(bf16[2,64,1024]{2,1,0:T(8,128)(2,1)} %slice.16), channel_id=1, source_target_pairs={{0,32},{32,64},{64,96},{96,128},{128,160},{160,192},{192,224},{224... | collective-permute-start | bytes 786440 | tf_op jit(solution)/shard_map/ppermute | solution.py:21
  114.5 4.0 %copy-start.3 = (bf16[2,64,2048]{2,1,0:T(8,128)(2,1)}, bf16[2,64,2048]{2,1,0:T(8,128)(2,1)S(1)}, u32[]{:S(2)}) copy-start(bf16[2,64,2048]{2,1,0:T(8,128)(2,1)S(1)} %collective-permute-done.12.refs_6_) | copy-start | bytes 1572868
  115.3 7.4 %collective-permute-start.14 = (bf16[2,64,1024]{2,1,0:T(8,128)(2,1)}, bf16[2,64,1024]{2,1,0:T(8,128)(2,1)}, u32[]{:S(2)}, u32[]{:S(2)}) collective-permute-start(bf16[2,64,1024]{2,1,0:T(8,128)(2,1)} %slice.17), channel_id=1, source_target_pairs={{0,224},{32,0},{64,32},{96,64},{128,96},{160,128},{192,160},{224,1... | collective-permute-start | bytes 786440 | tf_op jit(solution)/shard_map/ppermute | solution.py:21
  122.3 0.7 copy-start.8

commit v2 on v1

--- a/solution.py
+++ b/solution.py
@@ -44,6 +44,15 @@
     others = [(k, shift(both, "y", k)) for k in (1, 3, 2)]
     around = place([(0, both)] + others, "y", 1)
     return around.reshape(2, 64, rows.shape[-1])
+
+
+def spread_acts(block):
+    other = shift(block, "xh", 1)
+    block = place([(0, block), (1, other)], "xh", 0)
+    ahead, behind = shift(block, "y", 1), shift(block, "y", -1)
+    left, right = shift(ahead[:1], "y", 1), shift(behind[1:], "y", -1)
+    far_block = jnp.concatenate([left, right], axis=0)
+    return place([(0, block), (1, ahead), (3, behind), (2, far_block)], "y", 0)
 
 
 def ring_z(block):
@@ -103,15 +112,16 @@
     return dot(a[0], b[0]) + (dot(a[0], b[1]) + dot(a[1], b[0]))
 
 
-def tail_kernel(
-    backs, at_ref, keep_ref, given_ref, inv_ref, stay_ref, *refs
-):
-    pieces, (old_ref, out_ref, inv_buf, rows_ref, old_buf, new_buf, gain_ref, inv_sems, sems, old_sem, new_sems) = (
+def split_kernel(x_ref, high_ref, low_ref):
+    high_ref[...], low_ref[...] = split(x_ref[...])
+
+
+def tail_kernel(backs, at_ref, keep_ref, given_ref, high_ref, low_ref, stay_ref, *refs):
+    pieces, (old_ref, out_ref, rows_ref, old_buf, new_buf, sems, old_sem, new_sems) = (
         refs[: len(backs)], refs[len(backs):]
     )
     zero, z = at_ref[0] == 0, at_ref[1]
     depth, columns = pieces[0].shape[1:]
-    panel = inv_ref.shape[1]
     copies = []
     for i, (back, piece) in enumerate(zip(backs, pieces)):
         width = piece.shape[2]
@@ -126,9 +136,6 @@
                 )
             )
     old_copy = pltpu.make_async_copy(old_ref, old_buf, old_sem)
-    inv_copies = [pltpu.make_async_copy(inv_ref.at[p], inv_buf.at[p], inv_sems.at[p]) for p in (1, 0)]
-    for copy in inv_copies:
-        copy.start()
     for copy in copies:
         copy.start()
     old_copy.start()
@@ -136,27 +143,23 @@
     keep, given = keep_ref[...], given_ref[...].astype(F32)
     low, top = jnp.where(zero, keep, given), jnp.where(zero, given, keep)
     half = old_ref.shape[0] // 2
-    for copy in inv_copies:
-        copy.wait()
-    first_inv, second_inv = split(inv_buf[0]), split(inv_buf[1])
-    cross = split(jnp.concatenate([low[2 * half :], top[2 * half :]], axis=0))
-    for k, part in enumerate((low, top)):
-        second = dot3(split(part[half : 2 * half]), second_inv)
-        first = dot3(split(part[:half] - dot3(split(second), cross)), first_inv)
-        gain_ref[pl.ds(k * half, half), pl.ds(0, panel)] = first.astype(BF16)
-        gain_ref[pl.ds(k * half, half), pl.ds(panel, panel)] = second.astype(BF16)
+    first_hess = jnp.concatenate([low[:half], top[:half]], axis=0)
+    second_hess = jnp.concatenate([low[half : 2 * half], top[half : 2 * half]], axis=0)
+    cross = jnp.concatenate([low[2 * half :], top[2 * half :]], axis=0)
+    second = dot3(split(second_hess), (high_ref[1], low_ref[1]))
+    first = dot3(split(first_hess - dot3(split(second), split(cross))), (high_ref[0], low_ref[0]))
+    first, second = first.astype(BF16), second.astype(BF16)
 
     for copy in copies:
         copy.wait()
     old_copy.wait()
     stay = stay_ref[...] > 0.0
-    gain = gain_ref[...]
     chunks = new_sems.shape[0]
     width = columns // chunks
     outs = []
     for c in range(chunks):
         at = pl.ds(c * width, width)
-        change = dot(gain[:, :panel], rows_ref[0, :, at]) + dot(gain[:, panel:], rows_ref[1, :, at])
+        change = dot(first, rows_ref[0, :, at]) + dot(second, rows_ref[1, :, at])
         new = jnp.where(stay, old_buf[:, at].astype(F32) - change, 0.0)
         new_buf[:, at] = new.astype(BF16)
         outs.append(pltpu.make_async_copy(new_buf.at[:, at], out_ref.at[:, at], new_sems.at[c]))
@@ -187,9 +190,18 @@
 
     acts = to_all(acts, "z").reshape(128, tokens)
     near = gather_rows(rows.reshape(2, share, columns))
-    acts = to_all(acts, ("y", "xh"))
-    acts = acts.reshape(8, 8, 2, share, tokens).transpose(2, 1, 0, 3, 4).reshape(2, panel, tokens)
+    acts = spread_acts(acts).reshape(4, 2, 8, 2, share, tokens)
+    acts = acts.transpose(3, 2, 0, 1, 4, 5).reshape(2, panel, tokens)
     pieces = ring_z(near)
+    inverses, _ = lax.optimization_barrier((inverses, near))
+    parts = pl.pallas_call(
+        split_kernel,
+        out_shape=(jax.ShapeDtypeStruct(inverses.shape, BF16),) * 2,
+        in_specs=[VMEM],
+        out_specs=(VMEM, VMEM),
+        compiler_params=pltpu.CompilerParams(vmem_limit_bytes=12 * 1024 * 1024),
+        name="split",
+    )(inverses)
 
     half, cross_half = local // 2, panel // 2
     rows_in_half = 2 * half + cross_half
@@ -227,22 +239,19 @@
     return pl.pallas_call(
         functools.partial(tail_kernel, backs),
         out_shape=jax.ShapeDtypeStruct((local, columns), BF16),
-        in_specs=[SMEM, VMEM, VMEM, HBM, VMEM] + [HBM] * (len(backs) + 1),
+        in_specs=[SMEM, VMEM, VMEM, VMEM, VMEM, VMEM] + [HBM] * (len(backs) + 1),
         out_specs=HBM,
         scratch_shapes=[
-            pltpu.VMEM((2, panel, panel), F32),
             pltpu.VMEM((2, panel, columns), BF16),
             pltpu.VMEM((local, columns), BF16),
             pltpu.VMEM((local, columns), BF16),
-            pltpu.VMEM((local, 2 * panel), BF16),
-            pltpu.SemaphoreType.DMA((2,)),
             pltpu.SemaphoreType.DMA((len(backs), 2)),
             pltpu.SemaphoreType.DMA(()),
             pltpu.SemaphoreType.DMA((4,)),
         ],
         compiler_params=pltpu.CompilerParams(vmem_limit_bytes=20 * 1024 * 1024),
         name="tail",
-    )(at, keep, given, far(inverses), stay, *[far(piece) for _, piece in pieces], far(down_weight))
+    )(at, keep, given, *parts, stay, *[far(piece) for _, piece in pieces], far(down_weight))
 
 
 def solution(mesh):

time: 133 us -> 121 us (0.910)
  waiting for transfers between devices: 67.9 us -> 57.6 us
  local copies, waits for them, and re-layouts: 8.69 us -> 5.64 us
  matrix products: 4.68 us -> 2.69 us
    all_to_all x2 -> x1, waiting for transfers between devices: 11.9 us -> 1.23 us  [to_all(): lax.all_to_all(jnp.broadcast_to(x, (n, *x.shape)), axes, split_axis=0, co...]
    ppermute x15 -> x20, starting transfers between devices: 20.9 us -> 29.4 us  [shift(): return lax.ppermute(x, axis, [(i, (i + by) % n) for i in range(n)])]
    all_to_all x2 -> x1, starting transfers between devices: 15.8 us -> 8.47 us  [to_all(): lax.all_to_all(jnp.broadcast_to(x, (n, *x.shape)), axes, split_axis=0, co...]
    dynamic_update_slice x5 -> x10, local copies, waits for them, and re-layouts: 3.42 us -> 0.24 us  [place(): out = lax.dynamic_update_slice(out, jnp.expand_dims(piece, dim), at)]
    dot_general x1, matrix products: 2.52 us -> 0.39 us  [compute(): rows = jnp.dot(select, down_weight, preferred_element_type=F32).astype(BF16)]
    broadcast_in_dim x2 -> x1, local copies, waits for them, and re-layouts: 2.33 us -> 0.73 us  [to_all(): jnp.broadcast_to(x, (n, *x.shape))]
    ppermute x15 -> x20, waiting for transfers between devices: 56 us -> 56.4 us  [shift(): return lax.ppermute(x, axis, [(i, (i + by) % n) for i in range(n)])]
  transfers between devices with their start and end apart: 17 -> 21, of which waited for: 8 -> 11; matrix products, arithmetic and copies ran while one was open for 7% -> 4% of each run, Pallas kernels for 2% -> 3%
where the time goes in v2:
time: 121 us; the launch traced here: 119 us
  waiting for transfers between devices  57.6 us (48%)
  starting transfers between devices  37.9 us (31%)
  Pallas kernels  12.3 us (10%)
  local copies, waits for them, and re-layouts  5.64 us (5%)
  matrix products  2.69 us (2%)
  other arithmetic  1.91 us (2%)
    ppermute x20, waiting for transfers between devices, shift(): return lax.ppermute(x, axis, [(i, (i + by) % n) for i in range(n)])  56.4 us
    ppermute x20, starting transfers between devices, shift(): return lax.ppermute(x, axis, [(i, (i + by) % n) for i in range(n)])  29.4 us
    pallas_call x1, Pallas kernels, compute(): pl.pallas_call(functools.partial(tail_kernel, backs), out_shape=jax.Shape...  9.06 us
    all_to_all x1, starting transfers between devices, to_all(): lax.all_to_all(jnp.broadcast_to(x, (n, *x.shape)), axes, split_axis=0, co...  8.47 us
  transfers between devices with their start and end apart: 21, of which 11 were waited for; matrix products, arithmetic and copies ran while one was open for 4% of the time, Pallas kernels for 3%

profile of v2, /device:TPU:8, one launch (start us, length us, event | category | flops | bytes accessed | tf_op | source)
XLA Modules:
  0.0 119.3 jit_solution(14679757047108237809)
XLA Ops:
  0.0 0.8 fusion.11
  1.5 2.3 %convolution_convert_fusion.1 = bf16[16,1024]{1,0:T(8,128)(2,1)S(1)} fusion(s32[16]{0:T(128)S(1)} %sub.31, f32[1024]{0:T(1024)S(1)} %fusion.10, bf16[1024,2,448]{0,2,1:T(8,128)(2,1)} %param.5), kind=kOutput, calls=%fused_computation.10 | convolution fusion | flops 18832384 | bytes 1871936 | tf_op jit(solution)/shard_map/dot_general | solution.py:189
  4.5 8.5 %all-to-all-start = ((bf16[8,16,1024]{2,1,0:T(8,128)(2,1)}), bf16[8,16,1024]{2,1,0:T(8,128)(2,1)S(1)}, u32[]{:S(2)}, u32[]{:S(2)}) async-start(bf16[8,16,1024]{2,1,0:T(8,128)(2,1)} %broadcast_in_dim.60), calls=%async_computation | async-start | bytes 524288 | tf_op jit(solution)/shard_map/all_to_all | solution.py:26
  13.4 3.1 %collective-permute-start.8 = (bf16[2,8,2048]{2,1,0:T(8,128)(2,1)S(1)}, bf16[2,8,2048]{2,1,0:T(8,128)(2,1)S(1)}, u32[]{:S(2)}, u32[]{:S(2)}) collective-permute-start(bf16[2,8,2048]{2,1,0:T(8,128)(2,1)S(1)} %bitcast.74), channel_id=1, source_target_pairs={{0,4},{4,0},{1,5},{5,1},{2,6},{6,2},{3,7},{7,3},{8,12},{12,8},{9,1... | collective-permute-start | bytes 196616 | tf_op jit(solution)/shard_map/ppermute | solution.py:21
  17.2 2.0 %collective-permute-done.8 = bf16[2,8,2048]{2,1,0:T(8,128)(2,1)S(1)} collective-permute-done((bf16[2,8,2048]{2,1,0:T(8,128)(2,1)S(1)}, bf16[2,8,2048]{2,1,0:T(8,128)(2,1)S(1)}, u32[]{:S(2)}, u32[]{:S(2)}) %collective-permute-start.8) | collective-permute-done | bytes 65568 | tf_op jit(solution)/shard_map/ppermute | solution.py:21
  19.3 1.7 %collective-permute-start.9 = (bf16[2,2,8,2048]{3,2,1,0:T(8,128)(2,1)S(1)}, bf16[2,2,8,2048]{3,2,1,0:T(8,128)(2,1)S(1)}, u32[]{:S(2)}, u32[]{:S(2)}) collective-permute-start(bf16[2,2,8,2048]{3,2,1,0:T(8,128)(2,1)S(1)} %bitcast_dynamic-update-slice_fusion.10), channel_id=1, source_target_pairs={{0,8},{8,16},{16,24},{24,0},{1,9},{9,17},{17,25},{25,1},{2,10},{10... | collective-permute-start | bytes 393224 | tf_op jit(solution)/shard_map/ppermute | solution.py:21
  21.4 2.3 %collective-permute-start.11 = (bf16[2,2,8,2048]{3,2,1,0:T(8,128)(2,1)S(1)}, bf16[2,2,8,2048]{3,2,1,0:T(8,128)(2,1)S(1)}, u32[]{:S(2)}, u32[]{:S(2)}) collective-permute-start(bf16[2,2,8,2048]{3,2,1,0:T(8,128)(2,1)S(1)} %bitcast_dynamic-update-slice_fusion.10), channel_id=1, source_target_pairs={{0,16},{8,24},{16,0},{24,8},{1,17},{9,25},{17,1},{25,9},{2,18},{10... | collective-permute-start | bytes 393224 | tf_op jit(solution)/shard_map/ppermute | solution.py:21
  23.7 1.2 %all-to-all-done = bf16[8,16,1024]{2,1,0:T(8,128)(2,1)S(1)} async-done(((bf16[8,16,1024]{2,1,0:T(8,128)(2,1)}), bf16[8,16,1024]{2,1,0:T(8,128)(2,1)S(1)}, u32[]{:S(2)}, u32[]{:S(2)}) %all-to-all-start) | async-done | bytes 262176 | tf_op jit(solution)/shard_map/all_to_all | solution.py:26
  24.9 3.0 %collective-permute-start = (bf16[128,1024]{1,0:T(8,128)(2,1)S(1)}, bf16[128,1024]{1,0:T(8,128)(2,1)S(1)}, u32[]{:S(2)}, u32[]{:S(2)}) collective-permute-start(bf16[128,1024]{1,0:T(8,128)(2,1)S(1)} %bitcast.72), channel_id=1, source_target_pairs={{0,4},{4,0},{1,5},{5,1},{2,6},{6,2},{3,7},{7,3},{8,12},{12,8},{9,1... | collective-permute-start | bytes 786440 | tf_op jit(solution)/shard_map/ppermute | solution.py:21
  28.1 4.7 %collective-permute-done = bf16[128,1024]{1,0:T(8,128)(2,1)S(1)} collective-permute-done((bf16[128,1024]{1,0:T(8,128)(2,1)S(1)}, bf16[128,1024]{1,0:T(8,128)(2,1)S(1)}, u32[]{:S(2)}, u32[]{:S(2)}) %collective-permute-start) | collective-permute-done | bytes 262176 | tf_op jit(solution)/shard_map/ppermute | solution.py:21
  32.8 1.7 %collective-permute-start.1 = (bf16[2,128,1024]{2,1,0:T(8,128)(2,1)S(1)}, bf16[2,128,1024]{2,1,0:T(8,128)(2,1)S(1)}, u32[]{:S(2)}, u32[]{:S(2)}) collective-permute-start(bf16[2,128,1024]{2,1,0:T(8,128)(2,1)S(1)} %bitcast_dynamic-update-slice_fusion.3), channel_id=1, source_target_pairs={{0,8},{8,16},{16,24},{24,0},{1,9},{9,17},{17,25},{25,1},{2,10},{10... | collective-permute-start | bytes 1572872 | tf_op jit(solution)/shard_map/ppermute | solution.py:21
  35.2 9.6 %collective-permute-done.1 = bf16[2,128,1024]{2,1,0:T(8,128)(2,1)S(1)} collective-permute-done((bf16[2,128,1024]{2,1,0:T(8,128)(2,1)S(1)}, bf16[2,128,1024]{2,1,0:T(8,128)(2,1)S(1)}, u32[]{:S(2)}, u32[]{:S(2)}) %collective-permute-start.1) | collective-permute-done | bytes 524320 | tf_op jit(solution)/shard_map/ppermute | solution.py:21
  44.8 1.7 %collective-permute-start.3 = (bf16[1,128,1024]{2,1,0:T(8,128)(2,1)S(1)}, bf16[1,128,1024]{2,1,0:T(8,128)(2,1)S(1)}, u32[]{:S(2)}, u32[]{:S(2)}) collective-permute-start(bf16[1,128,1024]{2,1,0:T(8,128)(2,1)S(1)} %slice.24), channel_id=1, source_target_pairs={{0,8},{8,16},{16,24},{24,0},{1,9},{9,17},{17,25},{25,1},{2,10},{10... | collective-permute-start | bytes 786440 | tf_op jit(solution)/shard_map/ppermute | solution.py:21
  47.1 4.1 %collective-permute-done.3 = bf16[1,128,1024]{2,1,0:T(8,128)(2,1)S(1)} collective-permute-done((bf16[1,128,1024]{2,1,0:T(8,128)(2,1)S(1)}, bf16[1,128,1024]{2,1,0:T(8,128)(2,1)S(1)}, u32[]{:S(2)}, u32[]{:S(2)}) %collective-permute-start.3) | collective-permute-done | bytes 262176 | tf_op jit(solution)/shard_map/ppermute | solution.py:21
  51.3 1.7 %collective-permute-done.4 = bf16[1,128,1024]{2,1,0:T(8,128)(2,1)S(1)} collective-permute-done((bf16[1,128,1024]{2,1,0:T(8,128)(2,1)S(1)}, bf16[1,128,1024]{2,1,0:T(8,128)(2,1)S(1)}, u32[]{:S(2)}, u32[]{:S(2)}) %collective-permute-start.4) | collective-permute-done | bytes 262176 | tf_op jit(solution)/shard_map/ppermute | solution.py:21
  53.3 2.0 %partial.1 = (f32[712,512]{1,0:T(8,128)S(1)}, bf16[712,512]{1,0:T(8,128)(2,1)S(1)}) custom-call(s32[1]{0:T(128)} %bitcast.core_ref, s32[1]{0:T(128)} %copy.34.count_ref, bf16[448,1024]{1,0:T(8,128)(2,1)S(1)} %fusion.15.hidden_ref, bf16[2,512,1024]{2,1,0:T(8,128)(2,1)S(1)} %bitcast.67), custom_call_target="tpu_custom_call" | custom-call | tf_op jit(solution)/shard_map/partial/pallas_call | solution.py:208
  56.1 2.7 %collective-permute-start.13 = (bf16[2,64,2048]{2,1,0:T(8,128)(2,1)S(1)}, bf16[2,64,2048]{2,1,0:T(8,128)(2,1)S(1)}, u32[]{:S(2)}, u32[]{:S(2)}) collective-permute-start(bf16[2,64,2048]{2,1,0:T(8,128)(2,1)S(1)} %bitcast.70), channel_id=1, source_target_pairs={{0,224},{32,0},{64,32},{96,64},{128,96},{160,128},{192,160},{224,1... | collective-permute-start | bytes 1572872 | tf_op jit(solution)/shard_map/ppermute | solution.py:21
  59.1 1.6 %collective-permute-start.6 = (bf16[712,512]{1,0:T(8,128)(2,1)S(1)}, bf16[712,512]{1,0:T(8,128)(2,1)S(1)}, u32[]{:S(2)}, u32[]{:S(2)}) collective-permute-start(bf16[712,512]{1,0:T(8,128)(2,1)S(1)} %get-tuple-element.19), channel_id=1, source_target_pairs={{0,2},{2,0},{1,3},{3,1},{4,6},{6,4},{5,7},{7,5},{8,10},{10,8},{9,1... | collective-permute-start | bytes 2187272 | tf_op jit(solution)/shard_map/ppermute | solution.py:21
  60.7 10.4 %collective-permute-done.12.refs_1_ = bf16[2,64,2048]{2,1,0:T(8,128)(2,1)S(1)} collective-permute-done((bf16[2,64,2048]{2,1,0:T(8,128)(2,1)S(1)}, bf16[2,64,2048]{2,1,0:T(8,128)(2,1)S(1)}, u32[]{:S(2)}, u32[]{:S(2)}) %collective-permute-start.12) | collective-permute-done | bytes 524320 | tf_op jit(solution)/shard_map/ppermute | solution.py:21
  71.1 3.2 %collective-permute-start.15 = (bf16[2,64,2048]{2,1,0:T(8,128)(2,1)S(1)}, bf16[2,64,2048]{2,1,0:T(8,128)(2,1)S(1)}, u32[]{:S(2)}, u32[]{:S(2)}) collective-permute-start(bf16[2,64,2048]{2,1,0:T(8,128)(2,1)S(1)} %collective-permute-done.13.refs_2_), channel_id=1, source_target_pairs={{0,224},{32,0},{64,32},{96,64},{128,96},{160,128},{192,160},{224,1... | collective-permute-start | bytes 1572872 | tf_op jit(solution)/shard_map/ppermute | solution.py:21
  74.3 11.4 %collective-permute-done.14.refs_3_ = bf16[2,64,2048]{2,1,0:T(8,128)(2,1)S(1)} collective-permute-done((bf16[2,64,2048]{2,1,0:T(8,128)(2,1)S(1)}, bf16[2,64,2048]{2,1,0:T(8,128)(2,1)S(1)}, u32[]{:S(2)}, u32[]{:S(2)}) %collective-permute-start.14) | collective-permute-done | bytes 524320 | tf_op jit(solution)/shard_map/ppermute | solution.py:21
  85.7 3.2 %collective-permute-start.17 = (bf16[2,64,2048]{2,1,0:T(8,128)(2,1)S(1)}, bf16[2,64,2048]{2,1,0:T(8,128)(2,1)S(1)}, u32[]{:S(2)}, u32[]{:S(2)}) collective-permute-start(bf16[2,64,2048]{2,1,0:T(8,128)(2,1)S(1)} %collective-permute-done.15.refs_4_), channel_id=1, source_target_pairs={{0,224},{32,0},{64,32},{96,64},{128,96},{160,128},{192,160},{224,1... | collective-permute-start | bytes 1572872 | tf_op jit(solution)/shard_map/ppermute | solution.py:21
  89.0 1.0 join.1
  90.1 9.4 %collective-permute-done.16.refs_5_ = bf16[2,64,2048]{2,1,0:T(8,128)(2,1)S(1)} collective-permute-done((bf16[2,64,2048]{2,1,0:T(8,128)(2,1)S(1)}, bf16[2,64,2048]{2,1,0:T(8,128)(2,1)S(1)}, u32[]{:S(2)}, u32[]{:S(2)}) %collective-permute-start.16) | collective-permute-done | bytes 524320 | tf_op jit(solution)/shard_map/ppermute | solution.py:21
  99.5 0.8 copy-done.5
  100.3 0.7 slice.26
  101.1 0.8 copy-done.6
  102.6 3.2 %collective-permute-start.19 = (bf16[2,64,1024]{2,1,0:T(8,128)(2,1)}, bf16[2,64,1024]{2,1,0:T(8,128)(2,1)}, u32[]{:S(2)}, u32[]{:S(2)}) collective-permute-start(bf16[2,64,1024]{2,1,0:T(8,128)(2,1)} %slice.27), channel_id=1, source_target_pairs={{0,224},{32,0},{64,32},{96,64},{128,96},{160,128},{192,160},{224,1... | collective-permute-start | bytes 786440 | tf_op jit(solution)/shard_map/ppermute | solution.py:21
  105.9 0.9 copy.21.stay_ref
  107.1 1.9 %collective-permute-done.18.refs_7_ = bf16[2,64,1024]{2,1,0:T(8,128)(2,1)} collective-permute-done((bf16[2,64,1024]{2,1,0:T(8,128)(2,1)}, bf16[2,64,1024]{2,1,0:T(8,128)(2,1)}, u32[]{:S(2)}, u32[]{:S(2)}) %collective-permute-start.18) | collective-permute-done | bytes 262176 | tf_op jit(solution)/shard_map/ppermute | solution.py:21
  109.0 1.1 collective-permute-done.19.refs_8_
  110.1 9.1 %tail.1 = bf16[448,2048]{1,0:T(8,128)(2,1)} custom-call(s32[2]{0:T(128)S(1)} %pad_add_fusion.at_ref, f32[704,512]{1,0:T(8,128)S(1)} %get-tuple-element.14.keep_ref, bf16[704,512]{1,0:T(8,128)(2,1)} %collective-permute-done.7.given_ref, bf16[2,512,512]{2,1,0:T(8,128)(2,1)S(1)} %get-tuple-element.17.high_ref, ...), custom_call_target="tpu_custom_call" | custom-call | tf_op jit(solution)/shard_map/tail/pallas_call | solution.py:239
  (68 shorter events, 6.5 us)
Async XLA Ops:
  1.5 11.5 %copy-start.2 = (bf16[448,2048]{1,0:T(8,128)(2,1)S(1)}, bf16[448,2048]{1,0:T(8,128)(2,1)}, u32[]{:S(2)}) copy-start(bf16[448,2048]{1,0:T(8,128)(2,1)} %refs_9_.1) | copy-start | bytes 5505028
  4.5 20.3 %all-to-all-start = ((bf16[8,16,1024]{2,1,0:T(8,128)(2,1)}), bf16[8,16,1024]{2,1,0:T(8,128)(2,1)S(1)}, u32[]{:S(2)}, u32[]{:S(2)}) async-start(bf16[8,16,1024]{2,1,0:T(8,128)(2,1)} %broadcast_in_dim.60), calls=%async_computation | async-start | bytes 524288 | tf_op jit(solution)/shard_map/all_to_all | solution.py:26
  13.0 3.5 %copy-start.4 = (bf16[1024,2,448]{0,2,1:T(8,128)(2,1)S(1)}, bf16[1024,2,448]{0,2,1:T(8,128)(2,1)}, u32[]{:S(2)}) copy-start(bf16[1024,2,448]{0,2,1:T(8,128)(2,1)} %param.5) | copy-start | bytes 5505028
  13.4 5.8 %collective-permute-start.8 = (bf16[2,8,2048]{2,1,0:T(8,128)(2,1)S(1)}, bf16[2,8,2048]{2,1,0:T(8,128)(2,1)S(1)}, u32[]{:S(2)}, u32[]{:S(2)}) collective-permute-start(bf16[2,8,2048]{2,1,0:T(8,128)(2,1)S(1)} %bitcast.74), channel_id=1, source_target_pairs={{0,4},{4,0},{1,5},{5,1},{2,6},{6,2},{3,7},{7,3},{8,12},{12,8},{9,1... | collective-permute-start | bytes 196616 | tf_op jit(solution)/shard_map/ppermute | solution.py:21
  19.3 15.7 %collective-permute-start.9 = (bf16[2,2,8,2048]{3,2,1,0:T(8,128)(2,1)S(1)}, bf16[2,2,8,2048]{3,2,1,0:T(8,128)(2,1)S(1)}, u32[]{:S(2)}, u32[]{:S(2)}) collective-permute-start(bf16[2,2,8,2048]{3,2,1,0:T(8,128)(2,1)S(1)} %bitcast_dynamic-update-slice_fusion.10), channel_id=1, source_target_pairs={{0,8},{8,16},{16,24},{24,0},{1,9},{9,17},{17,25},{25,1},{2,10},{10... | collective-permute-start | bytes 393224 | tf_op jit(solution)/shard_map/ppermute | solution.py:21
  20.9 34.5 %collective-permute-start.10 = (bf16[2,2,8,2048]{3,2,1,0:T(8,128)(2,1)S(1)}, bf16[2,2,8,2048]{3,2,1,0:T(8,128)(2,1)S(1)}, u32[]{:S(2)}, u32[]{:S(2)}) collective-permute-start(bf16[2,2,8,2048]{3,2,1,0:T(8,128)(2,1)S(1)} %bitcast_dynamic-update-slice_fusion.10), channel_id=1, source_target_pairs={{0,24},{8,0},{16,8},{24,16},{1,25},{9,1},{17,9},{25,17},{2,26},{10... | collective-permute-start | bytes 393224 | tf_op jit(solution)/shard_map/ppermute | solution.py:21
  21.4 34.1 %collective-permute-start.11 = (bf16[2,2,8,2048]{3,2,1,0:T(8,128)(2,1)S(1)}, bf16[2,2,8,2048]{3,2,1,0:T(8,128)(2,1)S(1)}, u32[]{:S(2)}, u32[]{:S(2)}) collective-permute-start(bf16[2,2,8,2048]{3,2,1,0:T(8,128)(2,1)S(1)} %bitcast_dynamic-update-slice_fusion.10), channel_id=1, source_target_pairs={{0,16},{8,24},{16,0},{24,8},{1,17},{9,25},{17,1},{25,9},{2,18},{10... | collective-permute-start | bytes 393224 | tf_op jit(solution)/shard_map/ppermute | solution.py:21
  24.9 7.9 %collective-permute-start = (bf16[128,1024]{1,0:T(8,128)(2,1)S(1)}, bf16[128,1024]{1,0:T(8,128)(2,1)S(1)}, u32[]{:S(2)}, u32[]{:S(2)}) collective-permute-start(bf16[128,1024]{1,0:T(8,128)(2,1)S(1)} %bitcast.72), channel_id=1, source_target_pairs={{0,4},{4,0},{1,5},{5,1},{2,6},{6,2},{3,7},{7,3},{8,12},{12,8},{9,1... | collective-permute-start | bytes 786440 | tf_op jit(solution)/shard_map/ppermute | solution.py:21
  32.8 12.0 %collective-permute-start.1 = (bf16[2,128,1024]{2,1,0:T(8,128)(2,1)S(1)}, bf16[2,128,1024]{2,1,0:T(8,128)(2,1)S(1)}, u32[]{:S(2)}, u32[]{:S(2)}) collective-permute-start(bf16[2,128,1024]{2,1,0:T(8,128)(2,1)S(1)} %bitcast_dynamic-update-slice_fusion.3), channel_id=1, source_target_pairs={{0,8},{8,16},{16,24},{24,0},{1,9},{9,17},{17,25},{25,1},{2,10},{10... | collective-permute-start | bytes 1572872 | tf_op jit(solution)/shard_map/ppermute | solution.py:21
  34.5 12.1 %collective-permute-start.2 = (bf16[2,128,1024]{2,1,0:T(8,128)(2,1)S(1)}, bf16[2,128,1024]{2,1,0:T(8,128)(2,1)S(1)}, u32[]{:S(2)}, u32[]{:S(2)}) collective-permute-start(bf16[2,128,1024]{2,1,0:T(8,128)(2,1)S(1)} %bitcast_dynamic-update-slice_fusion.3), channel_id=1, source_target_pairs={{0,24},{8,0},{16,8},{24,16},{1,25},{9,1},{17,9},{25,17},{2,26},{10... | collective-permute-start | bytes 1572872 | tf_op jit(solution)/shard_map/ppermute | solution.py:21
  44.8 6.4 %collective-permute-start.3 = (bf16[1,128,1024]{2,1,0:T(8,128)(2,1)S(1)}, bf16[1,128,1024]{2,1,0:T(8,128)(2,1)S(1)}, u32[]{:S(2)}, u32[]{:S(2)}) collective-permute-start(bf16[1,128,1024]{2,1,0:T(8,128)(2,1)S(1)} %slice.24), channel_id=1, source_target_pairs={{0,8},{8,16},{16,24},{24,0},{1,9},{9,17},{17,25},{25,1},{2,10},{10... | collective-permute-start | bytes 786440 | tf_op jit(solution)/shard_map/ppermute | solution.py:21
  46.6 6.4 %collective-permute-start.4 = (bf16[1,128,1024]{2,1,0:T(8,128)(2,1)S(1)}, bf16[1,128,1024]{2,1,0:T(8,128)(2,1)S(1)}, u32[]{:S(2)}, u32[]{:S(2)}) collective-permute-start(bf16[1,128,1024]{2,1,0:T(8,128)(2,1)S(1)} %slice.25), channel_id=1, source_target_pairs={{0,24},{8,0},{16,8},{24,16},{1,25},{9,1},{17,9},{25,17},{2,26},{10... | collective-permute-start | bytes 786440 | tf_op jit(solution)/shard_map/ppermute | solution.py:21
  55.3 3.5 %collective-permute-start.5 = (bf16[712,512]{1,0:T(8,128)(2,1)S(1)}, bf16[712,512]{1,0:T(8,128)(2,1)S(1)}, u32[]{:S(2)}, u32[]{:S(2)}) collective-permute-start(bf16[712,512]{1,0:T(8,128)(2,1)S(1)} %get-tuple-element.13), channel_id=1, source_target_pairs={{0,1},{1,0},{2,3},{3,2},{4,5},{5,4},{6,7},{7,6},{8,9},{9,8},{10,11... | collective-permute-start | bytes 2187272 | tf_op jit(solution)/shard_map/ppermute | solution.py:21
  55.4 3.7 %copy-start.3 = (bf16[2,4,2,8,2048]{4,3,2,1,0:T(8,128)(2,1)}, bf16[2,4,2,8,2048]{4,3,2,1,0:T(8,128)(2,1)S(1)}, u32[]{:S(2)}) copy-start(bf16[2,4,2,8,2048]{4,3,2,1,0:T(8,128)(2,1)S(1)} %bitcast_dynamic-update-slice_fusion.8) | copy-start | bytes 1572868
  55.5 15.6 %collective-permute-start.12 = (bf16[2,64,2048]{2,1,0:T(8,128)(2,1)S(1)}, bf16[2,64,2048]{2,1,0:T(8,128)(2,1)S(1)}, u32[]{:S(2)}, u32[]{:S(2)}) collective-permute-start(bf16[2,64,2048]{2,1,0:T(8,128)(2,1)S(1)} %bitcast.69), channel_id=1, source_target_pairs={{0,32},{32,64},{64,96},{96,128},{128,160},{160,192},{192,224},{224... | collective-permute-start | bytes 1572872 | tf_op jit(solution)/shard_map/ppermute | solution.py:21
  56.1 15.0 %collective-permute-start.13 = (bf16[2,64,2048]{2,1,0:T(8,128)(2,1)S(1)}, bf16[2,64,2048]{2,1,0:T(8,128)(2,1)S(1)}, u32[]{:S(2)}, u32[]{:S(2)}) collective-permute-start(bf16[2,64,2048]{2,1,0:T(8,128)(2,1)S(1)} %bitcast.70), channel_id=1, source_target_pairs={{0,224},{32,0},{64,32},{96,64},{128,96},{160,128},{192,160},{224,1... | collective-permute-start | bytes 1572872 | tf_op jit(solution)/shard_map/ppermute | solution.py:21
  59.1 47.7 %copy-start = (f32[2,512,512]{2,1,0:T(8,128)S(1)}, f32[2,512,512]{2,1,0:T(8,128)}, u32[]{:S(2)}) copy-start(f32[2,512,512]{2,1,0:T(8,128)} %x_ref) | copy-start | bytes 6291460
  59.1 29.9 %collective-permute-start.6 = (bf16[712,512]{1,0:T(8,128)(2,1)S(1)}, bf16[712,512]{1,0:T(8,128)(2,1)S(1)}, u32[]{:S(2)}, u32[]{:S(2)}) collective-permute-start(bf16[712,512]{1,0:T(8,128)(2,1)S(1)} %get-tuple-element.19), channel_id=1, source_target_pairs={{0,2},{2,0},{1,3},{3,1},{4,6},{6,4},{5,7},{7,5},{8,10},{10,8},{9,1... | collective-permute-start | bytes 2187272 | tf_op jit(solution)/shard_map/ppermute | solution.py:21
  71.1 31.6 %copy-start.7 = (bf16[2,64,2048]{2,1,0:T(8,128)(2,1)}, bf16[2,64,2048]{2,1,0:T(8,128)(2,1)S(1)}, u32[]{:S(2)}) copy-start(bf16[2,64,2048]{2,1,0:T(8,128)(2,1)S(1)} %collective-permute-done.12.refs_1_) | copy-start | bytes 1572868
  71.1 14.7 %collective-permute-start.14 = (bf16[2,64,2048]{2,1,0:T(8,128)(2,1)S(1)}, bf16[2,64,2048]{2,1,0:T(8,128)(2,1)S(1)}, u32[]{:S(2)}, u32[]{:S(2)}) collective-permute-start(bf16[2,64,2048]{2,1,0:T(8,128)(2,1)S(1)} %collective-permute-done.12.refs_1_), channel_id=1, source_target_pairs={{0,32},{32,64},{64,96},{96,128},{128,160},{160,192},{192,224},{224... | collective-permute-start | bytes 1572872 | tf_op jit(solution)/shard_map/ppermute | solution.py:21
  71.1 34.8 %copy-start.8 = (bf16[2,64,2048]{2,1,0:T(8,128)(2,1)}, bf16[2,64,2048]{2,1,0:T(8,128)(2,1)S(1)}, u32[]{:S(2)}) copy-start(bf16[2,64,2048]{2,1,0:T(8,128)(2,1)S(1)} %collective-permute-done.13.refs_2_) | copy-start | bytes 1572868
  71.1 14.7 %collective-permute-start.15 = (bf16[2,64,2048]{2,1,0:T(8,128)(2,1)S(1)}, bf16[2,64,2048]{2,1,0:T(8,128)(2,1)S(1)}, u32[]{:S(2)}, u32[]{:S(2)}) collective-permute-start(bf16[2,64,2048]{2,1,0:T(8,128)(2,1)S(1)} %collective-permute-done.13.refs_2_), channel_id=1, source_target_pairs={{0,224},{32,0},{64,32},{96,64},{128,96},{160,128},{192,160},{224,1... | collective-permute-start | bytes 1572872 | tf_op jit(solution)/shard_map/ppermute | solution.py:21
  85.7 20.1 %copy-start.9 = (bf16[2,64,2048]{2,1,0:T(8,128)(2,1)}, bf16[2,64,2048]{2,1,0:T(8,128)(2,1)S(1)}, u32[]{:S(2)}) copy-start(bf16[2,64,2048]{2,1,0:T(8,128)(2,1)S(1)} %collective-permute-done.14.refs_3_) | copy-start | bytes 1572868
  85.7 13.8 %collective-permute-start.16 = (bf16[2,64,2048]{2,1,0:T(8,128)(2,1)S(1)}, bf16[2,64,2048]{2,1,0:T(8,128)(2,1)S(1)}, u32[]{:S(2)}, u32[]{:S(2)}) collective-permute-start(bf16[2,64,2048]{2,1,0:T(8,128)(2,1)S(1)} %collective-permute-done.14.refs_3_), channel_id=1, source_target_pairs={{0,32},{32,64},{64,96},{96,128},{128,160},{160,192},{192,224},{224... | collective-permute-start | bytes 1572872 | tf_op jit(solution)/shard_map/ppermute | solution.py:21
  85.7 20.1 %copy-start.10 = (bf16[2,64,2048]{2,1,0:T(8,128)(2,1)}, bf16[2,64,2048]{2,1,0:T(8,128)(2,1)S(1)}, u32[]{:S(2)}) copy-start(bf16[2,64,2048]{2,1,0:T(8,128)(2,1)S(1)} %collective-permute-done.15.refs_4_) | copy-start | bytes 1572868
  85.7 15.3 %collective-permute-start.17 = (bf16[2,64,2048]{2,1,0:T(8,128)(2,1)S(1)}, bf16[2,64,2048]{2,1,0:T(8,128)(2,1)S(1)}, u32[]{:S(2)}, u32[]{:S(2)}) collective-permute-start(bf16[2,64,2048]{2,1,0:T(8,128)(2,1)S(1)} %collective-permute-done.15.refs_4_), channel_id=1, source_target_pairs={{0,224},{32,0},{64,32},{96,64},{128,96},{160,128},{192,160},{224,1... | collective-permute-start | bytes 1572872 | tf_op jit(solution)/shard_map/ppermute | solution.py:21
  90.0 20.0 %collective-permute-start.7 = (bf16[704,512]{1,0:T(8,128)(2,1)}, bf16[704,512]{1,0:T(8,128)(2,1)}, u32[]{:S(2)}, u32[]{:S(2)}) collective-permute-start(bf16[704,512]{1,0:T(8,128)(2,1)} %get-tuple-element.15), channel_id=1, source_target_pairs={{0,1},{1,0},{2,3},{3,2},{4,5},{5,4},{6,7},{7,6},{8,9},{9,8},{10,11... | collective-permute-start | bytes 2162696 | tf_op jit(solution)/shard_map/ppermute | solution.py:21
  99.5 0.8 copy-start.5
  101.1 7.9 %collective-permute-start.18 = (bf16[2,64,1024]{2,1,0:T(8,128)(2,1)}, bf16[2,64,1024]{2,1,0:T(8,128)(2,1)}, u32[]{:S(2)}, u32[]{:S(2)}) collective-permute-start(bf16[2,64,1024]{2,1,0:T(8,128)(2,1)} %slice.26), channel_id=1, source_target_pairs={{0,32},{32,64},{64,96},{96,128},{128,160},{160,192},{192,224},{224... | collective-permute-start | bytes 786440 | tf_op jit(solution)/shard_map/ppermute | solution.py:21
  101.1 0.8 copy-start.6
  102.6 7.4 %collective-permute-start.19 = (bf16[2,64,1024]{2,1,0:T(8,128)(2,1)}, bf16[2,64,1024]{2,1,0:T(8,128)(2,1)}, u32[]{:S(2)}, u32[]{:S(2)}) collective-permute-start(bf16[2,64,1024]{2,1,0:T(8,128)(2,1)} %slice.27), channel_id=1, source_target_pairs={{0,224},{32,0},{64,32},{96,64},{128,96},{160,128},{192,160},{224,1... | collective-permute-start | bytes 786440 | tf_op jit(solution)/shard_map/ppermute | solution.py:21
  106.7 3.3 %copy-start.1 = (f32[448,1]{1,0:T(8,128)S(1)}, f32[448,1]{1,0:T(8,128)}, u32[]{:S(2)}) copy-start(f32[448,1]{1,0:T(8,128)} %copy.21.stay_ref) | copy-start | bytes 5380

commit v3 on v2

--- a/solution.py
+++ b/solution.py
@@ -61,14 +61,16 @@
     for step in (1, 2, 3):
         ahead, behind = shift(ahead, "z", 1), shift(behind, "z", -1)
         pieces += [(step, ahead), (8 - step, behind)]
-    half = block.shape[-1] // 2
-    ahead, behind = ahead[..., :half], behind[..., half:]
-    ahead, behind = shift(ahead, "z", 1), shift(behind, "z", -1)
+    ahead, behind = shift(ahead[:1], "z", 1), shift(behind[1:], "z", -1)
     return pieces + [(4, ahead), (4, behind)]
 
 
 def far(x):
     return pltpu.with_memory_space_constraint(x, pltpu.HBM)
+
+
+def close(x):
+    return pltpu.with_memory_space_constraint(x, pltpu.VMEM)
 
 
 def dot(a, b):
@@ -94,22 +96,38 @@
         ref[pl.ds(2 * half + cross, 8), :] = counts.astype(ref.dtype)
 
 
-def join_kernel(keep_ref, given_ref, out_ref, give_ref):
+def cut_kernel(y_ref, keep_ref, given_ref, hess_ref, hess_give, cross_ref, cross_give):
+    rows, quarter = hess_ref.shape[0], cross_ref.shape[0] - 8
+    at = pl.multiple_of(rows + y_ref[0] * quarter, 64)
+    spots = ((hess_ref, hess_give, 0, 0, rows), (cross_ref, cross_give, 0, at, quarter),
+             (cross_ref, cross_give, quarter, rows + 4 * quarter, 8))
+    for ref, give, to, start, size in spots:
+        total = keep_ref[pl.ds(start, size), :] + given_ref[pl.ds(start, size), :].astype(F32)
+        ref[pl.ds(to, size), :] = total
+        give[pl.ds(to, size), :] = total.astype(BF16)
+
+
+def join_cross_kernel(keep_ref, given_ref, out_ref, scale_ref):
+    total = keep_ref[...] + given_ref[...].astype(F32)
     rows = out_ref.shape[0]
-    counts = keep_ref[pl.ds(rows, 8), :] + given_ref[pl.ds(rows, 8), :].astype(F32)
-    scale = 1.0 / (32.0 * counts[0:1, :] + counts[1:2, :])
-    joined = (keep_ref[pl.ds(0, rows), :] + given_ref[pl.ds(0, rows), :].astype(F32)) * scale
-    out_ref[...] = joined
-    give_ref[...] = joined.astype(BF16)
+    scale = 1.0 / (32.0 * total[rows : rows + 1] + total[rows + 1 : rows + 2])
+    out_ref[...] = (total[:rows] * scale).astype(BF16)
+    scale_ref[...] = jnp.broadcast_to(scale, scale_ref.shape)
+
+
+def join_kernel(backs, y_ref, keep_ref, given_ref, scale_ref, *refs):
+    out_ref, rows = refs[-1], keep_ref.shape[0]
+    total = keep_ref[...] + given_ref[...].astype(F32)
+    out_ref[pl.ds(0, rows), :] = (total * scale_ref[0:1, :]).astype(BF16)
+    for back, ref in zip(backs, refs[:-1]):
+        quarter = ref.shape[0]
+        at = rows + lax.rem(y_ref[0] + 4 - back, 4) * quarter
+        out_ref[pl.ds(pl.multiple_of(at, 64), quarter), :] = ref[...]
 
 
 def split(x):
     high = x.astype(BF16)
     return high, (x - high.astype(F32)).astype(BF16)
-
-
-def dot3(a, b):
-    return dot(a[0], b[0]) + (dot(a[0], b[1]) + dot(a[1], b[0]))
 
 
 def split_kernel(x_ref, high_ref, low_ref):
@@ -124,15 +142,12 @@
     depth, columns = pieces[0].shape[1:]
     copies = []
     for i, (back, piece) in enumerate(zip(backs, pieces)):
-        width = piece.shape[2]
-        left = columns - width if i == len(backs) - 1 else 0
         row = pl.multiple_of(lax.rem(z + 8 - back, 8) * depth, depth)
-        for p in range(2):
+        first = 1 if i == len(backs) - 1 else 0
+        for p in range(piece.shape[0]):
             copies.append(
                 pltpu.make_async_copy(
-                    piece.at[p],
-                    rows_ref.at[p, pl.ds(row, depth), pl.ds(left, width)],
-                    sems.at[i, p],
+                    piece.at[p], rows_ref.at[first + p, pl.ds(row, depth), :], sems.at[i, p]
                 )
             )
     old_copy = pltpu.make_async_copy(old_ref, old_buf, old_sem)
@@ -140,15 +155,16 @@
         copy.start()
     old_copy.start()
 
-    keep, given = keep_ref[...], given_ref[...].astype(F32)
+    keep, given = keep_ref[...], given_ref[...]
     low, top = jnp.where(zero, keep, given), jnp.where(zero, given, keep)
     half = old_ref.shape[0] // 2
-    first_hess = jnp.concatenate([low[:half], top[:half]], axis=0)
+    first_hess = jnp.concatenate([low[:half], top[:half]], axis=0).astype(F32)
     second_hess = jnp.concatenate([low[half : 2 * half], top[half : 2 * half]], axis=0)
     cross = jnp.concatenate([low[2 * half :], top[2 * half :]], axis=0)
-    second = dot3(split(second_hess), (high_ref[1], low_ref[1]))
-    first = dot3(split(first_hess - dot3(split(second), split(cross))), (high_ref[0], low_ref[0]))
-    first, second = first.astype(BF16), second.astype(BF16)
+    second = (dot(second_hess, high_ref[1]) + dot(second_hess, low_ref[1])).astype(BF16)
+    high, rest = split(first_hess - dot(second, cross))
+    first = dot(high, high_ref[0]) + (dot(high, low_ref[0]) + dot(rest, high_ref[0]))
+    first = first.astype(BF16)
 
     for copy in copies:
         copy.wait()
@@ -179,14 +195,14 @@
     onehot = mine[:, None] == jnp.arange(local, dtype=jnp.int32)[None, :]
     select = onehot.astype(BF16)
 
-    rows = jnp.dot(select, down_weight, preferred_element_type=F32).astype(BF16)
-
     slot = jnp.arange(tokens, dtype=jnp.int32)
     valid = (slot < counts[0]).astype(F32)
     gate = gate_up[:, 0, :].astype(F32)
     up = gate_up[:, 1, :].astype(F32)
     hidden = (jax.nn.silu(gate) * up * valid[:, None]).astype(BF16)
     acts = lax.dot_general(select, hidden, NT, preferred_element_type=F32).astype(BF16)
+    acts, select = lax.optimization_barrier((acts, select))
+    rows = jnp.dot(select, down_weight, preferred_element_type=F32).astype(BF16)
 
     acts = to_all(acts, "z").reshape(128, tokens)
     near = gather_rows(rows.reshape(2, share, columns))
@@ -217,21 +233,40 @@
         name="partial",
     )(core[None], counts, hidden.T, acts)
     given = shift(give, "co", 1)
-    keep = keep + given.astype(F32)
-    give = keep.astype(BF16)
-    given = shift(give, "xl", 1)
-    keep, give = pl.pallas_call(
-        join_kernel,
-        out_shape=(
-            jax.ShapeDtypeStruct((rows_in_half, panel), F32),
-            jax.ShapeDtypeStruct((rows_in_half, panel), BF16),
+    y = lax.axis_index("y").astype(jnp.int32)[None]
+    small = pltpu.CompilerParams(vmem_limit_bytes=8 * 1024 * 1024)
+    quarter = cross_half // 4
+    hess, hess_give, cross, cross_give = pl.pallas_call(
+        cut_kernel,
+        out_shape=tuple(
+            jax.ShapeDtypeStruct((n, panel), d) for n in (2 * half, quarter + 8) for d in (F32, BF16)
         ),
+        in_specs=[SMEM, VMEM, VMEM],
+        out_specs=(VMEM,) * 4,
+        compiler_params=small,
+        name="cut",
+    )(y, keep, given)
+    cross_given = shift(cross_give, "xl", 1)
+    hess_given = shift(hess_give, "xl", 1)
+    cross, scale = pl.pallas_call(
+        join_cross_kernel,
+        out_shape=(jax.ShapeDtypeStruct((quarter, panel), BF16), jax.ShapeDtypeStruct((8, panel), F32)),
         in_specs=[VMEM, VMEM],
         out_specs=(VMEM, VMEM),
-        compiler_params=pltpu.CompilerParams(vmem_limit_bytes=12 * 1024 * 1024),
+        compiler_params=small,
+        name="join_cross",
+    )(cross, cross_given)
+    quarters = [(0, cross)] + [(k, shift(cross, "y", k)) for k in (1, 3, 2)]
+    keep = pl.pallas_call(
+        functools.partial(join_kernel, [k for k, _ in quarters]),
+        out_shape=jax.ShapeDtypeStruct((rows_in_half, panel), BF16),
+        in_specs=[SMEM] + [VMEM] * 7,
+        out_specs=VMEM,
+        compiler_params=small,
         name="join",
-    )(keep, given)
-    given = shift(give, "co", 1)
+    )(y, hess, hess_given, scale, *[piece for _, piece in quarters])
+    keep = close(keep)
+    given = close(shift(keep, "co", 1))
 
     stay = jnp.where(jnp.any(onehot, axis=0), 0.0, 1.0).astype(F32)[:, None]
     at = jnp.stack([core, lax.axis_index("z").astype(jnp.int32)])

time: 121 us -> 111 us (0.917)
  the two profiles are of different devices: /device:TPU:8 before, /device:TPU:124 now
where the time goes in v3:
time: 111 us
  waiting for transfers between devices  56.7 us (51%)
  starting transfers between devices  33.9 us (31%)
  Pallas kernels  10.8 us (10%)
  local copies, waits for them, and re-layouts  4.13 us (4%)
  matrix products  2.65 us (2%)
  other arithmetic  1.6 us (1%)
  between operations  1.26 us (1%)
    ppermute x24, waiting for transfers between devices, shift(): return lax.ppermute(x, axis, [(i, (i + by) % n) for i in range(n)])  56.7 us
    ppermute x24, starting transfers between devices, shift(): return lax.ppermute(x, axis, [(i, (i + by) % n) for i in range(n)])  26.2 us
    pallas_call x1, Pallas kernels, compute(): pl.pallas_call(functools.partial(tail_kernel, backs), out_shape=jax.Shape...  8.22 us
    all_to_all x1, starting transfers between devices, to_all(): lax.all_to_all(jnp.broadcast_to(x, (n, *x.shape)), axes, split_axis=0, co...  7.66 us
    dot_general x1, matrix products, compute(): lax.dot_general(select, hidden, NT, preferred_element_type=F32).astype(BF16)  2.29 us
  transfers between devices with their start and end apart: 25, of which 13 were waited for; matrix products, arithmetic and copies ran while one was open for 3% of the time, Pallas kernels for 2%

profile of v3, /device:TPU:124, one launch (start us, length us, event | category | flops | bytes accessed | tf_op | source)
XLA Modules:
  0.0 111.0 jit_solution(16826839488645157490)
XLA Ops:
  0.0 0.8 fusion.11
  1.6 2.3 %convolution_convert_fusion.1 = bf16[16,1024]{1,0:T(8,128)(2,1)S(1)} fusion(s32[16]{0:T(128)S(1)} %sub.31, f32[1024]{0:T(1024)S(1)} %fusion.10, bf16[1024,2,448]{0,2,1:T(8,128)(2,1)} %param.5), kind=kOutput, calls=%fused_computation.9 | convolution fusion | flops 18832384 | bytes 1871936 | tf_op jit(solution)/shard_map/dot_general | solution.py:203
  3.9 0.7 broadcast_in_dim.64
  4.6 7.7 %all-to-all-start = ((bf16[8,16,1024]{2,1,0:T(8,128)(2,1)}), bf16[8,16,1024]{2,1,0:T(8,128)(2,1)S(1)}, u32[]{:S(2)}, u32[]{:S(2)}) async-start(bf16[8,16,1024]{2,1,0:T(8,128)(2,1)} %broadcast_in_dim.64), calls=%async_computation | async-start | bytes 524288 | tf_op jit(solution)/shard_map/all_to_all | solution.py:26
  13.8 0.6 fusion.15.hidden_ref
  14.5 3.9 %collective-permute-done.12 = bf16[2,8,2048]{2,1,0:T(8,128)(2,1)S(1)} collective-permute-done((bf16[2,8,2048]{2,1,0:T(8,128)(2,1)S(1)}, bf16[2,8,2048]{2,1,0:T(8,128)(2,1)S(1)}, u32[]{:S(2)}, u32[]{:S(2)}) %collective-permute-start.12) | collective-permute-done | bytes 65568 | tf_op jit(solution)/shard_map/ppermute | solution.py:21
  18.8 1.8 %collective-permute-start.14 = (bf16[2,2,8,2048]{3,2,1,0:T(8,128)(2,1)S(1)}, bf16[2,2,8,2048]{3,2,1,0:T(8,128)(2,1)S(1)}, u32[]{:S(2)}, u32[]{:S(2)}) collective-permute-start(bf16[2,2,8,2048]{3,2,1,0:T(8,128)(2,1)S(1)} %bitcast_dynamic-update-slice_fusion.10), channel_id=1, source_target_pairs={{0,24},{8,0},{16,8},{24,16},{1,25},{9,1},{17,9},{25,17},{2,26},{10... | collective-permute-start | bytes 393224 | tf_op jit(solution)/shard_map/ppermute | solution.py:21
  20.6 1.2 %collective-permute-start.15 = (bf16[2,2,8,2048]{3,2,1,0:T(8,128)(2,1)S(1)}, bf16[2,2,8,2048]{3,2,1,0:T(8,128)(2,1)S(1)}, u32[]{:S(2)}, u32[]{:S(2)}) collective-permute-start(bf16[2,2,8,2048]{3,2,1,0:T(8,128)(2,1)S(1)} %bitcast_dynamic-update-slice_fusion.10), channel_id=1, source_target_pairs={{0,16},{8,24},{16,0},{24,8},{1,17},{9,25},{17,1},{25,9},{2,18},{10... | collective-permute-start | bytes 393224 | tf_op jit(solution)/shard_map/ppermute | solution.py:21
  21.9 2.4 %collective-permute-done.13 = bf16[2,2,8,2048]{3,2,1,0:T(8,128)(2,1)S(1)} collective-permute-done((bf16[2,2,8,2048]{3,2,1,0:T(8,128)(2,1)S(1)}, bf16[2,2,8,2048]{3,2,1,0:T(8,128)(2,1)S(1)}, u32[]{:S(2)}, u32[]{:S(2)}) %collective-permute-start.13) | collective-permute-done | bytes 131104 | tf_op jit(solution)/shard_map/ppermute | solution.py:21
  24.6 0.8 collective-permute-done.14
  25.5 6.7 %collective-permute-done = bf16[128,1024]{1,0:T(8,128)(2,1)S(1)} collective-permute-done((bf16[128,1024]{1,0:T(8,128)(2,1)S(1)}, bf16[128,1024]{1,0:T(8,128)(2,1)S(1)}, u32[]{:S(2)}, u32[]{:S(2)}) %collective-permute-start) | collective-permute-done | bytes 262176 | tf_op jit(solution)/shard_map/ppermute | solution.py:21
  32.2 2.2 %collective-permute-start.1 = (bf16[2,128,1024]{2,1,0:T(8,128)(2,1)S(1)}, bf16[2,128,1024]{2,1,0:T(8,128)(2,1)S(1)}, u32[]{:S(2)}, u32[]{:S(2)}) collective-permute-start(bf16[2,128,1024]{2,1,0:T(8,128)(2,1)S(1)} %bitcast_dynamic-update-slice_fusion.3), channel_id=1, source_target_pairs={{0,8},{8,16},{16,24},{24,0},{1,9},{9,17},{17,25},{25,1},{2,10},{10... | collective-permute-start | bytes 1572872 | tf_op jit(solution)/shard_map/ppermute | solution.py:21
  34.5 2.8 %collective-permute-start.16 = (bf16[2,64,2048]{2,1,0:T(8,128)(2,1)S(1)}, bf16[2,64,2048]{2,1,0:T(8,128)(2,1)S(1)}, u32[]{:S(2)}, u32[]{:S(2)}) collective-permute-start(bf16[2,64,2048]{2,1,0:T(8,128)(2,1)S(1)} %bitcast.71), channel_id=1, source_target_pairs={{0,32},{32,64},{64,96},{96,128},{128,160},{160,192},{192,224},{224... | collective-permute-start | bytes 1572872 | tf_op jit(solution)/shard_map/ppermute | solution.py:21
  37.5 6.8 %collective-permute-done.1 = bf16[2,128,1024]{2,1,0:T(8,128)(2,1)S(1)} collective-permute-done((bf16[2,128,1024]{2,1,0:T(8,128)(2,1)S(1)}, bf16[2,128,1024]{2,1,0:T(8,128)(2,1)S(1)}, u32[]{:S(2)}, u32[]{:S(2)}) %collective-permute-start.1) | collective-permute-done | bytes 524320 | tf_op jit(solution)/shard_map/ppermute | solution.py:21
  44.3 3.0 %collective-permute-start.3 = (bf16[1,128,1024]{2,1,0:T(8,128)(2,1)S(1)}, bf16[1,128,1024]{2,1,0:T(8,128)(2,1)S(1)}, u32[]{:S(2)}, u32[]{:S(2)}) collective-permute-start(bf16[1,128,1024]{2,1,0:T(8,128)(2,1)S(1)} %slice.24), channel_id=1, source_target_pairs={{0,8},{8,16},{16,24},{24,0},{1,9},{9,17},{17,25},{25,1},{2,10},{10... | collective-permute-start | bytes 786440 | tf_op jit(solution)/shard_map/ppermute | solution.py:21
  47.7 3.6 %collective-permute-done.3 = bf16[1,128,1024]{2,1,0:T(8,128)(2,1)S(1)} collective-permute-done((bf16[1,128,1024]{2,1,0:T(8,128)(2,1)S(1)}, bf16[1,128,1024]{2,1,0:T(8,128)(2,1)S(1)}, u32[]{:S(2)}, u32[]{:S(2)}) %collective-permute-start.3) | collective-permute-done | bytes 262176 | tf_op jit(solution)/shard_map/ppermute | solution.py:21
  51.3 3.9 %collective-permute-done.4 = bf16[1,128,1024]{2,1,0:T(8,128)(2,1)S(1)} collective-permute-done((bf16[1,128,1024]{2,1,0:T(8,128)(2,1)S(1)}, bf16[1,128,1024]{2,1,0:T(8,128)(2,1)S(1)}, u32[]{:S(2)}, u32[]{:S(2)}) %collective-permute-start.4) | collective-permute-done | bytes 262176 | tf_op jit(solution)/shard_map/ppermute | solution.py:21
  55.4 2.0 %partial.1 = (f32[712,512]{1,0:T(8,128)S(1)}, bf16[712,512]{1,0:T(8,128)(2,1)S(1)}) custom-call(s32[1]{0:T(128)} %bitcast.core_ref, s32[1]{0:T(128)} %copy.34.count_ref, bf16[448,1024]{1,0:T(8,128)(2,1)S(1)} %fusion.15.hidden_ref, bf16[2,512,1024]{2,1,0:T(8,128)(2,1)S(1)} %bitcast.69), custom_call_target="tpu_custom_call" | custom-call | tf_op jit(solution)/shard_map/partial/pallas_call | solution.py:224
  57.7 2.8 %collective-permute-start.18 = (bf16[2,64,2048]{2,1,0:T(8,128)(2,1)S(1)}, bf16[2,64,2048]{2,1,0:T(8,128)(2,1)S(1)}, u32[]{:S(2)}, u32[]{:S(2)}) collective-permute-start(bf16[2,64,2048]{2,1,0:T(8,128)(2,1)S(1)} %collective-permute-done.16.refs_1_), channel_id=1, source_target_pairs={{0,32},{32,64},{64,96},{96,128},{128,160},{160,192},{192,224},{224... | collective-permute-start | bytes 1572872 | tf_op jit(solution)/shard_map/ppermute | solution.py:21
  60.7 1.3 %collective-permute-start.6 = (bf16[448,512]{1,0:T(8,128)(2,1)S(1)}, bf16[448,512]{1,0:T(8,128)(2,1)S(1)}, u32[]{:S(2)}, u32[]{:S(2)}) collective-permute-start(bf16[448,512]{1,0:T(8,128)(2,1)S(1)} %get-tuple-element.22), channel_id=1, source_target_pairs={{0,2},{2,0},{1,3},{3,1},{4,6},{6,4},{5,7},{7,5},{8,10},{10,8},{9,1... | collective-permute-start | bytes 1376264 | tf_op jit(solution)/shard_map/ppermute | solution.py:21
  61.9 0.8 collective-permute-start.7
  62.8 9.4 %collective-permute-done.18.refs_3_ = bf16[2,64,2048]{2,1,0:T(8,128)(2,1)S(1)} collective-permute-done((bf16[2,64,2048]{2,1,0:T(8,128)(2,1)S(1)}, bf16[2,64,2048]{2,1,0:T(8,128)(2,1)S(1)}, u32[]{:S(2)}, u32[]{:S(2)}) %collective-permute-start.18) | collective-permute-done | bytes 524320 | tf_op jit(solution)/shard_map/ppermute | solution.py:21
  72.2 3.7 %collective-permute-start.20 = (bf16[2,64,2048]{2,1,0:T(8,128)(2,1)S(1)}, bf16[2,64,2048]{2,1,0:T(8,128)(2,1)S(1)}, u32[]{:S(2)}, u32[]{:S(2)}) collective-permute-start(bf16[2,64,2048]{2,1,0:T(8,128)(2,1)S(1)} %collective-permute-done.18.refs_3_), channel_id=1, source_target_pairs={{0,32},{32,64},{64,96},{96,128},{128,160},{160,192},{192,224},{224... | collective-permute-start | bytes 1572872 | tf_op jit(solution)/shard_map/ppermute | solution.py:21
  76.1 1.4 %collective-permute-start.8 = (bf16[64,512]{1,0:T(8,128)(2,1)S(1)}, bf16[64,512]{1,0:T(8,128)(2,1)S(1)}, u32[]{:S(2)}, u32[]{:S(2)}) collective-permute-start(bf16[64,512]{1,0:T(8,128)(2,1)S(1)} %get-tuple-element.26.refs_0_), channel_id=1, source_target_pairs={{0,8},{8,16},{16,24},{24,0},{1,9},{9,17},{17,25},{25,1},{2,10},{10... | collective-permute-start | bytes 196616 | tf_op jit(solution)/shard_map/ppermute | solution.py:21
  77.5 4.3 %collective-permute-done.10.refs_3_ = bf16[64,512]{1,0:T(8,128)(2,1)S(1)} collective-permute-done((bf16[64,512]{1,0:T(8,128)(2,1)S(1)}, bf16[64,512]{1,0:T(8,128)(2,1)S(1)}, u32[]{:S(2)}, u32[]{:S(2)}) %collective-permute-start.10) | collective-permute-done | bytes 65568 | tf_op jit(solution)/shard_map/ppermute | solution.py:21
  81.9 5.5 %collective-permute-done.9.refs_2_ = bf16[64,512]{1,0:T(8,128)(2,1)S(1)} collective-permute-done((bf16[64,512]{1,0:T(8,128)(2,1)S(1)}, bf16[64,512]{1,0:T(8,128)(2,1)S(1)}, u32[]{:S(2)}, u32[]{:S(2)}) %collective-permute-start.9) | collective-permute-done | bytes 65568 | tf_op jit(solution)/shard_map/ppermute | solution.py:21
  87.6 0.8 slice.26
  88.4 3.5 %collective-permute-start.22 = (bf16[1,64,2048]{2,1,0:T(8,128)(2,1)}, bf16[1,64,2048]{2,1,0:T(8,128)(2,1)S(1)}, u32[]{:S(2)}, u32[]{:S(2)}) collective-permute-start(bf16[1,64,2048]{2,1,0:T(8,128)(2,1)} %slice.26), channel_id=1, source_target_pairs={{0,32},{32,64},{64,96},{96,128},{128,160},{160,192},{192,224},{224... | collective-permute-start | bytes 786440 | tf_op jit(solution)/shard_map/ppermute | solution.py:21
  91.9 0.8 slice.27
  93.3 5.1 %collective-permute-done.22.refs_7_ = bf16[1,64,2048]{2,1,0:T(8,128)(2,1)S(1)} collective-permute-done((bf16[1,64,2048]{2,1,0:T(8,128)(2,1)}, bf16[1,64,2048]{2,1,0:T(8,128)(2,1)S(1)}, u32[]{:S(2)}, u32[]{:S(2)}) %collective-permute-start.22) | collective-permute-done | bytes 262176 | tf_op jit(solution)/shard_map/ppermute | solution.py:21
  98.4 4.2 %collective-permute-done.23.refs_8_ = bf16[1,64,2048]{2,1,0:T(8,128)(2,1)} collective-permute-done((bf16[1,64,2048]{2,1,0:T(8,128)(2,1)}, bf16[1,64,2048]{2,1,0:T(8,128)(2,1)}, u32[]{:S(2)}, u32[]{:S(2)}) %collective-permute-start.23) | collective-permute-done | bytes 262176 | tf_op jit(solution)/shard_map/ppermute | solution.py:21
  102.6 8.2 %tail.1 = bf16[448,2048]{1,0:T(8,128)(2,1)} custom-call(s32[2]{0:T(128)S(1)} %pad_add_fusion.at_ref, bf16[704,512]{1,0:T(8,128)(2,1)S(1)} %join.1.keep_ref, bf16[704,512]{1,0:T(8,128)(2,1)} %collective-permute-done.11.given_ref, bf16[2,512,512]{2,1,0:T(8,128)(2,1)S(1)} %get-tuple-element.29.high_ref, bf16[2,512,512]{2,1,0:T(8,128)(2,1)S(1)} %get-tuple-element.30.low_ref, ...), custom_call_target="tpu_custom_call" | custom-call | tf_op jit(solution)/shard_map/tail/pallas_call | solution.py:274
  (77 shorter events, 4.8 us)
Async XLA Ops:
  1.6 10.7 %copy-start.1 = (bf16[448,2048]{1,0:T(8,128)(2,1)S(1)}, bf16[448,2048]{1,0:T(8,128)(2,1)}, u32[]{:S(2)}) copy-start(bf16[448,2048]{1,0:T(8,128)(2,1)} %refs_9_.1) | copy-start | bytes 5505028
  4.6 19.6 %all-to-all-start = ((bf16[8,16,1024]{2,1,0:T(8,128)(2,1)}), bf16[8,16,1024]{2,1,0:T(8,128)(2,1)S(1)}, u32[]{:S(2)}, u32[]{:S(2)}) async-start(bf16[8,16,1024]{2,1,0:T(8,128)(2,1)} %broadcast_in_dim.64), calls=%async_computation | async-start | bytes 524288 | tf_op jit(solution)/shard_map/all_to_all | solution.py:26
  12.7 5.8 %collective-permute-start.12 = (bf16[2,8,2048]{2,1,0:T(8,128)(2,1)S(1)}, bf16[2,8,2048]{2,1,0:T(8,128)(2,1)S(1)}, u32[]{:S(2)}, u32[]{:S(2)}) collective-permute-start(bf16[2,8,2048]{2,1,0:T(8,128)(2,1)S(1)} %bitcast.76), channel_id=1, source_target_pairs={{0,4},{4,0},{1,5},{5,1},{2,6},{6,2},{3,7},{7,3},{8,12},{12,8},{9,1... | collective-permute-start | bytes 196616 | tf_op jit(solution)/shard_map/ppermute | solution.py:21
  18.5 5.8 %collective-permute-start.13 = (bf16[2,2,8,2048]{3,2,1,0:T(8,128)(2,1)S(1)}, bf16[2,2,8,2048]{3,2,1,0:T(8,128)(2,1)S(1)}, u32[]{:S(2)}, u32[]{:S(2)}) collective-permute-start(bf16[2,2,8,2048]{3,2,1,0:T(8,128)(2,1)S(1)} %bitcast_dynamic-update-slice_fusion.10), channel_id=1, source_target_pairs={{0,8},{8,16},{16,24},{24,0},{1,9},{9,17},{17,25},{25,1},{2,10},{10... | collective-permute-start | bytes 393224 | tf_op jit(solution)/shard_map/ppermute | solution.py:21
  18.8 6.7 %collective-permute-start.14 = (bf16[2,2,8,2048]{3,2,1,0:T(8,128)(2,1)S(1)}, bf16[2,2,8,2048]{3,2,1,0:T(8,128)(2,1)S(1)}, u32[]{:S(2)}, u32[]{:S(2)}) collective-permute-start(bf16[2,2,8,2048]{3,2,1,0:T(8,128)(2,1)S(1)} %bitcast_dynamic-update-slice_fusion.10), channel_id=1, source_target_pairs={{0,24},{8,0},{16,8},{24,16},{1,25},{9,1},{17,9},{25,17},{2,26},{10... | collective-permute-start | bytes 393224 | tf_op jit(solution)/shard_map/ppermute | solution.py:21
  20.6 13.9 %collective-permute-start.15 = (bf16[2,2,8,2048]{3,2,1,0:T(8,128)(2,1)S(1)}, bf16[2,2,8,2048]{3,2,1,0:T(8,128)(2,1)S(1)}, u32[]{:S(2)}, u32[]{:S(2)}) collective-permute-start(bf16[2,2,8,2048]{3,2,1,0:T(8,128)(2,1)S(1)} %bitcast_dynamic-update-slice_fusion.10), channel_id=1, source_target_pairs={{0,16},{8,24},{16,0},{24,8},{1,17},{9,25},{17,1},{25,9},{2,18},{10... | collective-permute-start | bytes 393224 | tf_op jit(solution)/shard_map/ppermute | solution.py:21
  24.3 8.0 %collective-permute-start = (bf16[128,1024]{1,0:T(8,128)(2,1)S(1)}, bf16[128,1024]{1,0:T(8,128)(2,1)S(1)}, u32[]{:S(2)}, u32[]{:S(2)}) collective-permute-start(bf16[128,1024]{1,0:T(8,128)(2,1)S(1)} %bitcast.74), channel_id=1, source_target_pairs={{0,4},{4,0},{1,5},{5,1},{2,6},{6,2},{3,7},{7,3},{8,12},{12,8},{9,1... | collective-permute-start | bytes 786440 | tf_op jit(solution)/shard_map/ppermute | solution.py:21
  32.2 12.1 %collective-permute-start.1 = (bf16[2,128,1024]{2,1,0:T(8,128)(2,1)S(1)}, bf16[2,128,1024]{2,1,0:T(8,128)(2,1)S(1)}, u32[]{:S(2)}, u32[]{:S(2)}) collective-permute-start(bf16[2,128,1024]{2,1,0:T(8,128)(2,1)S(1)} %bitcast_dynamic-update-slice_fusion.3), channel_id=1, source_target_pairs={{0,8},{8,16},{16,24},{24,0},{1,9},{9,17},{17,25},{25,1},{2,10},{10... | collective-permute-start | bytes 1572872 | tf_op jit(solution)/shard_map/ppermute | solution.py:21
  34.4 13.0 %collective-permute-start.2 = (bf16[2,128,1024]{2,1,0:T(8,128)(2,1)S(1)}, bf16[2,128,1024]{2,1,0:T(8,128)(2,1)S(1)}, u32[]{:S(2)}, u32[]{:S(2)}) collective-permute-start(bf16[2,128,1024]{2,1,0:T(8,128)(2,1)S(1)} %bitcast_dynamic-update-slice_fusion.3), channel_id=1, source_target_pairs={{0,24},{8,0},{16,8},{24,16},{1,25},{9,1},{17,9},{25,17},{2,26},{10... | collective-permute-start | bytes 1572872 | tf_op jit(solution)/shard_map/ppermute | solution.py:21
  34.5 9.9 %copy-start.2 = (bf16[2,4,2,8,2048]{4,3,2,1,0:T(8,128)(2,1)}, bf16[2,4,2,8,2048]{4,3,2,1,0:T(8,128)(2,1)S(1)}, u32[]{:S(2)}) copy-start(bf16[2,4,2,8,2048]{4,3,2,1,0:T(8,128)(2,1)S(1)} %bitcast_dynamic-update-slice_fusion.8) | copy-start | bytes 1572868
  34.5 23.2 %collective-permute-start.16 = (bf16[2,64,2048]{2,1,0:T(8,128)(2,1)S(1)}, bf16[2,64,2048]{2,1,0:T(8,128)(2,1)S(1)}, u32[]{:S(2)}, u32[]{:S(2)}) collective-permute-start(bf16[2,64,2048]{2,1,0:T(8,128)(2,1)S(1)} %bitcast.71), channel_id=1, source_target_pairs={{0,32},{32,64},{64,96},{96,128},{128,160},{160,192},{192,224},{224... | collective-permute-start | bytes 1572872 | tf_op jit(solution)/shard_map/ppermute | solution.py:21
  37.2 23.2 %collective-permute-start.17 = (bf16[2,64,2048]{2,1,0:T(8,128)(2,1)S(1)}, bf16[2,64,2048]{2,1,0:T(8,128)(2,1)S(1)}, u32[]{:S(2)}, u32[]{:S(2)}) collective-permute-start(bf16[2,64,2048]{2,1,0:T(8,128)(2,1)S(1)} %bitcast.72), channel_id=1, source_target_pairs={{0,224},{32,0},{64,32},{96,64},{128,96},{160,128},{192,160},{224,1... | collective-permute-start | bytes 1572872 | tf_op jit(solution)/shard_map/ppermute | solution.py:21
  44.3 6.9 %collective-permute-start.3 = (bf16[1,128,1024]{2,1,0:T(8,128)(2,1)S(1)}, bf16[1,128,1024]{2,1,0:T(8,128)(2,1)S(1)}, u32[]{:S(2)}, u32[]{:S(2)}) collective-permute-start(bf16[1,128,1024]{2,1,0:T(8,128)(2,1)S(1)} %slice.24), channel_id=1, source_target_pairs={{0,8},{8,16},{16,24},{24,0},{1,9},{9,17},{17,25},{25,1},{2,10},{10... | collective-permute-start | bytes 786440 | tf_op jit(solution)/shard_map/ppermute | solution.py:21
  47.5 7.7 %collective-permute-start.4 = (bf16[1,128,1024]{2,1,0:T(8,128)(2,1)S(1)}, bf16[1,128,1024]{2,1,0:T(8,128)(2,1)S(1)}, u32[]{:S(2)}, u32[]{:S(2)}) collective-permute-start(bf16[1,128,1024]{2,1,0:T(8,128)(2,1)S(1)} %slice.25), channel_id=1, source_target_pairs={{0,24},{8,0},{16,8},{24,16},{1,25},{9,1},{17,9},{25,17},{2,26},{10... | collective-permute-start | bytes 786440 | tf_op jit(solution)/shard_map/ppermute | solution.py:21
  57.4 3.1 %collective-permute-start.5 = (bf16[712,512]{1,0:T(8,128)(2,1)S(1)}, bf16[712,512]{1,0:T(8,128)(2,1)S(1)}, u32[]{:S(2)}, u32[]{:S(2)}) collective-permute-start(bf16[712,512]{1,0:T(8,128)(2,1)S(1)} %get-tuple-element.20), channel_id=1, source_target_pairs={{0,1},{1,0},{2,3},{3,2},{4,5},{5,4},{6,7},{7,6},{8,9},{9,8},{10,11... | collective-permute-start | bytes 2187272 | tf_op jit(solution)/shard_map/ppermute | solution.py:21
  57.7 29.8 %copy-start.6 = (bf16[2,64,2048]{2,1,0:T(8,128)(2,1)}, bf16[2,64,2048]{2,1,0:T(8,128)(2,1)S(1)}, u32[]{:S(2)}) copy-start(bf16[2,64,2048]{2,1,0:T(8,128)(2,1)S(1)} %collective-permute-done.16.refs_1_) | copy-start | bytes 1572868
  57.7 14.5 %collective-permute-start.18 = (bf16[2,64,2048]{2,1,0:T(8,128)(2,1)S(1)}, bf16[2,64,2048]{2,1,0:T(8,128)(2,1)S(1)}, u32[]{:S(2)}, u32[]{:S(2)}) collective-permute-start(bf16[2,64,2048]{2,1,0:T(8,128)(2,1)S(1)} %collective-permute-done.16.refs_1_), channel_id=1, source_target_pairs={{0,32},{32,64},{64,96},{96,128},{128,160},{160,192},{192,224},{224... | collective-permute-start | bytes 1572872 | tf_op jit(solution)/shard_map/ppermute | solution.py:21
  60.5 27.0 %copy-start.7 = (bf16[2,64,2048]{2,1,0:T(8,128)(2,1)}, bf16[2,64,2048]{2,1,0:T(8,128)(2,1)S(1)}, u32[]{:S(2)}) copy-start(bf16[2,64,2048]{2,1,0:T(8,128)(2,1)S(1)} %collective-permute-done.17.refs_2_) | copy-start | bytes 1572868
  60.5 15.4 %collective-permute-start.19 = (bf16[2,64,2048]{2,1,0:T(8,128)(2,1)S(1)}, bf16[2,64,2048]{2,1,0:T(8,128)(2,1)S(1)}, u32[]{:S(2)}, u32[]{:S(2)}) collective-permute-start(bf16[2,64,2048]{2,1,0:T(8,128)(2,1)S(1)} %collective-permute-done.17.refs_2_), channel_id=1, source_target_pairs={{0,224},{32,0},{64,32},{96,64},{128,96},{160,128},{192,160},{224,1... | collective-permute-start | bytes 1572872 | tf_op jit(solution)/shard_map/ppermute | solution.py:21
  60.7 26.7 %collective-permute-start.6 = (bf16[448,512]{1,0:T(8,128)(2,1)S(1)}, bf16[448,512]{1,0:T(8,128)(2,1)S(1)}, u32[]{:S(2)}, u32[]{:S(2)}) collective-permute-start(bf16[448,512]{1,0:T(8,128)(2,1)S(1)} %get-tuple-element.22), channel_id=1, source_target_pairs={{0,2},{2,0},{1,3},{3,1},{4,6},{6,4},{5,7},{7,5},{8,10},{10,8},{9,1... | collective-permute-start | bytes 1376264 | tf_op jit(solution)/shard_map/ppermute | solution.py:21
  61.9 14.0 %collective-permute-start.7 = (bf16[72,512]{1,0:T(8,128)(2,1)S(1)}, bf16[72,512]{1,0:T(8,128)(2,1)S(1)}, u32[]{:S(2)}, u32[]{:S(2)}) collective-permute-start(bf16[72,512]{1,0:T(8,128)(2,1)S(1)} %get-tuple-element.24), channel_id=1, source_target_pairs={{0,2},{2,0},{1,3},{3,1},{4,6},{6,4},{5,7},{7,5},{8,10},{10,8},{9,1... | collective-permute-start | bytes 221192 | tf_op jit(solution)/shard_map/ppermute | solution.py:21
  72.2 20.5 %copy-start.8 = (bf16[2,64,2048]{2,1,0:T(8,128)(2,1)}, bf16[2,64,2048]{2,1,0:T(8,128)(2,1)S(1)}, u32[]{:S(2)}) copy-start(bf16[2,64,2048]{2,1,0:T(8,128)(2,1)S(1)} %collective-permute-done.18.refs_3_) | copy-start | bytes 1572868
  72.2 15.4 %collective-permute-start.20 = (bf16[2,64,2048]{2,1,0:T(8,128)(2,1)S(1)}, bf16[2,64,2048]{2,1,0:T(8,128)(2,1)S(1)}, u32[]{:S(2)}, u32[]{:S(2)}) collective-permute-start(bf16[2,64,2048]{2,1,0:T(8,128)(2,1)S(1)} %collective-permute-done.18.refs_3_), channel_id=1, source_target_pairs={{0,32},{32,64},{64,96},{96,128},{128,160},{160,192},{192,224},{224... | collective-permute-start | bytes 1572872 | tf_op jit(solution)/shard_map/ppermute | solution.py:21
  75.9 16.8 %copy-start.9 = (bf16[2,64,2048]{2,1,0:T(8,128)(2,1)}, bf16[2,64,2048]{2,1,0:T(8,128)(2,1)S(1)}, u32[]{:S(2)}) copy-start(bf16[2,64,2048]{2,1,0:T(8,128)(2,1)S(1)} %collective-permute-done.19.refs_4_) | copy-start | bytes 1572868
  75.9 16.0 %collective-permute-start.21 = (bf16[2,64,2048]{2,1,0:T(8,128)(2,1)S(1)}, bf16[2,64,2048]{2,1,0:T(8,128)(2,1)S(1)}, u32[]{:S(2)}, u32[]{:S(2)}) collective-permute-start(bf16[2,64,2048]{2,1,0:T(8,128)(2,1)S(1)} %collective-permute-done.19.refs_4_), channel_id=1, source_target_pairs={{0,224},{32,0},{64,32},{96,64},{128,96},{160,128},{192,160},{224,1... | collective-permute-start | bytes 1572872 | tf_op jit(solution)/shard_map/ppermute | solution.py:21
  76.0 17.1 %copy-start = (f32[2,512,512]{2,1,0:T(8,128)S(1)}, f32[2,512,512]{2,1,0:T(8,128)}, u32[]{:S(2)}) copy-start(f32[2,512,512]{2,1,0:T(8,128)} %x_ref) | copy-start | bytes 6291460
  76.0 5.9 %collective-permute-start.10 = (bf16[64,512]{1,0:T(8,128)(2,1)S(1)}, bf16[64,512]{1,0:T(8,128)(2,1)S(1)}, u32[]{:S(2)}, u32[]{:S(2)}) collective-permute-start(bf16[64,512]{1,0:T(8,128)(2,1)S(1)} %get-tuple-element.26.refs_0_), channel_id=1, source_target_pairs={{0,16},{8,24},{16,0},{24,8},{1,17},{9,25},{17,1},{25,9},{2,18},{10... | collective-permute-start | bytes 196616 | tf_op jit(solution)/shard_map/ppermute | solution.py:21
  76.1 5.8 %collective-permute-start.8 = (bf16[64,512]{1,0:T(8,128)(2,1)S(1)}, bf16[64,512]{1,0:T(8,128)(2,1)S(1)}, u32[]{:S(2)}, u32[]{:S(2)}) collective-permute-start(bf16[64,512]{1,0:T(8,128)(2,1)S(1)} %get-tuple-element.26.refs_0_), channel_id=1, source_target_pairs={{0,8},{8,16},{16,24},{24,0},{1,9},{9,17},{17,25},{25,1},{2,10},{10... | collective-permute-start | bytes 196616 | tf_op jit(solution)/shard_map/ppermute | solution.py:21
  81.8 5.5 %collective-permute-start.9 = (bf16[64,512]{1,0:T(8,128)(2,1)S(1)}, bf16[64,512]{1,0:T(8,128)(2,1)S(1)}, u32[]{:S(2)}, u32[]{:S(2)}) collective-permute-start(bf16[64,512]{1,0:T(8,128)(2,1)S(1)} %get-tuple-element.26.refs_0_), channel_id=1, source_target_pairs={{0,24},{8,0},{16,8},{24,16},{1,25},{9,1},{17,9},{25,17},{2,26},{10... | collective-permute-start | bytes 196616 | tf_op jit(solution)/shard_map/ppermute | solution.py:21
  87.5 15.1 %collective-permute-start.11 = (bf16[704,512]{1,0:T(8,128)(2,1)S(1)}, bf16[704,512]{1,0:T(8,128)(2,1)}, u32[]{:S(2)}, u32[]{:S(2)}) collective-permute-start(bf16[704,512]{1,0:T(8,128)(2,1)S(1)} %join.1.keep_ref), channel_id=1, source_target_pairs={{0,1},{1,0},{2,3},{3,2},{4,5},{5,4},{6,7},{7,6},{8,9},{9,8},{10,11... | collective-permute-start | bytes 2162696 | tf_op jit(solution)/shard_map/ppermute | solution.py:21
  88.4 10.0 %collective-permute-start.22 = (bf16[1,64,2048]{2,1,0:T(8,128)(2,1)}, bf16[1,64,2048]{2,1,0:T(8,128)(2,1)S(1)}, u32[]{:S(2)}, u32[]{:S(2)}) collective-permute-start(bf16[1,64,2048]{2,1,0:T(8,128)(2,1)} %slice.26), channel_id=1, source_target_pairs={{0,32},{32,64},{64,96},{96,128},{128,160},{160,192},{192,224},{224... | collective-permute-start | bytes 786440 | tf_op jit(solution)/shard_map/ppermute | solution.py:21
  92.7 9.9 %collective-permute-start.23 = (bf16[1,64,2048]{2,1,0:T(8,128)(2,1)}, bf16[1,64,2048]{2,1,0:T(8,128)(2,1)}, u32[]{:S(2)}, u32[]{:S(2)}) collective-permute-start(bf16[1,64,2048]{2,1,0:T(8,128)(2,1)} %slice.27), channel_id=1, source_target_pairs={{0,224},{32,0},{64,32},{96,64},{128,96},{160,128},{192,160},{224,1... | collective-permute-start | bytes 786440 | tf_op jit(solution)/shard_map/ppermute | solution.py:21
  (4 other events, 11.7 us)

commit v4 on v3

--- a/solution.py
+++ b/solution.py
@@ -61,12 +61,8 @@
     for step in (1, 2, 3):
         ahead, behind = shift(ahead, "z", 1), shift(behind, "z", -1)
         pieces += [(step, ahead), (8 - step, behind)]
-    ahead, behind = shift(ahead[:1], "z", 1), shift(behind[1:], "z", -1)
+    ahead, behind = shift(close(ahead[:1]), "z", 1), shift(close(behind[1:]), "z", -1)
     return pieces + [(4, ahead), (4, behind)]
-
-
-def far(x):
-    return pltpu.with_memory_space_constraint(x, pltpu.HBM)
 
 
 def close(x):
@@ -134,26 +130,10 @@
     high_ref[...], low_ref[...] = split(x_ref[...])
 
 
-def tail_kernel(backs, at_ref, keep_ref, given_ref, high_ref, low_ref, stay_ref, *refs):
-    pieces, (old_ref, out_ref, rows_ref, old_buf, new_buf, sems, old_sem, new_sems) = (
-        refs[: len(backs)], refs[len(backs):]
-    )
+def tail_kernel(backs, at_ref, keep_ref, given_ref, high_ref, low_ref, stay_ref, old_ref, *refs):
+    pieces, (out_ref, rows_ref, new_buf, new_sems) = refs[: len(backs)], refs[len(backs):]
     zero, z = at_ref[0] == 0, at_ref[1]
     depth, columns = pieces[0].shape[1:]
-    copies = []
-    for i, (back, piece) in enumerate(zip(backs, pieces)):
-        row = pl.multiple_of(lax.rem(z + 8 - back, 8) * depth, depth)
-        first = 1 if i == len(backs) - 1 else 0
-        for p in range(piece.shape[0]):
-            copies.append(
-                pltpu.make_async_copy(
-                    piece.at[p], rows_ref.at[first + p, pl.ds(row, depth), :], sems.at[i, p]
-                )
-            )
-    old_copy = pltpu.make_async_copy(old_ref, old_buf, old_sem)
-    for copy in copies:
-        copy.start()
-    old_copy.start()
 
     keep, given = keep_ref[...], given_ref[...]
     low, top = jnp.where(zero, keep, given), jnp.where(zero, given, keep)
@@ -166,9 +146,11 @@
     first = dot(high, high_ref[0]) + (dot(high, low_ref[0]) + dot(rest, high_ref[0]))
     first = first.astype(BF16)
 
-    for copy in copies:
-        copy.wait()
-    old_copy.wait()
+    for i, (back, piece) in enumerate(zip(backs, pieces)):
+        row = pl.multiple_of(lax.rem(z + 8 - back, 8) * depth, depth)
+        start = 1 if i == len(backs) - 1 else 0
+        for p in range(piece.shape[0]):
+            rows_ref[start + p, pl.ds(row, depth), :] = piece[p]
     stay = stay_ref[...] > 0.0
     chunks = new_sems.shape[0]
     width = columns // chunks
@@ -176,7 +158,7 @@
     for c in range(chunks):
         at = pl.ds(c * width, width)
         change = dot(first, rows_ref[0, :, at]) + dot(second, rows_ref[1, :, at])
-        new = jnp.where(stay, old_buf[:, at].astype(F32) - change, 0.0)
+        new = jnp.where(stay, old_ref[:, at].astype(F32) - change, 0.0)
         new_buf[:, at] = new.astype(BF16)
         outs.append(pltpu.make_async_copy(new_buf.at[:, at], out_ref.at[:, at], new_sems.at[c]))
         outs[-1].start()
@@ -197,10 +179,12 @@
 
     slot = jnp.arange(tokens, dtype=jnp.int32)
     valid = (slot < counts[0]).astype(F32)
-    gate = gate_up[:, 0, :].astype(F32)
-    up = gate_up[:, 1, :].astype(F32)
-    hidden = (jax.nn.silu(gate) * up * valid[:, None]).astype(BF16)
-    acts = lax.dot_general(select, hidden, NT, preferred_element_type=F32).astype(BF16)
+
+    def activate(gate, up):
+        return (jax.nn.silu(gate.astype(F32)) * up.astype(F32) * valid).astype(BF16)
+
+    hidden = activate(gate_up[:, 0, :].T, gate_up[:, 1, :].T)
+    acts = activate(dot_nt(select, gate_up[:, 0, :]), dot_nt(select, gate_up[:, 1, :]))
     acts, select = lax.optimization_barrier((acts, select))
     rows = jnp.dot(select, down_weight, preferred_element_type=F32).astype(BF16)
 
@@ -231,7 +215,7 @@
         out_specs=(VMEM, VMEM),
         compiler_params=pltpu.CompilerParams(vmem_limit_bytes=12 * 1024 * 1024),
         name="partial",
-    )(core[None], counts, hidden.T, acts)
+    )(core[None], counts, hidden, acts)
     given = shift(give, "co", 1)
     y = lax.axis_index("y").astype(jnp.int32)[None]
     small = pltpu.CompilerParams(vmem_limit_bytes=8 * 1024 * 1024)
@@ -274,19 +258,16 @@
     return pl.pallas_call(
         functools.partial(tail_kernel, backs),
         out_shape=jax.ShapeDtypeStruct((local, columns), BF16),
-        in_specs=[SMEM, VMEM, VMEM, VMEM, VMEM, VMEM] + [HBM] * (len(backs) + 1),
+        in_specs=[SMEM] + [VMEM] * (6 + len(backs)),
         out_specs=HBM,
         scratch_shapes=[
             pltpu.VMEM((2, panel, columns), BF16),
             pltpu.VMEM((local, columns), BF16),
-            pltpu.VMEM((local, columns), BF16),
-            pltpu.SemaphoreType.DMA((len(backs), 2)),
-            pltpu.SemaphoreType.DMA(()),
             pltpu.SemaphoreType.DMA((4,)),
         ],
-        compiler_params=pltpu.CompilerParams(vmem_limit_bytes=20 * 1024 * 1024),
+        compiler_params=pltpu.CompilerParams(vmem_limit_bytes=16 * 1024 * 1024),
         name="tail",
-    )(at, keep, given, *parts, stay, *[far(piece) for _, piece in pieces], far(down_weight))
+    )(at, keep, given, *parts, stay, down_weight, *[close(piece) for _, piece in pieces])
 
 
 def solution(mesh):

time: 111 us -> 115 us (1.036)
  the two profiles are of different devices: /device:TPU:124 before, /device:TPU:126 now
where the time goes in v4:
time: 115 us
  waiting for transfers between devices  51.1 us (44%)
  starting transfers between devices  36.1 us (31%)
  local copies, waits for them, and re-layouts  12.6 us (11%)
  Pallas kernels  8.27 us (7%)
  matrix products  3.87 us (3%)
  other arithmetic  1.74 us (2%)
  between operations  1.24 us (1%)
    ppermute x24, waiting for transfers between devices, shift(): return lax.ppermute(x, axis, [(i, (i + by) % n) for i in range(n)])  51.1 us
    ppermute x24, starting transfers between devices, shift(): return lax.ppermute(x, axis, [(i, (i + by) % n) for i in range(n)])  28.5 us
    all_to_all x1, starting transfers between devices, to_all(): lax.all_to_all(jnp.broadcast_to(x, (n, *x.shape)), axes, split_axis=0, co...  7.66 us
    pallas_call x1, Pallas kernels, compute(): pl.pallas_call(functools.partial(tail_kernel, backs), out_shape=jax.Shape...  5.72 us
    unnamed x30, local copies, waits for them, and re-layouts  5.3 us
    dynamic_update_slice x10, local copies, waits for them, and re-layouts, place(): out = lax.dynamic_update_slice(out, jnp.expand_dims(piece, dim), at)  3.58 us
    dot_general x2, matrix products, dot_nt(): return lax.dot_general(a, b, NT, preferred_element_type=F32)  2.9 us
  transfers between devices with their start and end apart: 25, of which 12 were waited for; matrix products, arithmetic and copies ran while one was open for 7% of the time, Pallas kernels for 2%

profile of v4, /device:TPU:126, one launch (start us, length us, event | category | flops | bytes accessed | tf_op | source)
XLA Modules:
  0.0 114.9 jit_solution(11249625944767135533)
XLA Ops:
  1.1 1.4 %fusion.8 = f32[16,1024]{1,0:T(8,128)S(1)} fusion(bf16[1024,2,448]{0,2,1:T(8,128)(2,1)} %param.5, s32[16]{0:T(128)S(1)} %sub.31), kind=kOutput, calls=%fused_computation.13 | convolution fusion | flops 14687232 | bytes 983104 | tf_op jit(solution)/shard_map/dot_general | solution.py:77
  3.2 1.5 %fusion.6 = bf16[16,1024]{1,0:T(8,128)(2,1)S(1)} fusion(bf16[1024,2,448]{0,2,1:T(8,128)(2,1)} %param.5, f32[16,1024]{1,0:T(8,128)S(1)} %fusion.8, f32[1024]{0:T(1024)S(1)} %fusion.17, s32[16]{0:T(128)S(1)} %sub.31), kind=kOutput, calls=%fused_computation.11 | convolution fusion | flops 14801920 | bytes 1019968 | tf_op jit(solution)/shard_map/dot_general | solution.py:77
  5.4 7.7 %all-to-all-start = ((bf16[8,16,1024]{2,1,0:T(8,128)(2,1)}), bf16[8,16,1024]{2,1,0:T(8,128)(2,1)S(1)}, u32[]{:S(2)}, u32[]{:S(2)}) async-start(bf16[8,16,1024]{2,1,0:T(8,128)(2,1)} %broadcast_in_dim.65), calls=%async_computation | async-start | bytes 524288 | tf_op jit(solution)/shard_map/all_to_all | solution.py:26
  13.7 1.0 bitcast_dynamic-update-slice_fusion.9
  14.7 1.4 %collective-permute-start.12 = (bf16[2,8,2048]{2,1,0:T(8,128)(2,1)S(1)}, bf16[2,8,2048]{2,1,0:T(8,128)(2,1)S(1)}, u32[]{:S(2)}, u32[]{:S(2)}) collective-permute-start(bf16[2,8,2048]{2,1,0:T(8,128)(2,1)S(1)} %bitcast.84), channel_id=1, source_target_pairs={{0,4},{4,0},{1,5},{5,1},{2,6},{6,2},{3,7},{7,3},{8,12},{12,8},{9,1... | collective-permute-start | bytes 196616 | tf_op jit(solution)/shard_map/ppermute | solution.py:21
  16.8 3.6 %collective-permute-done.12 = bf16[2,8,2048]{2,1,0:T(8,128)(2,1)S(1)} collective-permute-done((bf16[2,8,2048]{2,1,0:T(8,128)(2,1)S(1)}, bf16[2,8,2048]{2,1,0:T(8,128)(2,1)S(1)}, u32[]{:S(2)}, u32[]{:S(2)}) %collective-permute-start.12) | collective-permute-done | bytes 65568 | tf_op jit(solution)/shard_map/ppermute | solution.py:21
  21.3 1.8 %collective-permute-start.14 = (bf16[2,2,8,2048]{3,2,1,0:T(8,128)(2,1)}, bf16[2,2,8,2048]{3,2,1,0:T(8,128)(2,1)}, u32[]{:S(2)}, u32[]{:S(2)}) collective-permute-start(bf16[2,2,8,2048]{3,2,1,0:T(8,128)(2,1)} %bitcast_dynamic-update-slice_fusion.10), channel_id=1, source_target_pairs={{0,24},{8,0},{16,8},{24,16},{1,25},{9,1},{17,9},{25,17},{2,26},{10... | collective-permute-start | bytes 393224 | tf_op jit(solution)/shard_map/ppermute | solution.py:21
  23.1 1.2 %collective-permute-start.15 = (bf16[2,2,8,2048]{3,2,1,0:T(8,128)(2,1)}, bf16[2,2,8,2048]{3,2,1,0:T(8,128)(2,1)}, u32[]{:S(2)}, u32[]{:S(2)}) collective-permute-start(bf16[2,2,8,2048]{3,2,1,0:T(8,128)(2,1)} %bitcast_dynamic-update-slice_fusion.10), channel_id=1, source_target_pairs={{0,16},{8,24},{16,0},{24,8},{1,17},{9,25},{17,1},{25,9},{2,18},{10... | collective-permute-start | bytes 393224 | tf_op jit(solution)/shard_map/ppermute | solution.py:21
  25.3 1.6 %collective-permute-done.13 = bf16[2,2,8,2048]{3,2,1,0:T(8,128)(2,1)S(1)} collective-permute-done((bf16[2,2,8,2048]{3,2,1,0:T(8,128)(2,1)}, bf16[2,2,8,2048]{3,2,1,0:T(8,128)(2,1)S(1)}, u32[]{:S(2)}, u32[]{:S(2)}) %collective-permute-start.13) | collective-permute-done | bytes 131104 | tf_op jit(solution)/shard_map/ppermute | solution.py:21
  26.9 1.5 %collective-permute-start = (bf16[128,1024]{1,0:T(8,128)(2,1)S(1)}, bf16[128,1024]{1,0:T(8,128)(2,1)S(1)}, u32[]{:S(2)}, u32[]{:S(2)}) collective-permute-start(bf16[128,1024]{1,0:T(8,128)(2,1)S(1)} %bitcast.82), channel_id=1, source_target_pairs={{0,4},{4,0},{1,5},{5,1},{2,6},{6,2},{3,7},{7,3},{8,12},{12,8},{9,1... | collective-permute-start | bytes 786440 | tf_op jit(solution)/shard_map/ppermute | solution.py:21
  29.4 5.5 %collective-permute-done = bf16[128,1024]{1,0:T(8,128)(2,1)S(1)} collective-permute-done((bf16[128,1024]{1,0:T(8,128)(2,1)S(1)}, bf16[128,1024]{1,0:T(8,128)(2,1)S(1)}, u32[]{:S(2)}, u32[]{:S(2)}) %collective-permute-start) | collective-permute-done | bytes 262176 | tf_op jit(solution)/shard_map/ppermute | solution.py:21
  34.9 2.3 %collective-permute-start.1 = (bf16[2,128,1024]{2,1,0:T(8,128)(2,1)S(1)}, bf16[2,128,1024]{2,1,0:T(8,128)(2,1)S(1)}, u32[]{:S(2)}, u32[]{:S(2)}) collective-permute-start(bf16[2,128,1024]{2,1,0:T(8,128)(2,1)S(1)} %bitcast_dynamic-update-slice_fusion.3), channel_id=1, source_target_pairs={{0,8},{8,16},{16,24},{24,0},{1,9},{9,17},{17,25},{25,1},{2,10},{10... | collective-permute-start | bytes 1572872 | tf_op jit(solution)/shard_map/ppermute | solution.py:21
  38.1 2.8 %collective-permute-start.16 = (bf16[2,64,2048]{2,1,0:T(8,128)(2,1)S(1)}, bf16[2,64,2048]{2,1,0:T(8,128)(2,1)S(1)}, u32[]{:S(2)}, u32[]{:S(2)}) collective-permute-start(bf16[2,64,2048]{2,1,0:T(8,128)(2,1)S(1)} %bitcast.78), channel_id=1, source_target_pairs={{0,32},{32,64},{64,96},{96,128},{128,160},{160,192},{192,224},{224... | collective-permute-start | bytes 1572872 | tf_op jit(solution)/shard_map/ppermute | solution.py:21
  41.2 5.8 %collective-permute-done.1 = bf16[2,128,1024]{2,1,0:T(8,128)(2,1)S(1)} collective-permute-done((bf16[2,128,1024]{2,1,0:T(8,128)(2,1)S(1)}, bf16[2,128,1024]{2,1,0:T(8,128)(2,1)S(1)}, u32[]{:S(2)}, u32[]{:S(2)}) %collective-permute-start.1) | collective-permute-done | bytes 524320 | tf_op jit(solution)/shard_map/ppermute | solution.py:21
  47.0 3.0 %collective-permute-start.3 = (bf16[1,128,1024]{2,1,0:T(8,128)(2,1)S(1)}, bf16[1,128,1024]{2,1,0:T(8,128)(2,1)S(1)}, u32[]{:S(2)}, u32[]{:S(2)}) collective-permute-start(bf16[1,128,1024]{2,1,0:T(8,128)(2,1)S(1)} %slice.26), channel_id=1, source_target_pairs={{0,8},{8,16},{16,24},{24,0},{1,9},{9,17},{17,25},{25,1},{2,10},{10... | collective-permute-start | bytes 786440 | tf_op jit(solution)/shard_map/ppermute | solution.py:21
  50.3 3.6 %collective-permute-done.3 = bf16[1,128,1024]{2,1,0:T(8,128)(2,1)S(1)} collective-permute-done((bf16[1,128,1024]{2,1,0:T(8,128)(2,1)S(1)}, bf16[1,128,1024]{2,1,0:T(8,128)(2,1)S(1)}, u32[]{:S(2)}, u32[]{:S(2)}) %collective-permute-start.3) | collective-permute-done | bytes 262176 | tf_op jit(solution)/shard_map/ppermute | solution.py:21
  53.9 3.9 %collective-permute-done.4 = bf16[1,128,1024]{2,1,0:T(8,128)(2,1)S(1)} collective-permute-done((bf16[1,128,1024]{2,1,0:T(8,128)(2,1)S(1)}, bf16[1,128,1024]{2,1,0:T(8,128)(2,1)S(1)}, u32[]{:S(2)}, u32[]{:S(2)}) %collective-permute-start.4) | collective-permute-done | bytes 262176 | tf_op jit(solution)/shard_map/ppermute | solution.py:21
  58.1 2.0 %partial.1 = (f32[712,512]{1,0:T(8,128)S(1)}, bf16[712,512]{1,0:T(8,128)(2,1)S(1)}) custom-call(s32[1]{0:T(128)} %bitcast.core_ref, s32[1]{0:T(128)} %copy.34.count_ref, bf16[448,1024]{1,0:T(8,128)(2,1)S(1)} %fusion.1.hidden_ref, bf16[2,512,1024]{2,1,0:T(8,128)(2,1)S(1)} %bitcast.77), custom_call_target="tpu_custom_call" | custom-call | tf_op jit(solution)/shard_map/partial/pallas_call | solution.py:208
  60.4 2.9 %collective-permute-start.18 = (bf16[2,64,2048]{2,1,0:T(8,128)(2,1)S(1)}, bf16[2,64,2048]{2,1,0:T(8,128)(2,1)S(1)}, u32[]{:S(2)}, u32[]{:S(2)}) collective-permute-start(bf16[2,64,2048]{2,1,0:T(8,128)(2,1)S(1)} %collective-permute-done.16.refs_1_), channel_id=1, source_target_pairs={{0,32},{32,64},{64,96},{96,128},{128,160},{160,192},{192,224},{224... | collective-permute-start | bytes 1572872 | tf_op jit(solution)/shard_map/ppermute | solution.py:21
  64.2 1.4 %collective-permute-start.7 = (bf16[72,512]{1,0:T(8,128)(2,1)S(1)}, bf16[72,512]{1,0:T(8,128)(2,1)S(1)}, u32[]{:S(2)}, u32[]{:S(2)}) collective-permute-start(bf16[72,512]{1,0:T(8,128)(2,1)S(1)} %get-tuple-element.24), channel_id=1, source_target_pairs={{0,2},{2,0},{1,3},{3,1},{4,6},{6,4},{5,7},{7,5},{8,10},{10,8},{9,1... | collective-permute-start | bytes 221192 | tf_op jit(solution)/shard_map/ppermute | solution.py:21
  65.6 9.5 %collective-permute-done.18.refs_3_ = bf16[2,64,2048]{2,1,0:T(8,128)(2,1)S(1)} collective-permute-done((bf16[2,64,2048]{2,1,0:T(8,128)(2,1)S(1)}, bf16[2,64,2048]{2,1,0:T(8,128)(2,1)S(1)}, u32[]{:S(2)}, u32[]{:S(2)}) %collective-permute-start.18) | collective-permute-done | bytes 524320 | tf_op jit(solution)/shard_map/ppermute | solution.py:21
  75.0 3.7 %collective-permute-start.20 = (bf16[2,64,2048]{2,1,0:T(8,128)(2,1)S(1)}, bf16[2,64,2048]{2,1,0:T(8,128)(2,1)S(1)}, u32[]{:S(2)}, u32[]{:S(2)}) collective-permute-start(bf16[2,64,2048]{2,1,0:T(8,128)(2,1)S(1)} %collective-permute-done.18.refs_3_), channel_id=1, source_target_pairs={{0,32},{32,64},{64,96},{96,128},{128,160},{160,192},{192,224},{224... | collective-permute-start | bytes 1572872 | tf_op jit(solution)/shard_map/ppermute | solution.py:21
  78.9 1.5 %collective-permute-start.8 = (bf16[64,512]{1,0:T(8,128)(2,1)S(1)}, bf16[64,512]{1,0:T(8,128)(2,1)S(1)}, u32[]{:S(2)}, u32[]{:S(2)}) collective-permute-start(bf16[64,512]{1,0:T(8,128)(2,1)S(1)} %get-tuple-element.26.refs_0_), channel_id=1, source_target_pairs={{0,8},{8,16},{16,24},{24,0},{1,9},{9,17},{17,25},{25,1},{2,10},{10... | collective-permute-start | bytes 196616 | tf_op jit(solution)/shard_map/ppermute | solution.py:21
  80.3 4.3 %collective-permute-done.10.refs_3_ = bf16[64,512]{1,0:T(8,128)(2,1)S(1)} collective-permute-done((bf16[64,512]{1,0:T(8,128)(2,1)S(1)}, bf16[64,512]{1,0:T(8,128)(2,1)S(1)}, u32[]{:S(2)}, u32[]{:S(2)}) %collective-permute-start.10) | collective-permute-done | bytes 65568 | tf_op jit(solution)/shard_map/ppermute | solution.py:21
  84.7 5.5 %collective-permute-done.9.refs_2_ = bf16[64,512]{1,0:T(8,128)(2,1)S(1)} collective-permute-done((bf16[64,512]{1,0:T(8,128)(2,1)S(1)}, bf16[64,512]{1,0:T(8,128)(2,1)S(1)}, u32[]{:S(2)}, u32[]{:S(2)}) %collective-permute-start.9) | collective-permute-done | bytes 65568 | tf_op jit(solution)/shard_map/ppermute | solution.py:21
  91.9 3.5 %collective-permute-start.22 = (bf16[1,64,2048]{2,1,0:T(8,128)(2,1)}, bf16[1,64,2048]{2,1,0:T(8,128)(2,1)}, u32[]{:S(2)}, u32[]{:S(2)}) collective-permute-start(bf16[1,64,2048]{2,1,0:T(8,128)(2,1)} %slice.28), channel_id=1, source_target_pairs={{0,32},{32,64},{64,96},{96,128},{128,160},{160,192},{192,224},{224... | collective-permute-start | bytes 786440 | tf_op jit(solution)/shard_map/ppermute | solution.py:21
  97.2 1.6 %copy-done.1 = f32[2,512,512]{2,1,0:T(8,128)S(1)} copy-done((f32[2,512,512]{2,1,0:T(8,128)S(1)}, f32[2,512,512]{2,1,0:T(8,128)}, u32[]{:S(2)}) %copy-start.1) | copy-done | bytes 2097176
  99.1 2.8 %collective-permute-done.22.refs_7_ = bf16[1,64,2048]{2,1,0:T(8,128)(2,1)} collective-permute-done((bf16[1,64,2048]{2,1,0:T(8,128)(2,1)}, bf16[1,64,2048]{2,1,0:T(8,128)(2,1)}, u32[]{:S(2)}, u32[]{:S(2)}) %collective-permute-start.22) | collective-permute-done | bytes 262176 | tf_op jit(solution)/shard_map/ppermute | solution.py:21
  102.0 5.0 %collective-permute-done.23.refs_8_ = bf16[1,64,2048]{2,1,0:T(8,128)(2,1)} collective-permute-done((bf16[1,64,2048]{2,1,0:T(8,128)(2,1)}, bf16[1,64,2048]{2,1,0:T(8,128)(2,1)}, u32[]{:S(2)}, u32[]{:S(2)}) %collective-permute-start.23) | collective-permute-done | bytes 262176 | tf_op jit(solution)/shard_map/ppermute | solution.py:21
  107.0 1.0 copy-done.11
  108.0 1.0 copy-done.13
  109.0 5.7 %tail.1 = bf16[448,2048]{1,0:T(8,128)(2,1)} custom-call(s32[2]{0:T(128)S(1)} %pad_add_fusion.at_ref, bf16[704,512]{1,0:T(8,128)(2,1)S(1)} %join.1.keep_ref, bf16[704,512]{1,0:T(8,128)(2,1)} %collective-permute-done.11.given_ref, bf16[2,512,512]{2,1,0:T(8,128)(2,1)S(1)} %get-tuple-element.29.high_ref, bf16[2,512,512]{2,1,0:T(8,128)(2,1)S(1)} %get-tuple-element.30.low_ref, ...), custom_call_target="tpu_custom_call" | custom-call | tf_op jit(solution)/shard_map/tail/pallas_call | solution.py:258
  (86 shorter events, 12.9 us)
Async XLA Ops:
  0.0 13.7 %copy-start = (bf16[448,2048]{1,0:T(8,128)(2,1)S(1)}, bf16[448,2048]{1,0:T(8,128)(2,1)}, u32[]{:S(2)}) copy-start(bf16[448,2048]{1,0:T(8,128)(2,1)} %old_ref.1) | copy-start | bytes 5505028
  5.4 21.5 %all-to-all-start = ((bf16[8,16,1024]{2,1,0:T(8,128)(2,1)}), bf16[8,16,1024]{2,1,0:T(8,128)(2,1)S(1)}, u32[]{:S(2)}, u32[]{:S(2)}) async-start(bf16[8,16,1024]{2,1,0:T(8,128)(2,1)} %broadcast_in_dim.65), calls=%async_computation | async-start | bytes 524288 | tf_op jit(solution)/shard_map/all_to_all | solution.py:26
  14.7 5.8 %collective-permute-start.12 = (bf16[2,8,2048]{2,1,0:T(8,128)(2,1)S(1)}, bf16[2,8,2048]{2,1,0:T(8,128)(2,1)S(1)}, u32[]{:S(2)}, u32[]{:S(2)}) collective-permute-start(bf16[2,8,2048]{2,1,0:T(8,128)(2,1)S(1)} %bitcast.84), channel_id=1, source_target_pairs={{0,4},{4,0},{1,5},{5,1},{2,6},{6,2},{3,7},{7,3},{8,12},{12,8},{9,1... | collective-permute-start | bytes 196616 | tf_op jit(solution)/shard_map/ppermute | solution.py:21
  21.1 5.8 %collective-permute-start.13 = (bf16[2,2,8,2048]{3,2,1,0:T(8,128)(2,1)}, bf16[2,2,8,2048]{3,2,1,0:T(8,128)(2,1)S(1)}, u32[]{:S(2)}, u32[]{:S(2)}) collective-permute-start(bf16[2,2,8,2048]{3,2,1,0:T(8,128)(2,1)} %bitcast_dynamic-update-slice_fusion.10), channel_id=1, source_target_pairs={{0,8},{8,16},{16,24},{24,0},{1,9},{9,17},{17,25},{25,1},{2,10},{10... | collective-permute-start | bytes 393224 | tf_op jit(solution)/shard_map/ppermute | solution.py:21
  21.3 7.1 %collective-permute-start.14 = (bf16[2,2,8,2048]{3,2,1,0:T(8,128)(2,1)}, bf16[2,2,8,2048]{3,2,1,0:T(8,128)(2,1)}, u32[]{:S(2)}, u32[]{:S(2)}) collective-permute-start(bf16[2,2,8,2048]{3,2,1,0:T(8,128)(2,1)} %bitcast_dynamic-update-slice_fusion.10), channel_id=1, source_target_pairs={{0,24},{8,0},{16,8},{24,16},{1,25},{9,1},{17,9},{25,17},{2,26},{10... | collective-permute-start | bytes 393224 | tf_op jit(solution)/shard_map/ppermute | solution.py:21
  23.1 14.1 %collective-permute-start.15 = (bf16[2,2,8,2048]{3,2,1,0:T(8,128)(2,1)}, bf16[2,2,8,2048]{3,2,1,0:T(8,128)(2,1)}, u32[]{:S(2)}, u32[]{:S(2)}) collective-permute-start(bf16[2,2,8,2048]{3,2,1,0:T(8,128)(2,1)} %bitcast_dynamic-update-slice_fusion.10), channel_id=1, source_target_pairs={{0,16},{8,24},{16,0},{24,8},{1,17},{9,25},{17,1},{25,9},{2,18},{10... | collective-permute-start | bytes 393224 | tf_op jit(solution)/shard_map/ppermute | solution.py:21
  26.9 8.0 %collective-permute-start = (bf16[128,1024]{1,0:T(8,128)(2,1)S(1)}, bf16[128,1024]{1,0:T(8,128)(2,1)S(1)}, u32[]{:S(2)}, u32[]{:S(2)}) collective-permute-start(bf16[128,1024]{1,0:T(8,128)(2,1)S(1)} %bitcast.82), channel_id=1, source_target_pairs={{0,4},{4,0},{1,5},{5,1},{2,6},{6,2},{3,7},{7,3},{8,12},{12,8},{9,1... | collective-permute-start | bytes 786440 | tf_op jit(solution)/shard_map/ppermute | solution.py:21
  34.9 12.1 %collective-permute-start.1 = (bf16[2,128,1024]{2,1,0:T(8,128)(2,1)S(1)}, bf16[2,128,1024]{2,1,0:T(8,128)(2,1)S(1)}, u32[]{:S(2)}, u32[]{:S(2)}) collective-permute-start(bf16[2,128,1024]{2,1,0:T(8,128)(2,1)S(1)} %bitcast_dynamic-update-slice_fusion.3), channel_id=1, source_target_pairs={{0,8},{8,16},{16,24},{24,0},{1,9},{9,17},{17,25},{25,1},{2,10},{10... | collective-permute-start | bytes 1572872 | tf_op jit(solution)/shard_map/ppermute | solution.py:21
  37.2 12.9 %collective-permute-start.2 = (bf16[2,128,1024]{2,1,0:T(8,128)(2,1)S(1)}, bf16[2,128,1024]{2,1,0:T(8,128)(2,1)S(1)}, u32[]{:S(2)}, u32[]{:S(2)}) collective-permute-start(bf16[2,128,1024]{2,1,0:T(8,128)(2,1)S(1)} %bitcast_dynamic-update-slice_fusion.3), channel_id=1, source_target_pairs={{0,24},{8,0},{16,8},{24,16},{1,25},{9,1},{17,9},{25,17},{2,26},{10... | collective-permute-start | bytes 1572872 | tf_op jit(solution)/shard_map/ppermute | solution.py:21
  38.1 22.2 %collective-permute-start.16 = (bf16[2,64,2048]{2,1,0:T(8,128)(2,1)S(1)}, bf16[2,64,2048]{2,1,0:T(8,128)(2,1)S(1)}, u32[]{:S(2)}, u32[]{:S(2)}) collective-permute-start(bf16[2,64,2048]{2,1,0:T(8,128)(2,1)S(1)} %bitcast.78), channel_id=1, source_target_pairs={{0,32},{32,64},{64,96},{96,128},{128,160},{160,192},{192,224},{224... | collective-permute-start | bytes 1572872 | tf_op jit(solution)/shard_map/ppermute | solution.py:21
  40.9 22.4 %collective-permute-start.17 = (bf16[2,64,2048]{2,1,0:T(8,128)(2,1)S(1)}, bf16[2,64,2048]{2,1,0:T(8,128)(2,1)S(1)}, u32[]{:S(2)}, u32[]{:S(2)}) collective-permute-start(bf16[2,64,2048]{2,1,0:T(8,128)(2,1)S(1)} %bitcast.79), channel_id=1, source_target_pairs={{0,224},{32,0},{64,32},{96,64},{128,96},{160,128},{192,160},{224,1... | collective-permute-start | bytes 1572872 | tf_op jit(solution)/shard_map/ppermute | solution.py:21
  47.0 6.9 %collective-permute-start.3 = (bf16[1,128,1024]{2,1,0:T(8,128)(2,1)S(1)}, bf16[1,128,1024]{2,1,0:T(8,128)(2,1)S(1)}, u32[]{:S(2)}, u32[]{:S(2)}) collective-permute-start(bf16[1,128,1024]{2,1,0:T(8,128)(2,1)S(1)} %slice.26), channel_id=1, source_target_pairs={{0,8},{8,16},{16,24},{24,0},{1,9},{9,17},{17,25},{25,1},{2,10},{10... | collective-permute-start | bytes 786440 | tf_op jit(solution)/shard_map/ppermute | solution.py:21
  50.2 7.7 %collective-permute-start.4 = (bf16[1,128,1024]{2,1,0:T(8,128)(2,1)S(1)}, bf16[1,128,1024]{2,1,0:T(8,128)(2,1)S(1)}, u32[]{:S(2)}, u32[]{:S(2)}) collective-permute-start(bf16[1,128,1024]{2,1,0:T(8,128)(2,1)S(1)} %slice.27), channel_id=1, source_target_pairs={{0,24},{8,0},{16,8},{24,16},{1,25},{9,1},{17,9},{25,17},{2,26},{10... | collective-permute-start | bytes 786440 | tf_op jit(solution)/shard_map/ppermute | solution.py:21
  60.1 3.2 %collective-permute-start.5 = (bf16[712,512]{1,0:T(8,128)(2,1)S(1)}, bf16[712,512]{1,0:T(8,128)(2,1)S(1)}, u32[]{:S(2)}, u32[]{:S(2)}) collective-permute-start(bf16[712,512]{1,0:T(8,128)(2,1)S(1)} %get-tuple-element.20), channel_id=1, source_target_pairs={{0,1},{1,0},{2,3},{3,2},{4,5},{5,4},{6,7},{7,6},{8,9},{9,8},{10,11... | collective-permute-start | bytes 2187272 | tf_op jit(solution)/shard_map/ppermute | solution.py:21
  60.4 29.9 %copy-start.6 = (bf16[2,64,2048]{2,1,0:T(8,128)(2,1)}, bf16[2,64,2048]{2,1,0:T(8,128)(2,1)S(1)}, u32[]{:S(2)}) copy-start(bf16[2,64,2048]{2,1,0:T(8,128)(2,1)S(1)} %collective-permute-done.16.refs_1_) | copy-start | bytes 1572868
  60.4 14.7 %collective-permute-start.18 = (bf16[2,64,2048]{2,1,0:T(8,128)(2,1)S(1)}, bf16[2,64,2048]{2,1,0:T(8,128)(2,1)S(1)}, u32[]{:S(2)}, u32[]{:S(2)}) collective-permute-start(bf16[2,64,2048]{2,1,0:T(8,128)(2,1)S(1)} %collective-permute-done.16.refs_1_), channel_id=1, source_target_pairs={{0,32},{32,64},{64,96},{96,128},{128,160},{160,192},{192,224},{224... | collective-permute-start | bytes 1572872 | tf_op jit(solution)/shard_map/ppermute | solution.py:21
  63.3 27.0 %copy-start.8 = (bf16[2,64,2048]{2,1,0:T(8,128)(2,1)}, bf16[2,64,2048]{2,1,0:T(8,128)(2,1)S(1)}, u32[]{:S(2)}) copy-start(bf16[2,64,2048]{2,1,0:T(8,128)(2,1)S(1)} %collective-permute-done.17.refs_2_) | copy-start | bytes 1572868
  63.3 15.4 %collective-permute-start.19 = (bf16[2,64,2048]{2,1,0:T(8,128)(2,1)S(1)}, bf16[2,64,2048]{2,1,0:T(8,128)(2,1)S(1)}, u32[]{:S(2)}, u32[]{:S(2)}) collective-permute-start(bf16[2,64,2048]{2,1,0:T(8,128)(2,1)S(1)} %collective-permute-done.17.refs_2_), channel_id=1, source_target_pairs={{0,224},{32,0},{64,32},{96,64},{128,96},{160,128},{192,160},{224,1... | collective-permute-start | bytes 1572872 | tf_op jit(solution)/shard_map/ppermute | solution.py:21
  63.5 26.7 %collective-permute-start.6 = (bf16[448,512]{1,0:T(8,128)(2,1)S(1)}, bf16[448,512]{1,0:T(8,128)(2,1)S(1)}, u32[]{:S(2)}, u32[]{:S(2)}) collective-permute-start(bf16[448,512]{1,0:T(8,128)(2,1)S(1)} %get-tuple-element.22), channel_id=1, source_target_pairs={{0,2},{2,0},{1,3},{3,1},{4,6},{6,4},{5,7},{7,5},{8,10},{10,8},{9,1... | collective-permute-start | bytes 1376264 | tf_op jit(solution)/shard_map/ppermute | solution.py:21
  64.2 14.5 %collective-permute-start.7 = (bf16[72,512]{1,0:T(8,128)(2,1)S(1)}, bf16[72,512]{1,0:T(8,128)(2,1)S(1)}, u32[]{:S(2)}, u32[]{:S(2)}) collective-permute-start(bf16[72,512]{1,0:T(8,128)(2,1)S(1)} %get-tuple-element.24), channel_id=1, source_target_pairs={{0,2},{2,0},{1,3},{3,1},{4,6},{6,4},{5,7},{7,5},{8,10},{10,8},{9,1... | collective-permute-start | bytes 221192 | tf_op jit(solution)/shard_map/ppermute | solution.py:21
  75.0 15.4 %copy-start.10 = (bf16[2,64,2048]{2,1,0:T(8,128)(2,1)}, bf16[2,64,2048]{2,1,0:T(8,128)(2,1)S(1)}, u32[]{:S(2)}) copy-start(bf16[2,64,2048]{2,1,0:T(8,128)(2,1)S(1)} %collective-permute-done.18.refs_3_) | copy-start | bytes 1572868
  75.0 15.4 %collective-permute-start.20 = (bf16[2,64,2048]{2,1,0:T(8,128)(2,1)S(1)}, bf16[2,64,2048]{2,1,0:T(8,128)(2,1)S(1)}, u32[]{:S(2)}, u32[]{:S(2)}) collective-permute-start(bf16[2,64,2048]{2,1,0:T(8,128)(2,1)S(1)} %collective-permute-done.18.refs_3_), channel_id=1, source_target_pairs={{0,32},{32,64},{64,96},{96,128},{128,160},{160,192},{192,224},{224... | collective-permute-start | bytes 1572872 | tf_op jit(solution)/shard_map/ppermute | solution.py:21
  78.7 18.3 %copy-start.12 = (bf16[2,64,2048]{2,1,0:T(8,128)(2,1)}, bf16[2,64,2048]{2,1,0:T(8,128)(2,1)S(1)}, u32[]{:S(2)}) copy-start(bf16[2,64,2048]{2,1,0:T(8,128)(2,1)S(1)} %collective-permute-done.19.refs_4_) | copy-start | bytes 1572868
  78.7 16.7 %collective-permute-start.21 = (bf16[2,64,2048]{2,1,0:T(8,128)(2,1)S(1)}, bf16[2,64,2048]{2,1,0:T(8,128)(2,1)S(1)}, u32[]{:S(2)}, u32[]{:S(2)}) collective-permute-start(bf16[2,64,2048]{2,1,0:T(8,128)(2,1)S(1)} %collective-permute-done.19.refs_4_), channel_id=1, source_target_pairs={{0,224},{32,0},{64,32},{96,64},{128,96},{160,128},{192,160},{224,1... | collective-permute-start | bytes 1572872 | tf_op jit(solution)/shard_map/ppermute | solution.py:21
  78.8 5.9 %collective-permute-start.10 = (bf16[64,512]{1,0:T(8,128)(2,1)S(1)}, bf16[64,512]{1,0:T(8,128)(2,1)S(1)}, u32[]{:S(2)}, u32[]{:S(2)}) collective-permute-start(bf16[64,512]{1,0:T(8,128)(2,1)S(1)} %get-tuple-element.26.refs_0_), channel_id=1, source_target_pairs={{0,16},{8,24},{16,0},{24,8},{1,17},{9,25},{17,1},{25,9},{2,18},{10... | collective-permute-start | bytes 196616 | tf_op jit(solution)/shard_map/ppermute | solution.py:21
  78.9 5.8 %collective-permute-start.8 = (bf16[64,512]{1,0:T(8,128)(2,1)S(1)}, bf16[64,512]{1,0:T(8,128)(2,1)S(1)}, u32[]{:S(2)}, u32[]{:S(2)}) collective-permute-start(bf16[64,512]{1,0:T(8,128)(2,1)S(1)} %get-tuple-element.26.refs_0_), channel_id=1, source_target_pairs={{0,8},{8,16},{16,24},{24,0},{1,9},{9,17},{17,25},{25,1},{2,10},{10... | collective-permute-start | bytes 196616 | tf_op jit(solution)/shard_map/ppermute | solution.py:21
  84.7 5.5 %collective-permute-start.9 = (bf16[64,512]{1,0:T(8,128)(2,1)S(1)}, bf16[64,512]{1,0:T(8,128)(2,1)S(1)}, u32[]{:S(2)}, u32[]{:S(2)}) collective-permute-start(bf16[64,512]{1,0:T(8,128)(2,1)S(1)} %get-tuple-element.26.refs_0_), channel_id=1, source_target_pairs={{0,24},{8,0},{16,8},{24,16},{1,25},{9,1},{17,9},{25,17},{2,26},{10... | collective-permute-start | bytes 196616 | tf_op jit(solution)/shard_map/ppermute | solution.py:21
  90.3 16.6 %collective-permute-start.11 = (bf16[704,512]{1,0:T(8,128)(2,1)S(1)}, bf16[704,512]{1,0:T(8,128)(2,1)}, u32[]{:S(2)}, u32[]{:S(2)}) collective-permute-start(bf16[704,512]{1,0:T(8,128)(2,1)S(1)} %join.1.keep_ref), channel_id=1, source_target_pairs={{0,1},{1,0},{2,3},{3,2},{4,5},{5,4},{6,7},{7,6},{8,9},{9,8},{10,11... | collective-permute-start | bytes 2162696 | tf_op jit(solution)/shard_map/ppermute | solution.py:21
  91.9 10.0 %collective-permute-start.22 = (bf16[1,64,2048]{2,1,0:T(8,128)(2,1)}, bf16[1,64,2048]{2,1,0:T(8,128)(2,1)}, u32[]{:S(2)}, u32[]{:S(2)}) collective-permute-start(bf16[1,64,2048]{2,1,0:T(8,128)(2,1)} %slice.28), channel_id=1, source_target_pairs={{0,32},{32,64},{64,96},{96,128},{128,160},{160,192},{192,224},{224... | collective-permute-start | bytes 786440 | tf_op jit(solution)/shard_map/ppermute | solution.py:21
  97.0 9.9 %collective-permute-start.23 = (bf16[1,64,2048]{2,1,0:T(8,128)(2,1)}, bf16[1,64,2048]{2,1,0:T(8,128)(2,1)}, u32[]{:S(2)}, u32[]{:S(2)}) collective-permute-start(bf16[1,64,2048]{2,1,0:T(8,128)(2,1)} %slice.29), channel_id=1, source_target_pairs={{0,224},{32,0},{64,32},{96,64},{128,96},{160,128},{192,160},{224,1... | collective-permute-start | bytes 786440 | tf_op jit(solution)/shard_map/ppermute | solution.py:21
  98.8 8.1 %copy-start.7 = (bf16[2,64,2048]{2,1,0:T(8,128)(2,1)S(1)}, bf16[2,64,2048]{2,1,0:T(8,128)(2,1)}, u32[]{:S(2)}) copy-start(bf16[2,64,2048]{2,1,0:T(8,128)(2,1)} %copy-done.6) | copy-start | bytes 1572868
  98.8 8.1 %copy-start.9 = (bf16[2,64,2048]{2,1,0:T(8,128)(2,1)S(1)}, bf16[2,64,2048]{2,1,0:T(8,128)(2,1)}, u32[]{:S(2)}) copy-start(bf16[2,64,2048]{2,1,0:T(8,128)(2,1)} %copy-done.8) | copy-start | bytes 1572868
  (8 other events, 24.6 us)

commit v5 on v3

--- a/solution.py
+++ b/solution.py
@@ -14,6 +14,7 @@
 VMEM = pl.BlockSpec(memory_space=pltpu.VMEM)
 SMEM = pl.BlockSpec(memory_space=pltpu.SMEM)
 HBM = pl.BlockSpec(memory_space=pltpu.HBM)
+ANY = pl.BlockSpec(memory_space=pl.ANY)
 
 
 def shift(x, axis, by):
@@ -55,13 +56,38 @@
     return place([(0, block), (1, ahead), (3, behind), (2, far_block)], "y", 0)
 
 
+def halve_kernel(ahead_ref, behind_ref, first_ref, second_ref, sems):
+    copies = [
+        pltpu.make_async_copy(ahead_ref.at[pl.ds(0, 1)], first_ref, sems.at[0]),
+        pltpu.make_async_copy(behind_ref.at[pl.ds(1, 1)], second_ref, sems.at[1]),
+    ]
+    for copy in copies:
+        copy.start()
+    for copy in copies:
+        copy.wait()
+
+
+def halve(ahead, behind):
+    half = jax.ShapeDtypeStruct((1, *ahead.shape[1:]), ahead.dtype)
+    return pl.pallas_call(
+        halve_kernel,
+        out_shape=(half, half),
+        in_specs=[ANY, ANY],
+        out_specs=(ANY, ANY),
+        scratch_shapes=[pltpu.SemaphoreType.DMA((2,))],
+        compiler_params=pltpu.CompilerParams(vmem_limit_bytes=2 * 1024 * 1024),
+        name="halve",
+    )(ahead, behind)
+
+
 def ring_z(block):
     pieces = [(0, block)]
     ahead, behind = block, block
     for step in (1, 2, 3):
         ahead, behind = shift(ahead, "z", 1), shift(behind, "z", -1)
         pieces += [(step, ahead), (8 - step, behind)]
-    ahead, behind = shift(ahead[:1], "z", 1), shift(behind[1:], "z", -1)
+    ahead, behind = halve(ahead, behind)
+    ahead, behind = shift(ahead, "z", 1), shift(behind, "z", -1)
     return pieces + [(4, ahead), (4, behind)]
 
 
@@ -140,20 +166,20 @@
     )
     zero, z = at_ref[0] == 0, at_ref[1]
     depth, columns = pieces[0].shape[1:]
-    copies = []
-    for i, (back, piece) in enumerate(zip(backs, pieces)):
-        row = pl.multiple_of(lax.rem(z + 8 - back, 8) * depth, depth)
-        first = 1 if i == len(backs) - 1 else 0
-        for p in range(piece.shape[0]):
-            copies.append(
-                pltpu.make_async_copy(
-                    piece.at[p], rows_ref.at[first + p, pl.ds(row, depth), :], sems.at[i, p]
-                )
-            )
-    old_copy = pltpu.make_async_copy(old_ref, old_buf, old_sem)
-    for copy in copies:
-        copy.start()
-    old_copy.start()
+    chunks = new_sems.shape[0]
+    width = columns // chunks
+    copies = [[] for _ in range(chunks)]
+    for c in range(chunks):
+        at = pl.ds(c * width, width)
+        for i, (back, piece) in enumerate(zip(backs, pieces)):
+            row = pl.multiple_of(lax.rem(z + 8 - back, 8) * depth, depth)
+            start = 1 if i == len(backs) - 1 else 0
+            for p in range(piece.shape[0]):
+                to = rows_ref.at[start + p, pl.ds(row, depth), at]
+                copies[c].append(pltpu.make_async_copy(piece.at[p, :, at], to, sems.at[c, i, p]))
+        copies[c].append(pltpu.make_async_copy(old_ref.at[:, at], old_buf.at[:, at], old_sem.at[c]))
+        for copy in copies[c]:
+            copy.start()
 
     keep, given = keep_ref[...], given_ref[...]
     low, top = jnp.where(zero, keep, given), jnp.where(zero, given, keep)
@@ -166,14 +192,11 @@
     first = dot(high, high_ref[0]) + (dot(high, low_ref[0]) + dot(rest, high_ref[0]))
     first = first.astype(BF16)
 
-    for copy in copies:
-        copy.wait()
-    old_copy.wait()
     stay = stay_ref[...] > 0.0
-    chunks = new_sems.shape[0]
-    width = columns // chunks
     outs = []
     for c in range(chunks):
+        for copy in copies[c]:
+            copy.wait()
         at = pl.ds(c * width, width)
         change = dot(first, rows_ref[0, :, at]) + dot(second, rows_ref[1, :, at])
         new = jnp.where(stay, old_buf[:, at].astype(F32) - change, 0.0)
@@ -280,9 +303,9 @@
             pltpu.VMEM((2, panel, columns), BF16),
             pltpu.VMEM((local, columns), BF16),
             pltpu.VMEM((local, columns), BF16),
-            pltpu.SemaphoreType.DMA((len(backs), 2)),
-            pltpu.SemaphoreType.DMA(()),
-            pltpu.SemaphoreType.DMA((4,)),
+            pltpu.SemaphoreType.DMA((2, len(backs), 2)),
+            pltpu.SemaphoreType.DMA((2,)),
+            pltpu.SemaphoreType.DMA((2,)),
         ],
         compiler_params=pltpu.CompilerParams(vmem_limit_bytes=20 * 1024 * 1024),
         name="tail",

time: 111 us -> 108 us (0.973)
  the two profiles are of different devices: /device:TPU:124 before, /device:TPU:8 now
where the time goes in v5:
time: 108 us; the launch traced here: 107 us
  waiting for transfers between devices  45.5 us (42%)
  starting transfers between devices  39.7 us (37%)
  Pallas kernels  10.7 us (10%)
  local copies, waits for them, and re-layouts  4.13 us (4%)
  other arithmetic  3.05 us (3%)
  matrix products  2.65 us (2%)
  between operations  1.23 us (1%)
    ppermute x24, waiting for transfers between devices, shift(): return lax.ppermute(x, axis, [(i, (i + by) % n) for i in range(n)])  41.2 us
    ppermute x24, starting transfers between devices, shift(): return lax.ppermute(x, axis, [(i, (i + by) % n) for i in range(n)])  31.3 us
    all_to_all x1, starting transfers between devices, to_all(): lax.all_to_all(jnp.broadcast_to(x, (n, *x.shape)), axes, split_axis=0, co...  8.47 us
    pallas_call x1, Pallas kernels, compute(): pl.pallas_call(functools.partial(tail_kernel, backs), out_shape=jax.Shape...  8.03 us
    all_to_all x1, waiting for transfers between devices, to_all(): lax.all_to_all(jnp.broadcast_to(x, (n, *x.shape)), axes, split_axis=0, co...  4.31 us
    unnamed x20, local copies, waits for them, and re-layouts  2.32 us
    dot_general x1, matrix products, compute(): lax.dot_general(select, hidden, NT, preferred_element_type=F32).astype(BF16)  2.29 us
  transfers between devices with their start and end apart: 25, of which 11 were waited for; matrix products, arithmetic and copies ran while one was open for 4% of the time, Pallas kernels for 2%

profile of v5, /device:TPU:8, one launch (start us, length us, event | category | flops | bytes accessed | tf_op | source)
XLA Modules:
  0.0 107.0 jit_solution(639883751715052841)
XLA Ops:
  0.0 0.8 fusion.11
  1.6 2.3 %convolution_convert_fusion.1 = bf16[16,1024]{1,0:T(8,128)(2,1)S(1)} fusion(s32[16]{0:T(128)S(1)} %sub.31, f32[1024]{0:T(1024)S(1)} %fusion.10, bf16[1024,2,448]{0,2,1:T(8,128)(2,1)} %param.5), kind=kOutput, calls=%fused_computation.9 | convolution fusion | flops 18832384 | bytes 1871936 | tf_op jit(solution)/shard_map/dot_general | solution.py:226
  4.3 3.0 %collective-permute-start.12 = (bf16[2,8,2048]{2,1,0:T(8,128)(2,1)S(1)}, bf16[2,8,2048]{2,1,0:T(8,128)(2,1)S(1)}, u32[]{:S(2)}, u32[]{:S(2)}) collective-permute-start(bf16[2,8,2048]{2,1,0:T(8,128)(2,1)S(1)} %bitcast.76), channel_id=1, source_target_pairs={{0,4},{4,0},{1,5},{5,1},{2,6},{6,2},{3,7},{7,3},{8,12},{12,8},{9,1... | collective-permute-start | bytes 196616 | tf_op jit(solution)/shard_map/ppermute | solution.py:22
  7.3 0.7 broadcast_in_dim.64
  8.0 8.5 %all-to-all-start = ((bf16[8,16,1024]{2,1,0:T(8,128)(2,1)}), bf16[8,16,1024]{2,1,0:T(8,128)(2,1)S(1)}, u32[]{:S(2)}, u32[]{:S(2)}) async-start(bf16[8,16,1024]{2,1,0:T(8,128)(2,1)} %broadcast_in_dim.64), calls=%async_computation | async-start | bytes 524288 | tf_op jit(solution)/shard_map/all_to_all | solution.py:27
  16.5 2.1 %fusion.15.hidden_ref = bf16[448,1024]{1,0:T(8,128)(2,1)S(1)} fusion(f32[1024]{0:T(1024)S(1)} %fusion.10, bf16[1024,2,448]{0,2,1:T(8,128)(2,1)} %param.5), kind=kLoop, calls=%fused_computation.33 | loop fusion | flops 4128768 | bytes 2756608 | tf_op jit(solution)/shard_map/transpose | solution.py:257
  18.7 1.7 %collective-permute-start.13 = (bf16[2,2,8,2048]{3,2,1,0:T(8,128)(2,1)S(1)}, bf16[2,2,8,2048]{3,2,1,0:T(8,128)(2,1)S(1)}, u32[]{:S(2)}, u32[]{:S(2)}) collective-permute-start(bf16[2,2,8,2048]{3,2,1,0:T(8,128)(2,1)S(1)} %bitcast_dynamic-update-slice_fusion.10), channel_id=1, source_target_pairs={{0,8},{8,16},{16,24},{24,0},{1,9},{9,17},{17,25},{25,1},{2,10},{10... | collective-permute-start | bytes 393224 | tf_op jit(solution)/shard_map/ppermute | solution.py:22
  20.8 2.3 %collective-permute-start.15 = (bf16[2,2,8,2048]{3,2,1,0:T(8,128)(2,1)S(1)}, bf16[2,2,8,2048]{3,2,1,0:T(8,128)(2,1)S(1)}, u32[]{:S(2)}, u32[]{:S(2)}) collective-permute-start(bf16[2,2,8,2048]{3,2,1,0:T(8,128)(2,1)S(1)} %bitcast_dynamic-update-slice_fusion.10), channel_id=1, source_target_pairs={{0,16},{8,24},{16,0},{24,8},{1,17},{9,25},{17,1},{25,9},{2,18},{10... | collective-permute-start | bytes 393224 | tf_op jit(solution)/shard_map/ppermute | solution.py:22
  23.8 4.3 %all-to-all-done = bf16[8,16,1024]{2,1,0:T(8,128)(2,1)S(1)} async-done(((bf16[8,16,1024]{2,1,0:T(8,128)(2,1)}), bf16[8,16,1024]{2,1,0:T(8,128)(2,1)S(1)}, u32[]{:S(2)}, u32[]{:S(2)}) %all-to-all-start) | async-done | bytes 262176 | tf_op jit(solution)/shard_map/all_to_all | solution.py:27
  28.7 7.3 %collective-permute-done = bf16[128,1024]{1,0:T(8,128)(2,1)S(1)} collective-permute-done((bf16[128,1024]{1,0:T(8,128)(2,1)S(1)}, bf16[128,1024]{1,0:T(8,128)(2,1)S(1)}, u32[]{:S(2)}, u32[]{:S(2)}) %collective-permute-start) | collective-permute-done | bytes 262176 | tf_op jit(solution)/shard_map/ppermute | solution.py:22
  36.0 1.7 %collective-permute-start.1 = (bf16[2,128,1024]{2,1,0:T(8,128)(2,1)S(1)}, bf16[2,128,1024]{2,1,0:T(8,128)(2,1)S(1)}, u32[]{:S(2)}, u32[]{:S(2)}) collective-permute-start(bf16[2,128,1024]{2,1,0:T(8,128)(2,1)S(1)} %bitcast_dynamic-update-slice_fusion.3), channel_id=1, source_target_pairs={{0,8},{8,16},{16,24},{24,0},{1,9},{9,17},{17,25},{25,1},{2,10},{10... | collective-permute-start | bytes 1572872 | tf_op jit(solution)/shard_map/ppermute | solution.py:22
  38.8 2.7 %collective-permute-start.17 = (bf16[2,64,2048]{2,1,0:T(8,128)(2,1)S(1)}, bf16[2,64,2048]{2,1,0:T(8,128)(2,1)S(1)}, u32[]{:S(2)}, u32[]{:S(2)}) collective-permute-start(bf16[2,64,2048]{2,1,0:T(8,128)(2,1)S(1)} %bitcast.72), channel_id=1, source_target_pairs={{0,224},{32,0},{64,32},{96,64},{128,96},{160,128},{192,160},{224,1... | collective-permute-start | bytes 1572872 | tf_op jit(solution)/shard_map/ppermute | solution.py:22
  41.8 6.3 %collective-permute-done.1 = bf16[2,128,1024]{2,1,0:T(8,128)(2,1)S(1)} collective-permute-done((bf16[2,128,1024]{2,1,0:T(8,128)(2,1)S(1)}, bf16[2,128,1024]{2,1,0:T(8,128)(2,1)S(1)}, u32[]{:S(2)}, u32[]{:S(2)}) %collective-permute-start.1) | collective-permute-done | bytes 524320 | tf_op jit(solution)/shard_map/ppermute | solution.py:22
  48.0 1.7 %collective-permute-start.3 = (bf16[1,128,1024]{2,1,0:T(8,128)(2,1)S(1)}, bf16[1,128,1024]{2,1,0:T(8,128)(2,1)S(1)}, u32[]{:S(2)}, u32[]{:S(2)}) collective-permute-start(bf16[1,128,1024]{2,1,0:T(8,128)(2,1)S(1)} %slice.16), channel_id=1, source_target_pairs={{0,8},{8,16},{16,24},{24,0},{1,9},{9,17},{17,25},{25,1},{2,10},{10... | collective-permute-start | bytes 786440 | tf_op jit(solution)/shard_map/ppermute | solution.py:22
  50.4 4.1 %collective-permute-done.3 = bf16[1,128,1024]{2,1,0:T(8,128)(2,1)S(1)} collective-permute-done((bf16[1,128,1024]{2,1,0:T(8,128)(2,1)S(1)}, bf16[1,128,1024]{2,1,0:T(8,128)(2,1)S(1)}, u32[]{:S(2)}, u32[]{:S(2)}) %collective-permute-start.3) | collective-permute-done | bytes 262176 | tf_op jit(solution)/shard_map/ppermute | solution.py:22
  54.5 1.7 %collective-permute-done.4 = bf16[1,128,1024]{2,1,0:T(8,128)(2,1)S(1)} collective-permute-done((bf16[1,128,1024]{2,1,0:T(8,128)(2,1)S(1)}, bf16[1,128,1024]{2,1,0:T(8,128)(2,1)S(1)}, u32[]{:S(2)}, u32[]{:S(2)}) %collective-permute-start.4) | collective-permute-done | bytes 262176 | tf_op jit(solution)/shard_map/ppermute | solution.py:22
  56.5 2.0 %partial.1 = (f32[712,512]{1,0:T(8,128)S(1)}, bf16[712,512]{1,0:T(8,128)(2,1)S(1)}) custom-call(s32[1]{0:T(128)} %bitcast.core_ref, s32[1]{0:T(128)} %copy.34.count_ref, bf16[448,1024]{1,0:T(8,128)(2,1)S(1)} %fusion.15.hidden_ref, bf16[2,512,1024]{2,1,0:T(8,128)(2,1)S(1)} %bitcast.69), custom_call_target="tpu_custom_call" | custom-call | tf_op jit(solution)/shard_map/partial/pallas_call | solution.py:247
  59.4 2.7 %collective-permute-start.19 = (bf16[2,64,2048]{2,1,0:T(8,128)(2,1)S(1)}, bf16[2,64,2048]{2,1,0:T(8,128)(2,1)S(1)}, u32[]{:S(2)}, u32[]{:S(2)}) collective-permute-start(bf16[2,64,2048]{2,1,0:T(8,128)(2,1)S(1)} %collective-permute-done.17.refs_2_), channel_id=1, source_target_pairs={{0,224},{32,0},{64,32},{96,64},{128,96},{160,128},{192,160},{224,1... | collective-permute-start | bytes 1572872 | tf_op jit(solution)/shard_map/ppermute | solution.py:22
  62.3 0.7 collective-permute-start.6
  63.0 1.4 %collective-permute-start.7 = (bf16[72,512]{1,0:T(8,128)(2,1)S(1)}, bf16[72,512]{1,0:T(8,128)(2,1)S(1)}, u32[]{:S(2)}, u32[]{:S(2)}) collective-permute-start(bf16[72,512]{1,0:T(8,128)(2,1)S(1)} %get-tuple-element.26), channel_id=1, source_target_pairs={{0,2},{2,0},{1,3},{3,1},{4,6},{6,4},{5,7},{7,5},{8,10},{10,8},{9,1... | collective-permute-start | bytes 221192 | tf_op jit(solution)/shard_map/ppermute | solution.py:22
  64.4 9.9 %collective-permute-done.18.refs_3_ = bf16[2,64,2048]{2,1,0:T(8,128)(2,1)S(1)} collective-permute-done((bf16[2,64,2048]{2,1,0:T(8,128)(2,1)S(1)}, bf16[2,64,2048]{2,1,0:T(8,128)(2,1)S(1)}, u32[]{:S(2)}, u32[]{:S(2)}) %collective-permute-start.18) | collective-permute-done | bytes 524320 | tf_op jit(solution)/shard_map/ppermute | solution.py:22
  74.3 3.2 %collective-permute-start.21 = (bf16[2,64,2048]{2,1,0:T(8,128)(2,1)S(1)}, bf16[2,64,2048]{2,1,0:T(8,128)(2,1)S(1)}, u32[]{:S(2)}, u32[]{:S(2)}) collective-permute-start(bf16[2,64,2048]{2,1,0:T(8,128)(2,1)S(1)} %collective-permute-done.19.refs_4_), channel_id=1, source_target_pairs={{0,224},{32,0},{64,32},{96,64},{128,96},{160,128},{192,160},{224,1... | collective-permute-start | bytes 1572872 | tf_op jit(solution)/shard_map/ppermute | solution.py:22
  77.6 2.2 %collective-permute-start.10 = (bf16[64,512]{1,0:T(8,128)(2,1)S(1)}, bf16[64,512]{1,0:T(8,128)(2,1)S(1)}, u32[]{:S(2)}, u32[]{:S(2)}) collective-permute-start(bf16[64,512]{1,0:T(8,128)(2,1)S(1)} %get-tuple-element.28.refs_0_), channel_id=1, source_target_pairs={{0,16},{8,24},{16,0},{24,8},{1,17},{9,25},{17,1},{25,9},{2,18},{10... | collective-permute-start | bytes 196616 | tf_op jit(solution)/shard_map/ppermute | solution.py:22
  79.8 3.6 %collective-permute-done.10.refs_3_ = bf16[64,512]{1,0:T(8,128)(2,1)S(1)} collective-permute-done((bf16[64,512]{1,0:T(8,128)(2,1)S(1)}, bf16[64,512]{1,0:T(8,128)(2,1)S(1)}, u32[]{:S(2)}, u32[]{:S(2)}) %collective-permute-start.10) | collective-permute-done | bytes 65568 | tf_op jit(solution)/shard_map/ppermute | solution.py:22
  83.4 1.2 %collective-permute-start.9 = (bf16[64,512]{1,0:T(8,128)(2,1)S(1)}, bf16[64,512]{1,0:T(8,128)(2,1)S(1)}, u32[]{:S(2)}, u32[]{:S(2)}) collective-permute-start(bf16[64,512]{1,0:T(8,128)(2,1)S(1)} %get-tuple-element.28.refs_0_), channel_id=1, source_target_pairs={{0,24},{8,0},{16,8},{24,16},{1,25},{9,1},{17,9},{25,17},{2,26},{10... | collective-permute-start | bytes 196616 | tf_op jit(solution)/shard_map/ppermute | solution.py:22
  84.6 3.1 %collective-permute-done.9.refs_2_ = bf16[64,512]{1,0:T(8,128)(2,1)S(1)} collective-permute-done((bf16[64,512]{1,0:T(8,128)(2,1)S(1)}, bf16[64,512]{1,0:T(8,128)(2,1)S(1)}, u32[]{:S(2)}, u32[]{:S(2)}) %collective-permute-start.9) | collective-permute-done | bytes 65568 | tf_op jit(solution)/shard_map/ppermute | solution.py:22
  88.0 0.9 collective-permute-done.20.ahead_ref.refs_5_
  89.1 3.2 %collective-permute-start.23 = (bf16[1,64,2048]{2,1,0:T(8,128)(2,1)S(1)}, bf16[1,64,2048]{2,1,0:T(8,128)(2,1)}, u32[]{:S(2)}, u32[]{:S(2)}) collective-permute-start(bf16[1,64,2048]{2,1,0:T(8,128)(2,1)S(1)} %get-tuple-element.34), channel_id=1, source_target_pairs={{0,224},{32,0},{64,32},{96,64},{128,96},{160,128},{192,160},{224,1... | collective-permute-start | bytes 786440 | tf_op jit(solution)/shard_map/ppermute | solution.py:22
  92.5 1.6 %copy-done.2 = f32[2,512,512]{2,1,0:T(8,128)S(1)} copy-done((f32[2,512,512]{2,1,0:T(8,128)S(1)}, f32[2,512,512]{2,1,0:T(8,128)}, u32[]{:S(2)}) %copy-start.2) | copy-done | bytes 2097176
  94.4 3.6 %collective-permute-done.22.refs_7_ = bf16[1,64,2048]{2,1,0:T(8,128)(2,1)S(1)} collective-permute-done((bf16[1,64,2048]{2,1,0:T(8,128)(2,1)S(1)}, bf16[1,64,2048]{2,1,0:T(8,128)(2,1)S(1)}, u32[]{:S(2)}, u32[]{:S(2)}) %collective-permute-start.22) | collective-permute-done | bytes 262176 | tf_op jit(solution)/shard_map/ppermute | solution.py:22
  98.1 0.7 copy-done.9
  98.8 8.0 %tail.1 = bf16[448,2048]{1,0:T(8,128)(2,1)} custom-call(s32[2]{0:T(128)S(1)} %pad_add_fusion.at_ref, bf16[704,512]{1,0:T(8,128)(2,1)S(1)} %join.1.keep_ref, bf16[704,512]{1,0:T(8,128)(2,1)S(1)} %collective-permute-done.11.given_ref, bf16[2,512,512]{2,1,0:T(8,128)(2,1)S(1)} %get-tuple-element.31.high_ref, bf16[2,512,512]{2,1,0:T(8,128)(2,1)S(1)} %get-tuple-element.32.low_ref, ...), custom_call_target="tpu_custom_call" | custom-call | tf_op jit(solution)/shard_map/tail/pallas_call | solution.py:297
  (74 shorter events, 6.6 us)
Async XLA Ops:
  4.3 14.4 %collective-permute-start.12 = (bf16[2,8,2048]{2,1,0:T(8,128)(2,1)S(1)}, bf16[2,8,2048]{2,1,0:T(8,128)(2,1)S(1)}, u32[]{:S(2)}, u32[]{:S(2)}) collective-permute-start(bf16[2,8,2048]{2,1,0:T(8,128)(2,1)S(1)} %bitcast.76), channel_id=1, source_target_pairs={{0,4},{4,0},{1,5},{5,1},{2,6},{6,2},{3,7},{7,3},{8,12},{12,8},{9,1... | collective-permute-start | bytes 196616 | tf_op jit(solution)/shard_map/ppermute | solution.py:22
  8.0 20.1 %all-to-all-start = ((bf16[8,16,1024]{2,1,0:T(8,128)(2,1)}), bf16[8,16,1024]{2,1,0:T(8,128)(2,1)S(1)}, u32[]{:S(2)}, u32[]{:S(2)}) async-start(bf16[8,16,1024]{2,1,0:T(8,128)(2,1)} %broadcast_in_dim.64), calls=%async_computation | async-start | bytes 524288 | tf_op jit(solution)/shard_map/all_to_all | solution.py:27
  18.7 5.1 %collective-permute-start.13 = (bf16[2,2,8,2048]{3,2,1,0:T(8,128)(2,1)S(1)}, bf16[2,2,8,2048]{3,2,1,0:T(8,128)(2,1)S(1)}, u32[]{:S(2)}, u32[]{:S(2)}) collective-permute-start(bf16[2,2,8,2048]{3,2,1,0:T(8,128)(2,1)S(1)} %bitcast_dynamic-update-slice_fusion.10), channel_id=1, source_target_pairs={{0,8},{8,16},{16,24},{24,0},{1,9},{9,17},{17,25},{25,1},{2,10},{10... | collective-permute-start | bytes 393224 | tf_op jit(solution)/shard_map/ppermute | solution.py:22
  20.4 8.2 %collective-permute-start.14 = (bf16[2,2,8,2048]{3,2,1,0:T(8,128)(2,1)S(1)}, bf16[2,2,8,2048]{3,2,1,0:T(8,128)(2,1)S(1)}, u32[]{:S(2)}, u32[]{:S(2)}) collective-permute-start(bf16[2,2,8,2048]{3,2,1,0:T(8,128)(2,1)S(1)} %bitcast_dynamic-update-slice_fusion.10), channel_id=1, source_target_pairs={{0,24},{8,0},{16,8},{24,16},{1,25},{9,1},{17,9},{25,17},{2,26},{10... | collective-permute-start | bytes 393224 | tf_op jit(solution)/shard_map/ppermute | solution.py:22
  20.8 17.3 %collective-permute-start.15 = (bf16[2,2,8,2048]{3,2,1,0:T(8,128)(2,1)S(1)}, bf16[2,2,8,2048]{3,2,1,0:T(8,128)(2,1)S(1)}, u32[]{:S(2)}, u32[]{:S(2)}) collective-permute-start(bf16[2,2,8,2048]{3,2,1,0:T(8,128)(2,1)S(1)} %bitcast_dynamic-update-slice_fusion.10), channel_id=1, source_target_pairs={{0,16},{8,24},{16,0},{24,8},{1,17},{9,25},{17,1},{25,9},{2,18},{10... | collective-permute-start | bytes 393224 | tf_op jit(solution)/shard_map/ppermute | solution.py:22
  28.1 7.9 %collective-permute-start = (bf16[128,1024]{1,0:T(8,128)(2,1)S(1)}, bf16[128,1024]{1,0:T(8,128)(2,1)S(1)}, u32[]{:S(2)}, u32[]{:S(2)}) collective-permute-start(bf16[128,1024]{1,0:T(8,128)(2,1)S(1)} %bitcast.74), channel_id=1, source_target_pairs={{0,4},{4,0},{1,5},{5,1},{2,6},{6,2},{3,7},{7,3},{8,12},{12,8},{9,1... | collective-permute-start | bytes 786440 | tf_op jit(solution)/shard_map/ppermute | solution.py:22
  36.0 12.0 %collective-permute-start.1 = (bf16[2,128,1024]{2,1,0:T(8,128)(2,1)S(1)}, bf16[2,128,1024]{2,1,0:T(8,128)(2,1)S(1)}, u32[]{:S(2)}, u32[]{:S(2)}) collective-permute-start(bf16[2,128,1024]{2,1,0:T(8,128)(2,1)S(1)} %bitcast_dynamic-update-slice_fusion.3), channel_id=1, source_target_pairs={{0,8},{8,16},{16,24},{24,0},{1,9},{9,17},{17,25},{25,1},{2,10},{10... | collective-permute-start | bytes 1572872 | tf_op jit(solution)/shard_map/ppermute | solution.py:22
  37.7 12.1 %collective-permute-start.2 = (bf16[2,128,1024]{2,1,0:T(8,128)(2,1)S(1)}, bf16[2,128,1024]{2,1,0:T(8,128)(2,1)S(1)}, u32[]{:S(2)}, u32[]{:S(2)}) collective-permute-start(bf16[2,128,1024]{2,1,0:T(8,128)(2,1)S(1)} %bitcast_dynamic-update-slice_fusion.3), channel_id=1, source_target_pairs={{0,24},{8,0},{16,8},{24,16},{1,25},{9,1},{17,9},{25,17},{2,26},{10... | collective-permute-start | bytes 1572872 | tf_op jit(solution)/shard_map/ppermute | solution.py:22
  38.1 9.9 %copy-start.4 = (bf16[2,4,2,8,2048]{4,3,2,1,0:T(8,128)(2,1)}, bf16[2,4,2,8,2048]{4,3,2,1,0:T(8,128)(2,1)S(1)}, u32[]{:S(2)}) copy-start(bf16[2,4,2,8,2048]{4,3,2,1,0:T(8,128)(2,1)S(1)} %bitcast_dynamic-update-slice_fusion.8) | copy-start | bytes 1572868
  38.1 20.6 %collective-permute-start.16 = (bf16[2,64,2048]{2,1,0:T(8,128)(2,1)S(1)}, bf16[2,64,2048]{2,1,0:T(8,128)(2,1)S(1)}, u32[]{:S(2)}, u32[]{:S(2)}) collective-permute-start(bf16[2,64,2048]{2,1,0:T(8,128)(2,1)S(1)} %bitcast.71), channel_id=1, source_target_pairs={{0,32},{32,64},{64,96},{96,128},{128,160},{160,192},{192,224},{224... | collective-permute-start | bytes 1572872 | tf_op jit(solution)/shard_map/ppermute | solution.py:22
  38.8 20.7 %collective-permute-start.17 = (bf16[2,64,2048]{2,1,0:T(8,128)(2,1)S(1)}, bf16[2,64,2048]{2,1,0:T(8,128)(2,1)S(1)}, u32[]{:S(2)}, u32[]{:S(2)}) collective-permute-start(bf16[2,64,2048]{2,1,0:T(8,128)(2,1)S(1)} %bitcast.72), channel_id=1, source_target_pairs={{0,224},{32,0},{64,32},{96,64},{128,96},{160,128},{192,160},{224,1... | collective-permute-start | bytes 1572872 | tf_op jit(solution)/shard_map/ppermute | solution.py:22
  48.0 6.4 %collective-permute-start.3 = (bf16[1,128,1024]{2,1,0:T(8,128)(2,1)S(1)}, bf16[1,128,1024]{2,1,0:T(8,128)(2,1)S(1)}, u32[]{:S(2)}, u32[]{:S(2)}) collective-permute-start(bf16[1,128,1024]{2,1,0:T(8,128)(2,1)S(1)} %slice.16), channel_id=1, source_target_pairs={{0,8},{8,16},{16,24},{24,0},{1,9},{9,17},{17,25},{25,1},{2,10},{10... | collective-permute-start | bytes 786440 | tf_op jit(solution)/shard_map/ppermute | solution.py:22
  49.8 6.4 %collective-permute-start.4 = (bf16[1,128,1024]{2,1,0:T(8,128)(2,1)S(1)}, bf16[1,128,1024]{2,1,0:T(8,128)(2,1)S(1)}, u32[]{:S(2)}, u32[]{:S(2)}) collective-permute-start(bf16[1,128,1024]{2,1,0:T(8,128)(2,1)S(1)} %slice.17), channel_id=1, source_target_pairs={{0,24},{8,0},{16,8},{24,16},{1,25},{9,1},{17,9},{25,17},{2,26},{10... | collective-permute-start | bytes 786440 | tf_op jit(solution)/shard_map/ppermute | solution.py:22
  58.5 3.6 %collective-permute-start.5 = (bf16[712,512]{1,0:T(8,128)(2,1)S(1)}, bf16[712,512]{1,0:T(8,128)(2,1)S(1)}, u32[]{:S(2)}, u32[]{:S(2)}) collective-permute-start(bf16[712,512]{1,0:T(8,128)(2,1)S(1)} %get-tuple-element.22), channel_id=1, source_target_pairs={{0,1},{1,0},{2,3},{3,2},{4,5},{5,4},{6,7},{7,6},{8,9},{9,8},{10,11... | collective-permute-start | bytes 2187272 | tf_op jit(solution)/shard_map/ppermute | solution.py:22
  58.8 29.1 %copy-start.5 = (bf16[2,64,2048]{2,1,0:T(8,128)(2,1)}, bf16[2,64,2048]{2,1,0:T(8,128)(2,1)S(1)}, u32[]{:S(2)}) copy-start(bf16[2,64,2048]{2,1,0:T(8,128)(2,1)S(1)} %collective-permute-done.16.refs_1_) | copy-start | bytes 1572868
  58.8 15.5 %collective-permute-start.18 = (bf16[2,64,2048]{2,1,0:T(8,128)(2,1)S(1)}, bf16[2,64,2048]{2,1,0:T(8,128)(2,1)S(1)}, u32[]{:S(2)}, u32[]{:S(2)}) collective-permute-start(bf16[2,64,2048]{2,1,0:T(8,128)(2,1)S(1)} %collective-permute-done.16.refs_1_), channel_id=1, source_target_pairs={{0,32},{32,64},{64,96},{96,128},{128,160},{160,192},{192,224},{224... | collective-permute-start | bytes 1572872 | tf_op jit(solution)/shard_map/ppermute | solution.py:22
  59.4 28.4 %copy-start.6 = (bf16[2,64,2048]{2,1,0:T(8,128)(2,1)}, bf16[2,64,2048]{2,1,0:T(8,128)(2,1)S(1)}, u32[]{:S(2)}) copy-start(bf16[2,64,2048]{2,1,0:T(8,128)(2,1)S(1)} %collective-permute-done.17.refs_2_) | copy-start | bytes 1572868
  59.4 14.9 %collective-permute-start.19 = (bf16[2,64,2048]{2,1,0:T(8,128)(2,1)S(1)}, bf16[2,64,2048]{2,1,0:T(8,128)(2,1)S(1)}, u32[]{:S(2)}, u32[]{:S(2)}) collective-permute-start(bf16[2,64,2048]{2,1,0:T(8,128)(2,1)S(1)} %collective-permute-done.17.refs_2_), channel_id=1, source_target_pairs={{0,224},{32,0},{64,32},{96,64},{128,96},{160,128},{192,160},{224,1... | collective-permute-start | bytes 1572872 | tf_op jit(solution)/shard_map/ppermute | solution.py:22
  62.3 25.4 %collective-permute-start.6 = (bf16[448,512]{1,0:T(8,128)(2,1)S(1)}, bf16[448,512]{1,0:T(8,128)(2,1)S(1)}, u32[]{:S(2)}, u32[]{:S(2)}) collective-permute-start(bf16[448,512]{1,0:T(8,128)(2,1)S(1)} %get-tuple-element.24), channel_id=1, source_target_pairs={{0,2},{2,0},{1,3},{3,1},{4,6},{6,4},{5,7},{7,5},{8,10},{10,8},{9,1... | collective-permute-start | bytes 1376264 | tf_op jit(solution)/shard_map/ppermute | solution.py:22
  63.0 14.6 %collective-permute-start.7 = (bf16[72,512]{1,0:T(8,128)(2,1)S(1)}, bf16[72,512]{1,0:T(8,128)(2,1)S(1)}, u32[]{:S(2)}, u32[]{:S(2)}) collective-permute-start(bf16[72,512]{1,0:T(8,128)(2,1)S(1)} %get-tuple-element.26), channel_id=1, source_target_pairs={{0,2},{2,0},{1,3},{3,1},{4,6},{6,4},{5,7},{7,5},{8,10},{10,8},{9,1... | collective-permute-start | bytes 221192 | tf_op jit(solution)/shard_map/ppermute | solution.py:22
  74.3 18.0 %copy-start.7 = (bf16[2,64,2048]{2,1,0:T(8,128)(2,1)}, bf16[2,64,2048]{2,1,0:T(8,128)(2,1)S(1)}, u32[]{:S(2)}) copy-start(bf16[2,64,2048]{2,1,0:T(8,128)(2,1)S(1)} %collective-permute-done.18.refs_3_) | copy-start | bytes 1572868
  74.3 14.6 %collective-permute-start.20 = (bf16[2,64,2048]{2,1,0:T(8,128)(2,1)S(1)}, bf16[2,64,2048]{2,1,0:T(8,128)(2,1)S(1)}, u32[]{:S(2)}, u32[]{:S(2)}) collective-permute-start(bf16[2,64,2048]{2,1,0:T(8,128)(2,1)S(1)} %collective-permute-done.18.refs_3_), channel_id=1, source_target_pairs={{0,32},{32,64},{64,96},{96,128},{128,160},{160,192},{192,224},{224... | collective-permute-start | bytes 1572872 | tf_op jit(solution)/shard_map/ppermute | solution.py:22
  74.3 18.0 %copy-start.8 = (bf16[2,64,2048]{2,1,0:T(8,128)(2,1)}, bf16[2,64,2048]{2,1,0:T(8,128)(2,1)S(1)}, u32[]{:S(2)}) copy-start(bf16[2,64,2048]{2,1,0:T(8,128)(2,1)S(1)} %collective-permute-done.19.refs_4_) | copy-start | bytes 1572868
  74.3 14.6 %collective-permute-start.21 = (bf16[2,64,2048]{2,1,0:T(8,128)(2,1)S(1)}, bf16[2,64,2048]{2,1,0:T(8,128)(2,1)S(1)}, u32[]{:S(2)}, u32[]{:S(2)}) collective-permute-start(bf16[2,64,2048]{2,1,0:T(8,128)(2,1)S(1)} %collective-permute-done.19.refs_4_), channel_id=1, source_target_pairs={{0,224},{32,0},{64,32},{96,64},{128,96},{160,128},{192,160},{224,1... | collective-permute-start | bytes 1572872 | tf_op jit(solution)/shard_map/ppermute | solution.py:22
  77.6 5.9 %collective-permute-start.10 = (bf16[64,512]{1,0:T(8,128)(2,1)S(1)}, bf16[64,512]{1,0:T(8,128)(2,1)S(1)}, u32[]{:S(2)}, u32[]{:S(2)}) collective-permute-start(bf16[64,512]{1,0:T(8,128)(2,1)S(1)} %get-tuple-element.28.refs_0_), channel_id=1, source_target_pairs={{0,16},{8,24},{16,0},{24,8},{1,17},{9,25},{17,1},{25,9},{2,18},{10... | collective-permute-start | bytes 196616 | tf_op jit(solution)/shard_map/ppermute | solution.py:22
  79.8 4.8 %collective-permute-start.8 = (bf16[64,512]{1,0:T(8,128)(2,1)S(1)}, bf16[64,512]{1,0:T(8,128)(2,1)S(1)}, u32[]{:S(2)}, u32[]{:S(2)}) collective-permute-start(bf16[64,512]{1,0:T(8,128)(2,1)S(1)} %get-tuple-element.28.refs_0_), channel_id=1, source_target_pairs={{0,8},{8,16},{16,24},{24,0},{1,9},{9,17},{17,25},{25,1},{2,10},{10... | collective-permute-start | bytes 196616 | tf_op jit(solution)/shard_map/ppermute | solution.py:22
  83.4 4.3 %collective-permute-start.9 = (bf16[64,512]{1,0:T(8,128)(2,1)S(1)}, bf16[64,512]{1,0:T(8,128)(2,1)S(1)}, u32[]{:S(2)}, u32[]{:S(2)}) collective-permute-start(bf16[64,512]{1,0:T(8,128)(2,1)S(1)} %get-tuple-element.28.refs_0_), channel_id=1, source_target_pairs={{0,24},{8,0},{16,8},{24,16},{1,25},{9,1},{17,9},{25,17},{2,26},{10... | collective-permute-start | bytes 196616 | tf_op jit(solution)/shard_map/ppermute | solution.py:22
  87.9 10.2 %collective-permute-start.11 = (bf16[704,512]{1,0:T(8,128)(2,1)S(1)}, bf16[704,512]{1,0:T(8,128)(2,1)S(1)}, u32[]{:S(2)}, u32[]{:S(2)}) collective-permute-start(bf16[704,512]{1,0:T(8,128)(2,1)S(1)} %join.1.keep_ref), channel_id=1, source_target_pairs={{0,1},{1,0},{2,3},{3,2},{4,5},{5,4},{6,7},{7,6},{8,9},{9,8},{10,11... | collective-permute-start | bytes 2162696 | tf_op jit(solution)/shard_map/ppermute | solution.py:22
  88.9 9.2 %copy-start = (bf16[2,64,2048]{2,1,0:T(8,128)(2,1)}, bf16[2,64,2048]{2,1,0:T(8,128)(2,1)S(1)}, u32[]{:S(2)}) copy-start(bf16[2,64,2048]{2,1,0:T(8,128)(2,1)S(1)} %collective-permute-done.20.ahead_ref.refs_5_) | copy-start | bytes 1572868
  88.9 9.2 %copy-start.1 = (bf16[2,64,2048]{2,1,0:T(8,128)(2,1)}, bf16[2,64,2048]{2,1,0:T(8,128)(2,1)S(1)}, u32[]{:S(2)}) copy-start(bf16[2,64,2048]{2,1,0:T(8,128)(2,1)S(1)} %collective-permute-done.21.behind_ref.refs_6_) | copy-start | bytes 1572868
  89.0 9.1 %collective-permute-start.22 = (bf16[1,64,2048]{2,1,0:T(8,128)(2,1)S(1)}, bf16[1,64,2048]{2,1,0:T(8,128)(2,1)S(1)}, u32[]{:S(2)}, u32[]{:S(2)}) collective-permute-start(bf16[1,64,2048]{2,1,0:T(8,128)(2,1)S(1)} %get-tuple-element.33), channel_id=1, source_target_pairs={{0,32},{32,64},{64,96},{96,128},{128,160},{160,192},{192,224},{224... | collective-permute-start | bytes 786440 | tf_op jit(solution)/shard_map/ppermute | solution.py:22
  89.1 9.0 %collective-permute-start.23 = (bf16[1,64,2048]{2,1,0:T(8,128)(2,1)S(1)}, bf16[1,64,2048]{2,1,0:T(8,128)(2,1)}, u32[]{:S(2)}, u32[]{:S(2)}) collective-permute-start(bf16[1,64,2048]{2,1,0:T(8,128)(2,1)S(1)} %get-tuple-element.34), channel_id=1, source_target_pairs={{0,224},{32,0},{64,32},{96,64},{128,96},{160,128},{192,160},{224,1... | collective-permute-start | bytes 786440 | tf_op jit(solution)/shard_map/ppermute | solution.py:22
  (3 other events, 4.6 us)

commit v6 on v5

--- a/solution.py
+++ b/solution.py
@@ -89,10 +89,6 @@
     ahead, behind = halve(ahead, behind)
     ahead, behind = shift(ahead, "z", 1), shift(behind, "z", -1)
     return pieces + [(4, ahead), (4, behind)]
-
-
-def far(x):
-    return pltpu.with_memory_space_constraint(x, pltpu.HBM)
 
 
 def close(x):
@@ -160,26 +156,36 @@
     high_ref[...], low_ref[...] = split(x_ref[...])
 
 
-def tail_kernel(backs, at_ref, keep_ref, given_ref, high_ref, low_ref, stay_ref, *refs):
-    pieces, (old_ref, out_ref, rows_ref, old_buf, new_buf, sems, old_sem, new_sems) = (
-        refs[: len(backs)], refs[len(backs):]
-    )
+def stage_kernel(backs, z_ref, *refs):
+    pieces, (rows_ref, sems) = refs[: len(backs)], refs[len(backs):]
+    depth = pieces[0].shape[1]
+    copies = []
+    for i, (back, piece) in enumerate(zip(backs, pieces)):
+        row = pl.multiple_of(lax.rem(z_ref[0] + 8 - back, 8) * depth, depth)
+        for p in range(2):
+            to = rows_ref.at[p, pl.ds(row, depth), :]
+            copies.append(pltpu.make_async_copy(piece.at[p], to, sems.at[i, p]))
+    for copy in copies:
+        copy.start()
+    for copy in copies:
+        copy.wait()
+
+
+def tail_kernel(
+    at_ref, mine_ref, keep_ref, given_ref, high_ref, low_ref, old_ref, _, ahead_ref, behind_ref,
+    out_ref, rows_ref, new_buf, sems, new_sems,
+):
     zero, z = at_ref[0] == 0, at_ref[1]
-    depth, columns = pieces[0].shape[1:]
+    depth, columns = ahead_ref.shape[1:]
     chunks = new_sems.shape[0]
     width = columns // chunks
-    copies = [[] for _ in range(chunks)]
-    for c in range(chunks):
-        at = pl.ds(c * width, width)
-        for i, (back, piece) in enumerate(zip(backs, pieces)):
-            row = pl.multiple_of(lax.rem(z + 8 - back, 8) * depth, depth)
-            start = 1 if i == len(backs) - 1 else 0
-            for p in range(piece.shape[0]):
-                to = rows_ref.at[start + p, pl.ds(row, depth), at]
-                copies[c].append(pltpu.make_async_copy(piece.at[p, :, at], to, sems.at[c, i, p]))
-        copies[c].append(pltpu.make_async_copy(old_ref.at[:, at], old_buf.at[:, at], old_sem.at[c]))
-        for copy in copies[c]:
-            copy.start()
+    row = pl.ds(pl.multiple_of(lax.rem(z + 4, 8) * depth, depth), depth)
+    copies = [
+        pltpu.make_async_copy(ref.at[0], rows_ref.at[p, row, :], sems.at[p])
+        for p, ref in enumerate((ahead_ref, behind_ref))
+    ]
+    for copy in copies:
+        copy.start()
 
     keep, given = keep_ref[...], given_ref[...]
     low, top = jnp.where(zero, keep, given), jnp.where(zero, given, keep)
@@ -192,14 +198,17 @@
     first = dot(high, high_ref[0]) + (dot(high, low_ref[0]) + dot(rest, high_ref[0]))
     first = first.astype(BF16)
 
-    stay = stay_ref[...] > 0.0
+    index = lax.broadcasted_iota(jnp.int32, (old_ref.shape[0], width), 0)
+    gone = index == mine_ref[0]
+    for k in range(1, mine_ref.shape[0]):
+        gone = gone | (index == mine_ref[k])
+    for copy in copies:
+        copy.wait()
     outs = []
     for c in range(chunks):
-        for copy in copies[c]:
-            copy.wait()
         at = pl.ds(c * width, width)
         change = dot(first, rows_ref[0, :, at]) + dot(second, rows_ref[1, :, at])
-        new = jnp.where(stay, old_buf[:, at].astype(F32) - change, 0.0)
+        new = jnp.where(gone, 0.0, old_ref[:, at].astype(F32) - change)
         new_buf[:, at] = new.astype(BF16)
         outs.append(pltpu.make_async_copy(new_buf.at[:, at], out_ref.at[:, at], new_sems.at[c]))
         outs[-1].start()
@@ -291,25 +300,34 @@
     keep = close(keep)
     given = close(shift(keep, "co", 1))
 
-    stay = jnp.where(jnp.any(onehot, axis=0), 0.0, 1.0).astype(F32)[:, None]
     at = jnp.stack([core, lax.axis_index("z").astype(jnp.int32)])
-    backs = [back for back, _ in pieces]
-    return pl.pallas_call(
-        functools.partial(tail_kernel, backs),
-        out_shape=jax.ShapeDtypeStruct((local, columns), BF16),
-        in_specs=[SMEM, VMEM, VMEM, VMEM, VMEM, VMEM] + [HBM] * (len(backs) + 1),
-        out_specs=HBM,
+    staged = pl.pallas_call(
+        functools.partial(stage_kernel, [back for back, _ in pieces[:7]]),
+        out_shape=jax.ShapeDtypeStruct((2, panel, columns), BF16),
+        in_specs=[SMEM] + [ANY] * 7,
+        out_specs=VMEM,
+        scratch_shapes=[pltpu.SemaphoreType.DMA((7, 2))],
+        compiler_params=small,
+        name="stage",
+    )(at[1:], *[piece for _, piece in pieces[:7]])
+    out, _ = pl.pallas_call(
+        tail_kernel,
+        out_shape=(
+            jax.ShapeDtypeStruct((local, columns), BF16),
+            jax.ShapeDtypeStruct((2, panel, columns), BF16),
+        ),
+        in_specs=[SMEM, SMEM] + [VMEM] * 6 + [ANY] * 2,
+        out_specs=(HBM, VMEM),
+        input_output_aliases={7: 1},
         scratch_shapes=[
-            pltpu.VMEM((2, panel, columns), BF16),
             pltpu.VMEM((local, columns), BF16),
-            pltpu.VMEM((local, columns), BF16),
-            pltpu.SemaphoreType.DMA((2, len(backs), 2)),
             pltpu.SemaphoreType.DMA((2,)),
-            pltpu.SemaphoreType.DMA((2,)),
+            pltpu.SemaphoreType.DMA((4,)),
         ],
-        compiler_params=pltpu.CompilerParams(vmem_limit_bytes=20 * 1024 * 1024),
+        compiler_params=pltpu.CompilerParams(vmem_limit_bytes=16 * 1024 * 1024),
         name="tail",
-    )(at, keep, given, *parts, stay, *[far(piece) for _, piece in pieces], far(down_weight))
+    )(at, mine, keep, given, *parts, down_weight, close(staged), pieces[7][1], pieces[8][1])
+    return out
 
 
 def solution(mesh):

time: 108 us -> 124 us (1.15)
  waiting for transfers between devices: 45.5 us -> 61 us
  local copies, waits for them, and re-layouts: 4.13 us -> 6.59 us
  Pallas kernels: 10.7 us -> 8.93 us
  starting transfers between devices: 39.7 us -> 38.1 us
    ppermute x24, waiting for transfers between devices: 41.2 us -> 57.6 us  [shift(): return lax.ppermute(x, axis, [(i, (i + by) % n) for i in range(n)])]
    dynamic_update_slice x10, local copies, waits for them, and re-layouts: 0.23 us -> 4.49 us  [place(): out = lax.dynamic_update_slice(out, jnp.expand_dims(piece, dim), at)]
    unnamed x20 -> x4, local copies, waits for them, and re-layouts: 2.32 us -> 0.01 us
    pallas_call x1 -> x2, Pallas kernels: 8.03 us -> 6.3 us  [the longest x1 5.86 us: compute(): pl.pallas_call(tail_kernel, out_shape=(jax.ShapeDtypeStruct((local, colum...]
    ppermute x24, starting transfers between devices: 31.3 us -> 29.7 us  [shift(): return lax.ppermute(x, axis, [(i, (i + by) % n) for i in range(n)])]
  transfers between devices with their start and end apart: 25 -> 25, of which waited for: 11 -> 13; matrix products, arithmetic and copies ran while one was open for 4% -> 7% of each run, Pallas kernels for 2% -> 3%
where the time goes in v6:
time: 124 us; the launch traced here: 122 us
  waiting for transfers between devices  61 us (49%)
  starting transfers between devices  38.1 us (31%)
  Pallas kernels  8.93 us (7%)
  local copies, waits for them, and re-layouts  6.59 us (5%)
  matrix products  3.28 us (3%)
  other arithmetic  3.03 us (2%)
    ppermute x24, waiting for transfers between devices, shift(): return lax.ppermute(x, axis, [(i, (i + by) % n) for i in range(n)])  57.6 us
    ppermute x24, starting transfers between devices, shift(): return lax.ppermute(x, axis, [(i, (i + by) % n) for i in range(n)])  29.7 us
    all_to_all x1, starting transfers between devices, to_all(): lax.all_to_all(jnp.broadcast_to(x, (n, *x.shape)), axes, split_axis=0, co...  8.47 us
    pallas_call x1, Pallas kernels, compute(): pl.pallas_call(tail_kernel, out_shape=(jax.ShapeDtypeStruct((local, colum...  5.86 us
    dynamic_update_slice x10, local copies, waits for them, and re-layouts, place(): out = lax.dynamic_update_slice(out, jnp.expand_dims(piece, dim), at)  4.49 us
    all_to_all x1, waiting for transfers between devices, to_all(): lax.all_to_all(jnp.broadcast_to(x, (n, *x.shape)), axes, split_axis=0, co...  3.45 us
  transfers between devices with their start and end apart: 25, of which 13 were waited for; matrix products, arithmetic and copies ran while one was open for 7% of the time, Pallas kernels for 3%

profile of v6, /device:TPU:8, one launch (start us, length us, event | category | flops | bytes accessed | tf_op | source)
XLA Modules:
  0.0 122.1 jit_solution(10600590208682728056)
XLA Ops:
  1.6 2.3 %convolution_convert_fusion.1 = bf16[16,1024]{1,0:T(8,128)(2,1)S(1)} fusion(s32[16]{0:T(128)S(1)} %sub.26.mine_ref, f32[1024]{0:T(1024)S(1)} %fusion.9, bf16[1024,2,448]{0,2,1:T(8,128)(2,1)} %param.5), kind=kOutput, calls=%fused_computation.9 | convolution fusion | flops 18832384 | bytes 1871936 | tf_op jit(solution)/shard_map/dot_general | solution.py:235
  4.5 1.0 bitcast_dynamic-update-slice_fusion.9
  5.5 3.0 %collective-permute-start.12 = (bf16[2,8,2048]{2,1,0:T(8,128)(2,1)S(1)}, bf16[2,8,2048]{2,1,0:T(8,128)(2,1)S(1)}, u32[]{:S(2)}, u32[]{:S(2)}) collective-permute-start(bf16[2,8,2048]{2,1,0:T(8,128)(2,1)S(1)} %bitcast.75), channel_id=1, source_target_pairs={{0,4},{4,0},{1,5},{5,1},{2,6},{6,2},{3,7},{7,3},{8,12},{12,8},{9,1... | collective-permute-start | bytes 196616 | tf_op jit(solution)/shard_map/ppermute | solution.py:22
  9.3 8.5 %all-to-all-start = ((bf16[8,16,1024]{2,1,0:T(8,128)(2,1)}), bf16[8,16,1024]{2,1,0:T(8,128)(2,1)S(1)}, u32[]{:S(2)}, u32[]{:S(2)}) async-start(bf16[8,16,1024]{2,1,0:T(8,128)(2,1)} %broadcast_in_dim.55), calls=%async_computation | async-start | bytes 524288 | tf_op jit(solution)/shard_map/all_to_all | solution.py:27
  17.7 2.1 %fusion.14.hidden_ref = bf16[448,1024]{1,0:T(8,128)(2,1)S(1)} fusion(f32[1024]{0:T(1024)S(1)} %fusion.9, bf16[1024,2,448]{0,2,1:T(8,128)(2,1)} %param.5), kind=kLoop, calls=%fused_computation.31 | loop fusion | flops 4128768 | bytes 2756608 | tf_op jit(solution)/shard_map/transpose | solution.py:266
  20.6 2.3 %collective-permute-start.15 = (bf16[2,2,8,2048]{3,2,1,0:T(8,128)(2,1)}, bf16[2,2,8,2048]{3,2,1,0:T(8,128)(2,1)}, u32[]{:S(2)}, u32[]{:S(2)}) collective-permute-start(bf16[2,2,8,2048]{3,2,1,0:T(8,128)(2,1)} %bitcast_dynamic-update-slice_fusion.10), channel_id=1, source_target_pairs={{0,16},{8,24},{16,0},{24,8},{1,17},{9,25},{17,1},{25,9},{2,18},{10... | collective-permute-start | bytes 393224 | tf_op jit(solution)/shard_map/ppermute | solution.py:22
  22.9 1.3 %collective-permute-start.14 = (bf16[2,2,8,2048]{3,2,1,0:T(8,128)(2,1)}, bf16[2,2,8,2048]{3,2,1,0:T(8,128)(2,1)}, u32[]{:S(2)}, u32[]{:S(2)}) collective-permute-start(bf16[2,2,8,2048]{3,2,1,0:T(8,128)(2,1)} %bitcast_dynamic-update-slice_fusion.10), channel_id=1, source_target_pairs={{0,24},{8,0},{16,8},{24,16},{1,25},{9,1},{17,9},{25,17},{2,26},{10... | collective-permute-start | bytes 393224 | tf_op jit(solution)/shard_map/ppermute | solution.py:22
  24.9 0.9 bitcast_dynamic-update-slice_fusion.7
  25.9 3.4 %all-to-all-done = bf16[8,16,1024]{2,1,0:T(8,128)(2,1)S(1)} async-done(((bf16[8,16,1024]{2,1,0:T(8,128)(2,1)}), bf16[8,16,1024]{2,1,0:T(8,128)(2,1)S(1)}, u32[]{:S(2)}, u32[]{:S(2)}) %all-to-all-start) | async-done | bytes 262176 | tf_op jit(solution)/shard_map/all_to_all | solution.py:27
  31.1 6.1 %collective-permute-done = bf16[128,1024]{1,0:T(8,128)(2,1)S(1)} collective-permute-done((bf16[128,1024]{1,0:T(8,128)(2,1)S(1)}, bf16[128,1024]{1,0:T(8,128)(2,1)S(1)}, u32[]{:S(2)}, u32[]{:S(2)}) %collective-permute-start) | collective-permute-done | bytes 262176 | tf_op jit(solution)/shard_map/ppermute | solution.py:22
  37.8 1.6 %collective-permute-start.1 = (bf16[2,128,1024]{2,1,0:T(8,128)(2,1)S(1)}, bf16[2,128,1024]{2,1,0:T(8,128)(2,1)S(1)}, u32[]{:S(2)}, u32[]{:S(2)}) collective-permute-start(bf16[2,128,1024]{2,1,0:T(8,128)(2,1)S(1)} %bitcast_dynamic-update-slice_fusion.3), channel_id=1, source_target_pairs={{0,8},{8,16},{16,24},{24,0},{1,9},{9,17},{17,25},{25,1},{2,10},{10... | collective-permute-start | bytes 1572872 | tf_op jit(solution)/shard_map/ppermute | solution.py:22
  40.6 8.7 %collective-permute-done.2 = bf16[2,128,1024]{2,1,0:T(8,128)(2,1)S(1)} collective-permute-done((bf16[2,128,1024]{2,1,0:T(8,128)(2,1)S(1)}, bf16[2,128,1024]{2,1,0:T(8,128)(2,1)S(1)}, u32[]{:S(2)}, u32[]{:S(2)}) %collective-permute-start.2) | collective-permute-done | bytes 524320 | tf_op jit(solution)/shard_map/ppermute | solution.py:22
  49.5 2.1 %collective-permute-start.3 = (bf16[1,128,1024]{2,1,0:T(8,128)(2,1)S(1)}, bf16[1,128,1024]{2,1,0:T(8,128)(2,1)S(1)}, u32[]{:S(2)}, u32[]{:S(2)}) collective-permute-start(bf16[1,128,1024]{2,1,0:T(8,128)(2,1)S(1)} %slice.16), channel_id=1, source_target_pairs={{0,8},{8,16},{16,24},{24,0},{1,9},{9,17},{17,25},{25,1},{2,10},{10... | collective-permute-start | bytes 786440 | tf_op jit(solution)/shard_map/ppermute | solution.py:22
  51.6 4.1 %collective-permute-done.4 = bf16[1,128,1024]{2,1,0:T(8,128)(2,1)S(1)} collective-permute-done((bf16[1,128,1024]{2,1,0:T(8,128)(2,1)S(1)}, bf16[1,128,1024]{2,1,0:T(8,128)(2,1)S(1)}, u32[]{:S(2)}, u32[]{:S(2)}) %collective-permute-start.4) | collective-permute-done | bytes 262176 | tf_op jit(solution)/shard_map/ppermute | solution.py:22
  55.8 1.5 %collective-permute-done.3 = bf16[1,128,1024]{2,1,0:T(8,128)(2,1)S(1)} collective-permute-done((bf16[1,128,1024]{2,1,0:T(8,128)(2,1)S(1)}, bf16[1,128,1024]{2,1,0:T(8,128)(2,1)S(1)}, u32[]{:S(2)}, u32[]{:S(2)}) %collective-permute-start.3) | collective-permute-done | bytes 262176 | tf_op jit(solution)/shard_map/ppermute | solution.py:22
  57.6 2.0 %partial.1 = (f32[712,512]{1,0:T(8,128)S(1)}, bf16[712,512]{1,0:T(8,128)(2,1)S(1)}) custom-call(s32[1]{0:T(128)} %bitcast.core_ref, s32[1]{0:T(128)} %copy.29.count_ref, bf16[448,1024]{1,0:T(8,128)(2,1)S(1)} %fusion.14.hidden_ref, bf16[2,512,1024]{2,1,0:T(8,128)(2,1)S(1)} %bitcast.68), custom_call_target="tpu_custom_call" | custom-call | tf_op jit(solution)/shard_map/partial/pallas_call | solution.py:256
  60.8 2.0 %collective-permute-start.16 = (bf16[2,64,2048]{2,1,0:T(8,128)(2,1)S(1)}, bf16[2,64,2048]{2,1,0:T(8,128)(2,1)S(1)}, u32[]{:S(2)}, u32[]{:S(2)}) collective-permute-start(bf16[2,64,2048]{2,1,0:T(8,128)(2,1)S(1)} %bitcast.70), channel_id=1, source_target_pairs={{0,32},{32,64},{64,96},{96,128},{128,160},{160,192},{192,224},{224... | collective-permute-start | bytes 1572872 | tf_op jit(solution)/shard_map/ppermute | solution.py:22
  62.7 12.3 %collective-permute-done.17.refs_2_ = bf16[2,64,2048]{2,1,0:T(8,128)(2,1)S(1)} collective-permute-done((bf16[2,64,2048]{2,1,0:T(8,128)(2,1)S(1)}, bf16[2,64,2048]{2,1,0:T(8,128)(2,1)S(1)}, u32[]{:S(2)}, u32[]{:S(2)}) %collective-permute-start.17) | collective-permute-done | bytes 524320 | tf_op jit(solution)/shard_map/ppermute | solution.py:22
  75.0 1.5 %collective-permute-start.19 = (bf16[2,64,2048]{2,1,0:T(8,128)(2,1)S(1)}, bf16[2,64,2048]{2,1,0:T(8,128)(2,1)S(1)}, u32[]{:S(2)}, u32[]{:S(2)}) collective-permute-start(bf16[2,64,2048]{2,1,0:T(8,128)(2,1)S(1)} %collective-permute-done.17.refs_2_), channel_id=1, source_target_pairs={{0,224},{32,0},{64,32},{96,64},{128,96},{160,128},{192,160},{224,1... | collective-permute-start | bytes 1572872 | tf_op jit(solution)/shard_map/ppermute | solution.py:22
  77.9 1.4 %collective-permute-start.7 = (bf16[72,512]{1,0:T(8,128)(2,1)S(1)}, bf16[72,512]{1,0:T(8,128)(2,1)S(1)}, u32[]{:S(2)}, u32[]{:S(2)}) collective-permute-start(bf16[72,512]{1,0:T(8,128)(2,1)S(1)} %get-tuple-element.27), channel_id=1, source_target_pairs={{0,2},{2,0},{1,3},{3,1},{4,6},{6,4},{5,7},{7,5},{8,10},{10,8},{9,1... | collective-permute-start | bytes 221192 | tf_op jit(solution)/shard_map/ppermute | solution.py:22
  79.3 11.1 %collective-permute-done.7.given_ref = bf16[72,512]{1,0:T(8,128)(2,1)S(1)} collective-permute-done((bf16[72,512]{1,0:T(8,128)(2,1)S(1)}, bf16[72,512]{1,0:T(8,128)(2,1)S(1)}, u32[]{:S(2)}, u32[]{:S(2)}) %collective-permute-start.7) | collective-permute-done | bytes 73760 | tf_op jit(solution)/shard_map/ppermute | solution.py:22
  90.4 2.0 %collective-permute-start.10 = (bf16[64,512]{1,0:T(8,128)(2,1)S(1)}, bf16[64,512]{1,0:T(8,128)(2,1)S(1)}, u32[]{:S(2)}, u32[]{:S(2)}) collective-permute-start(bf16[64,512]{1,0:T(8,128)(2,1)S(1)} %get-tuple-element.29.refs_0_), channel_id=1, source_target_pairs={{0,16},{8,24},{16,0},{24,8},{1,17},{9,25},{17,1},{25,9},{2,18},{10... | collective-permute-start | bytes 196616 | tf_op jit(solution)/shard_map/ppermute | solution.py:22
  92.5 3.0 %collective-permute-start.21 = (bf16[2,64,2048]{2,1,0:T(8,128)(2,1)S(1)}, bf16[2,64,2048]{2,1,0:T(8,128)(2,1)S(1)}, u32[]{:S(2)}, u32[]{:S(2)}) collective-permute-start(bf16[2,64,2048]{2,1,0:T(8,128)(2,1)S(1)} %collective-permute-done.19.refs_4_), channel_id=1, source_target_pairs={{0,224},{32,0},{64,32},{96,64},{128,96},{160,128},{192,160},{224,1... | collective-permute-start | bytes 1572872 | tf_op jit(solution)/shard_map/ppermute | solution.py:22
  95.4 1.4 %collective-permute-start.9 = (bf16[64,512]{1,0:T(8,128)(2,1)S(1)}, bf16[64,512]{1,0:T(8,128)(2,1)S(1)}, u32[]{:S(2)}, u32[]{:S(2)}) collective-permute-start(bf16[64,512]{1,0:T(8,128)(2,1)S(1)} %get-tuple-element.29.refs_0_), channel_id=1, source_target_pairs={{0,24},{8,0},{16,8},{24,16},{1,25},{9,1},{17,9},{25,17},{2,26},{10... | collective-permute-start | bytes 196616 | tf_op jit(solution)/shard_map/ppermute | solution.py:22
  96.8 1.5 %collective-permute-start.8 = (bf16[64,512]{1,0:T(8,128)(2,1)S(1)}, bf16[64,512]{1,0:T(8,128)(2,1)S(1)}, u32[]{:S(2)}, u32[]{:S(2)}) collective-permute-start(bf16[64,512]{1,0:T(8,128)(2,1)S(1)} %get-tuple-element.29.refs_0_), channel_id=1, source_target_pairs={{0,8},{8,16},{16,24},{24,0},{1,9},{9,17},{17,25},{25,1},{2,10},{10... | collective-permute-start | bytes 196616 | tf_op jit(solution)/shard_map/ppermute | solution.py:22
  98.2 2.1 %collective-permute-done.9.refs_2_ = bf16[64,512]{1,0:T(8,128)(2,1)S(1)} collective-permute-done((bf16[64,512]{1,0:T(8,128)(2,1)S(1)}, bf16[64,512]{1,0:T(8,128)(2,1)S(1)}, u32[]{:S(2)}, u32[]{:S(2)}) %collective-permute-start.9) | collective-permute-done | bytes 65568 | tf_op jit(solution)/shard_map/ppermute | solution.py:22
  100.4 1.3 %collective-permute-done.8.refs_1_ = bf16[64,512]{1,0:T(8,128)(2,1)S(1)} collective-permute-done((bf16[64,512]{1,0:T(8,128)(2,1)S(1)}, bf16[64,512]{1,0:T(8,128)(2,1)S(1)}, u32[]{:S(2)}, u32[]{:S(2)}) %collective-permute-start.8) | collective-permute-done | bytes 65568 | tf_op jit(solution)/shard_map/ppermute | solution.py:22
  102.0 3.0 %collective-permute-done.21.refs_6_.behind_ref = bf16[2,64,2048]{2,1,0:T(8,128)(2,1)S(1)} collective-permute-done((bf16[2,64,2048]{2,1,0:T(8,128)(2,1)S(1)}, bf16[2,64,2048]{2,1,0:T(8,128)(2,1)S(1)}, u32[]{:S(2)}, u32[]{:S(2)}) %collective-permute-start.21) | collective-permute-done | bytes 524320 | tf_op jit(solution)/shard_map/ppermute | solution.py:22
  105.0 3.4 %collective-permute-done.20.refs_5_.ahead_ref = bf16[2,64,2048]{2,1,0:T(8,128)(2,1)S(1)} collective-permute-done((bf16[2,64,2048]{2,1,0:T(8,128)(2,1)S(1)}, bf16[2,64,2048]{2,1,0:T(8,128)(2,1)S(1)}, u32[]{:S(2)}, u32[]{:S(2)}) %collective-permute-start.20) | collective-permute-done | bytes 524320 | tf_op jit(solution)/shard_map/ppermute | solution.py:22
  108.5 3.2 %collective-permute-start.23 = (bf16[1,64,2048]{2,1,0:T(8,128)(2,1)S(1)}, bf16[1,64,2048]{2,1,0:T(8,128)(2,1)S(1)}, u32[]{:S(2)}, u32[]{:S(2)}) collective-permute-start(bf16[1,64,2048]{2,1,0:T(8,128)(2,1)S(1)} %get-tuple-element.35), channel_id=1, source_target_pairs={{0,224},{32,0},{64,32},{96,64},{128,96},{160,128},{192,160},{224,1... | collective-permute-start | bytes 786440 | tf_op jit(solution)/shard_map/ppermute | solution.py:22
  112.6 3.5 %collective-permute-done.22.ahead_ref = bf16[1,64,2048]{2,1,0:T(8,128)(2,1)S(1)} collective-permute-done((bf16[1,64,2048]{2,1,0:T(8,128)(2,1)S(1)}, bf16[1,64,2048]{2,1,0:T(8,128)(2,1)S(1)}, u32[]{:S(2)}, u32[]{:S(2)}) %collective-permute-start.22) | collective-permute-done | bytes 262176 | tf_op jit(solution)/shard_map/ppermute | solution.py:22
  116.1 5.9 %tail.1 = (bf16[448,2048]{1,0:T(8,128)(2,1)}, bf16[2,512,2048]{2,1,0:T(8,128)(2,1)S(1)}) custom-call(s32[2]{0:T(128)S(1)} %pad_add_fusion.at_ref, s32[16]{0:T(128)S(1)} %sub.26.mine_ref, bf16[704,512]{1,0:T(8,128)(2,1)S(1)} %join.1.keep_ref, bf16[704,512]{1,0:T(8,128)(2,1)S(1)} %collective-permute-done.11.given_ref, ...), custom_call_target="tpu_custom_call", output_to_operand_aliasing={{1}: (7, {})} | custom-call | tf_op jit(solution)/shard_map/tail/pallas_call | solution.py:313
  (57 shorter events, 11.4 us)
Async XLA Ops:
  1.6 3.0 %copy-start = (bf16[448,2048]{1,0:T(8,128)(2,1)S(1)}, bf16[448,2048]{1,0:T(8,128)(2,1)}, u32[]{:S(2)}) copy-start(bf16[448,2048]{1,0:T(8,128)(2,1)} %old_ref.1) | copy-start | bytes 5505028
  5.5 14.4 %collective-permute-start.12 = (bf16[2,8,2048]{2,1,0:T(8,128)(2,1)S(1)}, bf16[2,8,2048]{2,1,0:T(8,128)(2,1)S(1)}, u32[]{:S(2)}, u32[]{:S(2)}) collective-permute-start(bf16[2,8,2048]{2,1,0:T(8,128)(2,1)S(1)} %bitcast.75), channel_id=1, source_target_pairs={{0,4},{4,0},{1,5},{5,1},{2,6},{6,2},{3,7},{7,3},{8,12},{12,8},{9,1... | collective-permute-start | bytes 196616 | tf_op jit(solution)/shard_map/ppermute | solution.py:22
  9.3 20.1 %all-to-all-start = ((bf16[8,16,1024]{2,1,0:T(8,128)(2,1)}), bf16[8,16,1024]{2,1,0:T(8,128)(2,1)S(1)}, u32[]{:S(2)}, u32[]{:S(2)}) async-start(bf16[8,16,1024]{2,1,0:T(8,128)(2,1)} %broadcast_in_dim.55), calls=%async_computation | async-start | bytes 524288 | tf_op jit(solution)/shard_map/all_to_all | solution.py:27
  20.6 39.1 %collective-permute-start.15 = (bf16[2,2,8,2048]{3,2,1,0:T(8,128)(2,1)}, bf16[2,2,8,2048]{3,2,1,0:T(8,128)(2,1)}, u32[]{:S(2)}, u32[]{:S(2)}) collective-permute-start(bf16[2,2,8,2048]{3,2,1,0:T(8,128)(2,1)} %bitcast_dynamic-update-slice_fusion.10), channel_id=1, source_target_pairs={{0,16},{8,24},{16,0},{24,8},{1,17},{9,25},{17,1},{25,9},{2,18},{10... | collective-permute-start | bytes 393224 | tf_op jit(solution)/shard_map/ppermute | solution.py:22
  22.9 16.5 %collective-permute-start.14 = (bf16[2,2,8,2048]{3,2,1,0:T(8,128)(2,1)}, bf16[2,2,8,2048]{3,2,1,0:T(8,128)(2,1)}, u32[]{:S(2)}, u32[]{:S(2)}) collective-permute-start(bf16[2,2,8,2048]{3,2,1,0:T(8,128)(2,1)} %bitcast_dynamic-update-slice_fusion.10), channel_id=1, source_target_pairs={{0,24},{8,0},{16,8},{24,16},{1,25},{9,1},{17,9},{25,17},{2,26},{10... | collective-permute-start | bytes 393224 | tf_op jit(solution)/shard_map/ppermute | solution.py:22
  24.2 5.8 %collective-permute-start.13 = (bf16[2,2,8,2048]{3,2,1,0:T(8,128)(2,1)}, bf16[2,2,8,2048]{3,2,1,0:T(8,128)(2,1)}, u32[]{:S(2)}, u32[]{:S(2)}) collective-permute-start(bf16[2,2,8,2048]{3,2,1,0:T(8,128)(2,1)} %bitcast_dynamic-update-slice_fusion.10), channel_id=1, source_target_pairs={{0,8},{8,16},{16,24},{24,0},{1,9},{9,17},{17,25},{25,1},{2,10},{10... | collective-permute-start | bytes 393224 | tf_op jit(solution)/shard_map/ppermute | solution.py:22
  29.3 7.9 %collective-permute-start = (bf16[128,1024]{1,0:T(8,128)(2,1)S(1)}, bf16[128,1024]{1,0:T(8,128)(2,1)S(1)}, u32[]{:S(2)}, u32[]{:S(2)}) collective-permute-start(bf16[128,1024]{1,0:T(8,128)(2,1)S(1)} %bitcast.73), channel_id=1, source_target_pairs={{0,4},{4,0},{1,5},{5,1},{2,6},{6,2},{3,7},{7,3},{8,12},{12,8},{9,1... | collective-permute-start | bytes 786440 | tf_op jit(solution)/shard_map/ppermute | solution.py:22
  37.2 12.1 %collective-permute-start.2 = (bf16[2,128,1024]{2,1,0:T(8,128)(2,1)S(1)}, bf16[2,128,1024]{2,1,0:T(8,128)(2,1)S(1)}, u32[]{:S(2)}, u32[]{:S(2)}) collective-permute-start(bf16[2,128,1024]{2,1,0:T(8,128)(2,1)S(1)} %bitcast_dynamic-update-slice_fusion.3), channel_id=1, source_target_pairs={{0,24},{8,0},{16,8},{24,16},{1,25},{9,1},{17,9},{25,17},{2,26},{10... | collective-permute-start | bytes 1572872 | tf_op jit(solution)/shard_map/ppermute | solution.py:22
  37.8 11.7 %collective-permute-start.1 = (bf16[2,128,1024]{2,1,0:T(8,128)(2,1)S(1)}, bf16[2,128,1024]{2,1,0:T(8,128)(2,1)S(1)}, u32[]{:S(2)}, u32[]{:S(2)}) collective-permute-start(bf16[2,128,1024]{2,1,0:T(8,128)(2,1)S(1)} %bitcast_dynamic-update-slice_fusion.3), channel_id=1, source_target_pairs={{0,8},{8,16},{16,24},{24,0},{1,9},{9,17},{17,25},{25,1},{2,10},{10... | collective-permute-start | bytes 1572872 | tf_op jit(solution)/shard_map/ppermute | solution.py:22
  49.3 6.4 %collective-permute-start.4 = (bf16[1,128,1024]{2,1,0:T(8,128)(2,1)S(1)}, bf16[1,128,1024]{2,1,0:T(8,128)(2,1)S(1)}, u32[]{:S(2)}, u32[]{:S(2)}) collective-permute-start(bf16[1,128,1024]{2,1,0:T(8,128)(2,1)S(1)} %slice.17), channel_id=1, source_target_pairs={{0,24},{8,0},{16,8},{24,16},{1,25},{9,1},{17,9},{25,17},{2,26},{10... | collective-permute-start | bytes 786440 | tf_op jit(solution)/shard_map/ppermute | solution.py:22
  49.5 7.9 %collective-permute-start.3 = (bf16[1,128,1024]{2,1,0:T(8,128)(2,1)S(1)}, bf16[1,128,1024]{2,1,0:T(8,128)(2,1)S(1)}, u32[]{:S(2)}, u32[]{:S(2)}) collective-permute-start(bf16[1,128,1024]{2,1,0:T(8,128)(2,1)S(1)} %slice.16), channel_id=1, source_target_pairs={{0,8},{8,16},{16,24},{24,0},{1,9},{9,17},{17,25},{25,1},{2,10},{10... | collective-permute-start | bytes 786440 | tf_op jit(solution)/shard_map/ppermute | solution.py:22
  59.6 17.5 %collective-permute-start.5 = (bf16[712,512]{1,0:T(8,128)(2,1)S(1)}, bf16[712,512]{1,0:T(8,128)(2,1)S(1)}, u32[]{:S(2)}, u32[]{:S(2)}) collective-permute-start(bf16[712,512]{1,0:T(8,128)(2,1)S(1)} %get-tuple-element.23), channel_id=1, source_target_pairs={{0,1},{1,0},{2,3},{3,2},{4,5},{5,4},{6,7},{7,6},{8,9},{9,8},{10,11... | collective-permute-start | bytes 2187272 | tf_op jit(solution)/shard_map/ppermute | solution.py:22
  60.6 14.4 %collective-permute-start.17 = (bf16[2,64,2048]{2,1,0:T(8,128)(2,1)S(1)}, bf16[2,64,2048]{2,1,0:T(8,128)(2,1)S(1)}, u32[]{:S(2)}, u32[]{:S(2)}) collective-permute-start(bf16[2,64,2048]{2,1,0:T(8,128)(2,1)S(1)} %bitcast.69), channel_id=1, source_target_pairs={{0,224},{32,0},{64,32},{96,64},{128,96},{160,128},{192,160},{224,1... | collective-permute-start | bytes 1572872 | tf_op jit(solution)/shard_map/ppermute | solution.py:22
  60.8 15.7 %collective-permute-start.16 = (bf16[2,64,2048]{2,1,0:T(8,128)(2,1)S(1)}, bf16[2,64,2048]{2,1,0:T(8,128)(2,1)S(1)}, u32[]{:S(2)}, u32[]{:S(2)}) collective-permute-start(bf16[2,64,2048]{2,1,0:T(8,128)(2,1)S(1)} %bitcast.70), channel_id=1, source_target_pairs={{0,32},{32,64},{64,96},{96,128},{128,160},{160,192},{192,224},{224... | collective-permute-start | bytes 1572872 | tf_op jit(solution)/shard_map/ppermute | solution.py:22
  75.0 17.5 %collective-permute-start.19 = (bf16[2,64,2048]{2,1,0:T(8,128)(2,1)S(1)}, bf16[2,64,2048]{2,1,0:T(8,128)(2,1)S(1)}, u32[]{:S(2)}, u32[]{:S(2)}) collective-permute-start(bf16[2,64,2048]{2,1,0:T(8,128)(2,1)S(1)} %collective-permute-done.17.refs_2_), channel_id=1, source_target_pairs={{0,224},{32,0},{64,32},{96,64},{128,96},{160,128},{192,160},{224,1... | collective-permute-start | bytes 1572872 | tf_op jit(solution)/shard_map/ppermute | solution.py:22
  76.5 18.9 %collective-permute-start.18 = (bf16[2,64,2048]{2,1,0:T(8,128)(2,1)S(1)}, bf16[2,64,2048]{2,1,0:T(8,128)(2,1)S(1)}, u32[]{:S(2)}, u32[]{:S(2)}) collective-permute-start(bf16[2,64,2048]{2,1,0:T(8,128)(2,1)S(1)} %collective-permute-done.16.refs_1_), channel_id=1, source_target_pairs={{0,32},{32,64},{64,96},{96,128},{128,160},{160,192},{192,224},{224... | collective-permute-start | bytes 1572872 | tf_op jit(solution)/shard_map/ppermute | solution.py:22
  77.2 34.6 %copy-start.1 = (f32[2,512,512]{2,1,0:T(8,128)S(1)}, f32[2,512,512]{2,1,0:T(8,128)}, u32[]{:S(2)}) copy-start(f32[2,512,512]{2,1,0:T(8,128)} %x_ref) | copy-start | bytes 6291460
  77.2 24.5 %collective-permute-start.6 = (bf16[448,512]{1,0:T(8,128)(2,1)S(1)}, bf16[448,512]{1,0:T(8,128)(2,1)S(1)}, u32[]{:S(2)}, u32[]{:S(2)}) collective-permute-start(bf16[448,512]{1,0:T(8,128)(2,1)S(1)} %get-tuple-element.25), channel_id=1, source_target_pairs={{0,2},{2,0},{1,3},{3,1},{4,6},{6,4},{5,7},{7,5},{8,10},{10,8},{9,1... | collective-permute-start | bytes 1376264 | tf_op jit(solution)/shard_map/ppermute | solution.py:22
  77.9 12.5 %collective-permute-start.7 = (bf16[72,512]{1,0:T(8,128)(2,1)S(1)}, bf16[72,512]{1,0:T(8,128)(2,1)S(1)}, u32[]{:S(2)}, u32[]{:S(2)}) collective-permute-start(bf16[72,512]{1,0:T(8,128)(2,1)S(1)} %get-tuple-element.27), channel_id=1, source_target_pairs={{0,2},{2,0},{1,3},{3,1},{4,6},{6,4},{5,7},{7,5},{8,10},{10,8},{9,1... | collective-permute-start | bytes 221192 | tf_op jit(solution)/shard_map/ppermute | solution.py:22
  90.4 6.4 %collective-permute-start.10 = (bf16[64,512]{1,0:T(8,128)(2,1)S(1)}, bf16[64,512]{1,0:T(8,128)(2,1)S(1)}, u32[]{:S(2)}, u32[]{:S(2)}) collective-permute-start(bf16[64,512]{1,0:T(8,128)(2,1)S(1)} %get-tuple-element.29.refs_0_), channel_id=1, source_target_pairs={{0,16},{8,24},{16,0},{24,8},{1,17},{9,25},{17,1},{25,9},{2,18},{10... | collective-permute-start | bytes 196616 | tf_op jit(solution)/shard_map/ppermute | solution.py:22
  92.5 12.5 %collective-permute-start.21 = (bf16[2,64,2048]{2,1,0:T(8,128)(2,1)S(1)}, bf16[2,64,2048]{2,1,0:T(8,128)(2,1)S(1)}, u32[]{:S(2)}, u32[]{:S(2)}) collective-permute-start(bf16[2,64,2048]{2,1,0:T(8,128)(2,1)S(1)} %collective-permute-done.19.refs_4_), channel_id=1, source_target_pairs={{0,224},{32,0},{64,32},{96,64},{128,96},{160,128},{192,160},{224,1... | collective-permute-start | bytes 1572872 | tf_op jit(solution)/shard_map/ppermute | solution.py:22
  95.4 12.9 %collective-permute-start.20 = (bf16[2,64,2048]{2,1,0:T(8,128)(2,1)S(1)}, bf16[2,64,2048]{2,1,0:T(8,128)(2,1)S(1)}, u32[]{:S(2)}, u32[]{:S(2)}) collective-permute-start(bf16[2,64,2048]{2,1,0:T(8,128)(2,1)S(1)} %collective-permute-done.18.refs_3_), channel_id=1, source_target_pairs={{0,32},{32,64},{64,96},{96,128},{128,160},{160,192},{192,224},{224... | collective-permute-start | bytes 1572872 | tf_op jit(solution)/shard_map/ppermute | solution.py:22
  95.4 5.0 %collective-permute-start.9 = (bf16[64,512]{1,0:T(8,128)(2,1)S(1)}, bf16[64,512]{1,0:T(8,128)(2,1)S(1)}, u32[]{:S(2)}, u32[]{:S(2)}) collective-permute-start(bf16[64,512]{1,0:T(8,128)(2,1)S(1)} %get-tuple-element.29.refs_0_), channel_id=1, source_target_pairs={{0,24},{8,0},{16,8},{24,16},{1,25},{9,1},{17,9},{25,17},{2,26},{10... | collective-permute-start | bytes 196616 | tf_op jit(solution)/shard_map/ppermute | solution.py:22
  96.8 5.0 %collective-permute-start.8 = (bf16[64,512]{1,0:T(8,128)(2,1)S(1)}, bf16[64,512]{1,0:T(8,128)(2,1)S(1)}, u32[]{:S(2)}, u32[]{:S(2)}) collective-permute-start(bf16[64,512]{1,0:T(8,128)(2,1)S(1)} %get-tuple-element.29.refs_0_), channel_id=1, source_target_pairs={{0,8},{8,16},{16,24},{24,0},{1,9},{9,17},{17,25},{25,1},{2,10},{10... | collective-permute-start | bytes 196616 | tf_op jit(solution)/shard_map/ppermute | solution.py:22
  101.9 14.2 %collective-permute-start.11 = (bf16[704,512]{1,0:T(8,128)(2,1)S(1)}, bf16[704,512]{1,0:T(8,128)(2,1)S(1)}, u32[]{:S(2)}, u32[]{:S(2)}) collective-permute-start(bf16[704,512]{1,0:T(8,128)(2,1)S(1)} %join.1.keep_ref), channel_id=1, source_target_pairs={{0,1},{1,0},{2,3},{3,2},{4,5},{5,4},{6,7},{7,6},{8,9},{9,8},{10,11... | collective-permute-start | bytes 2162696 | tf_op jit(solution)/shard_map/ppermute | solution.py:22
  108.4 7.7 %collective-permute-start.22 = (bf16[1,64,2048]{2,1,0:T(8,128)(2,1)S(1)}, bf16[1,64,2048]{2,1,0:T(8,128)(2,1)S(1)}, u32[]{:S(2)}, u32[]{:S(2)}) collective-permute-start(bf16[1,64,2048]{2,1,0:T(8,128)(2,1)S(1)} %get-tuple-element.34), channel_id=1, source_target_pairs={{0,32},{32,64},{64,96},{96,128},{128,160},{160,192},{192,224},{224... | collective-permute-start | bytes 786440 | tf_op jit(solution)/shard_map/ppermute | solution.py:22
  108.5 7.6 %collective-permute-start.23 = (bf16[1,64,2048]{2,1,0:T(8,128)(2,1)S(1)}, bf16[1,64,2048]{2,1,0:T(8,128)(2,1)S(1)}, u32[]{:S(2)}, u32[]{:S(2)}) collective-permute-start(bf16[1,64,2048]{2,1,0:T(8,128)(2,1)S(1)} %get-tuple-element.35), channel_id=1, source_target_pairs={{0,224},{32,0},{64,32},{96,64},{128,96},{160,128},{192,160},{224,1... | collective-permute-start | bytes 786440 | tf_op jit(solution)/shard_map/ppermute | solution.py:22

commit v7 on v6

--- a/solution.py
+++ b/solution.py
@@ -39,11 +39,14 @@
     return out
 
 
-def gather_rows(rows):
+def gather_rows(rows, acts):
     other = shift(rows, "xh", 1)
     both = place([(0, rows), (1, other)], "xh", 1)
-    others = [(k, shift(both, "y", k)) for k in (1, 3, 2)]
-    around = place([(0, both)] + others, "y", 1)
+    others = []
+    for k in (1, 3, 2):
+        others.append(shift(both, "y", k))
+    others, _ = lax.optimization_barrier((others, acts))
+    around = place([(0, both)] + list(zip((1, 3, 2), others)), "y", 1)
     return around.reshape(2, 64, rows.shape[-1])
 
 
@@ -237,7 +240,7 @@
     rows = jnp.dot(select, down_weight, preferred_element_type=F32).astype(BF16)
 
     acts = to_all(acts, "z").reshape(128, tokens)
-    near = gather_rows(rows.reshape(2, share, columns))
+    near = gather_rows(rows.reshape(2, share, columns), acts)
     acts = spread_acts(acts).reshape(4, 2, 8, 2, share, tokens)
     acts = acts.transpose(3, 2, 0, 1, 4, 5).reshape(2, panel, tokens)
     pieces = ring_z(near)

time: 124 us -> 124 us (level)
  transfers between devices with their start and end apart: 25 -> 25, of which waited for: 13 -> 13; matrix products, arithmetic and copies ran while one was open for 7% -> 6% of each run, Pallas kernels for 3% -> 1%
where the time goes in v7:
time: 124 us; the launch traced here: 122 us
  waiting for transfers between devices  61 us (49%)
  starting transfers between devices  38.1 us (31%)
  Pallas kernels  8.93 us (7%)
  local copies, waits for them, and re-layouts  6.59 us (5%)
  matrix products  3.28 us (3%)
  other arithmetic  3.03 us (2%)
    ppermute x24, waiting for transfers between devices, shift(): return lax.ppermute(x, axis, [(i, (i + by) % n) for i in range(n)])  57.6 us
    ppermute x24, starting transfers between devices, shift(): return lax.ppermute(x, axis, [(i, (i + by) % n) for i in range(n)])  29.7 us
    all_to_all x1, starting transfers between devices, to_all(): lax.all_to_all(jnp.broadcast_to(x, (n, *x.shape)), axes, split_axis=0, co...  8.47 us
    pallas_call x1, Pallas kernels, compute(): pl.pallas_call(tail_kernel, out_shape=(jax.ShapeDtypeStruct((local, colum...  5.86 us
    dynamic_update_slice x10, local copies, waits for them, and re-layouts, place(): out = lax.dynamic_update_slice(out, jnp.expand_dims(piece, dim), at)  4.49 us
    all_to_all x1, waiting for transfers between devices, to_all(): lax.all_to_all(jnp.broadcast_to(x, (n, *x.shape)), axes, split_axis=0, co...  3.45 us
  transfers between devices with their start and end apart: 25, of which 13 were waited for; matrix products, arithmetic and copies ran while one was open for 6% of the time, Pallas kernels for 1%

profile of v7, /device:TPU:8, one launch (start us, length us, event | category | flops | bytes accessed | tf_op | source)
XLA Modules:
  0.0 122.1 jit_solution(8388030724286038762)
XLA Ops:
  1.6 2.3 %convolution_convert_fusion.1 = bf16[16,1024]{1,0:T(8,128)(2,1)S(1)} fusion(s32[16]{0:T(128)S(1)} %sub.26.mine_ref, f32[1024]{0:T(1024)S(1)} %fusion.9, bf16[1024,2,448]{0,2,1:T(8,128)(2,1)} %param.5), kind=kOutput, calls=%fused_computation.9 | convolution fusion | flops 18832384 | bytes 1871936 | tf_op jit(solution)/shard_map/dot_general | solution.py:238
  4.5 1.0 bitcast_dynamic-update-slice_fusion.9
  5.5 3.0 %collective-permute-start.12 = (bf16[2,8,2048]{2,1,0:T(8,128)(2,1)S(1)}, bf16[2,8,2048]{2,1,0:T(8,128)(2,1)S(1)}, u32[]{:S(2)}, u32[]{:S(2)}) collective-permute-start(bf16[2,8,2048]{2,1,0:T(8,128)(2,1)S(1)} %bitcast.75), channel_id=1, source_target_pairs={{0,4},{4,0},{1,5},{5,1},{2,6},{6,2},{3,7},{7,3},{8,12},{12,8},{9,1... | collective-permute-start | bytes 196616 | tf_op jit(solution)/shard_map/ppermute | solution.py:22
  9.3 8.5 %all-to-all-start = ((bf16[8,16,1024]{2,1,0:T(8,128)(2,1)}), bf16[8,16,1024]{2,1,0:T(8,128)(2,1)S(1)}, u32[]{:S(2)}, u32[]{:S(2)}) async-start(bf16[8,16,1024]{2,1,0:T(8,128)(2,1)} %broadcast_in_dim.55), calls=%async_computation | async-start | bytes 524288 | tf_op jit(solution)/shard_map/all_to_all | solution.py:27
  17.7 2.1 %fusion.14.hidden_ref = bf16[448,1024]{1,0:T(8,128)(2,1)S(1)} fusion(f32[1024]{0:T(1024)S(1)} %fusion.9, bf16[1024,2,448]{0,2,1:T(8,128)(2,1)} %param.5), kind=kLoop, calls=%fused_computation.31 | loop fusion | flops 4128768 | bytes 2756608 | tf_op jit(solution)/shard_map/transpose | solution.py:269
  20.6 2.3 %collective-permute-start.15 = (bf16[2,2,8,2048]{3,2,1,0:T(8,128)(2,1)}, bf16[2,2,8,2048]{3,2,1,0:T(8,128)(2,1)}, u32[]{:S(2)}, u32[]{:S(2)}) collective-permute-start(bf16[2,2,8,2048]{3,2,1,0:T(8,128)(2,1)} %bitcast_dynamic-update-slice_fusion.10), channel_id=1, source_target_pairs={{0,16},{8,24},{16,0},{24,8},{1,17},{9,25},{17,1},{25,9},{2,18},{10... | collective-permute-start | bytes 393224 | tf_op jit(solution)/shard_map/ppermute | solution.py:22
  22.9 1.3 %collective-permute-start.14 = (bf16[2,2,8,2048]{3,2,1,0:T(8,128)(2,1)}, bf16[2,2,8,2048]{3,2,1,0:T(8,128)(2,1)}, u32[]{:S(2)}, u32[]{:S(2)}) collective-permute-start(bf16[2,2,8,2048]{3,2,1,0:T(8,128)(2,1)} %bitcast_dynamic-update-slice_fusion.10), channel_id=1, source_target_pairs={{0,24},{8,0},{16,8},{24,16},{1,25},{9,1},{17,9},{25,17},{2,26},{10... | collective-permute-start | bytes 393224 | tf_op jit(solution)/shard_map/ppermute | solution.py:22
  24.9 0.9 bitcast_dynamic-update-slice_fusion.7
  25.9 3.4 %all-to-all-done = bf16[8,16,1024]{2,1,0:T(8,128)(2,1)S(1)} async-done(((bf16[8,16,1024]{2,1,0:T(8,128)(2,1)}), bf16[8,16,1024]{2,1,0:T(8,128)(2,1)S(1)}, u32[]{:S(2)}, u32[]{:S(2)}) %all-to-all-start) | async-done | bytes 262176 | tf_op jit(solution)/shard_map/all_to_all | solution.py:27
  31.1 6.1 %collective-permute-done = bf16[128,1024]{1,0:T(8,128)(2,1)S(1)} collective-permute-done((bf16[128,1024]{1,0:T(8,128)(2,1)S(1)}, bf16[128,1024]{1,0:T(8,128)(2,1)S(1)}, u32[]{:S(2)}, u32[]{:S(2)}) %collective-permute-start) | collective-permute-done | bytes 262176 | tf_op jit(solution)/shard_map/ppermute | solution.py:22
  37.8 1.6 %collective-permute-start.1 = (bf16[2,128,1024]{2,1,0:T(8,128)(2,1)S(1)}, bf16[2,128,1024]{2,1,0:T(8,128)(2,1)S(1)}, u32[]{:S(2)}, u32[]{:S(2)}) collective-permute-start(bf16[2,128,1024]{2,1,0:T(8,128)(2,1)S(1)} %bitcast_dynamic-update-slice_fusion.3), channel_id=1, source_target_pairs={{0,8},{8,16},{16,24},{24,0},{1,9},{9,17},{17,25},{25,1},{2,10},{10... | collective-permute-start | bytes 1572872 | tf_op jit(solution)/shard_map/ppermute | solution.py:22
  40.6 8.7 %collective-permute-done.2 = bf16[2,128,1024]{2,1,0:T(8,128)(2,1)S(1)} collective-permute-done((bf16[2,128,1024]{2,1,0:T(8,128)(2,1)S(1)}, bf16[2,128,1024]{2,1,0:T(8,128)(2,1)S(1)}, u32[]{:S(2)}, u32[]{:S(2)}) %collective-permute-start.2) | collective-permute-done | bytes 524320 | tf_op jit(solution)/shard_map/ppermute | solution.py:22
  49.5 2.1 %collective-permute-start.3 = (bf16[1,128,1024]{2,1,0:T(8,128)(2,1)S(1)}, bf16[1,128,1024]{2,1,0:T(8,128)(2,1)S(1)}, u32[]{:S(2)}, u32[]{:S(2)}) collective-permute-start(bf16[1,128,1024]{2,1,0:T(8,128)(2,1)S(1)} %slice.16), channel_id=1, source_target_pairs={{0,8},{8,16},{16,24},{24,0},{1,9},{9,17},{17,25},{25,1},{2,10},{10... | collective-permute-start | bytes 786440 | tf_op jit(solution)/shard_map/ppermute | solution.py:22
  51.6 4.1 %collective-permute-done.4 = bf16[1,128,1024]{2,1,0:T(8,128)(2,1)S(1)} collective-permute-done((bf16[1,128,1024]{2,1,0:T(8,128)(2,1)S(1)}, bf16[1,128,1024]{2,1,0:T(8,128)(2,1)S(1)}, u32[]{:S(2)}, u32[]{:S(2)}) %collective-permute-start.4) | collective-permute-done | bytes 262176 | tf_op jit(solution)/shard_map/ppermute | solution.py:22
  55.8 1.5 %collective-permute-done.3 = bf16[1,128,1024]{2,1,0:T(8,128)(2,1)S(1)} collective-permute-done((bf16[1,128,1024]{2,1,0:T(8,128)(2,1)S(1)}, bf16[1,128,1024]{2,1,0:T(8,128)(2,1)S(1)}, u32[]{:S(2)}, u32[]{:S(2)}) %collective-permute-start.3) | collective-permute-done | bytes 262176 | tf_op jit(solution)/shard_map/ppermute | solution.py:22
  57.6 2.0 %partial.1 = (f32[712,512]{1,0:T(8,128)S(1)}, bf16[712,512]{1,0:T(8,128)(2,1)S(1)}) custom-call(s32[1]{0:T(128)} %bitcast.core_ref, s32[1]{0:T(128)} %copy.29.count_ref, bf16[448,1024]{1,0:T(8,128)(2,1)S(1)} %fusion.14.hidden_ref, bf16[2,512,1024]{2,1,0:T(8,128)(2,1)S(1)} %bitcast.68), custom_call_target="tpu_custom_call" | custom-call | tf_op jit(solution)/shard_map/partial/pallas_call | solution.py:259
  60.8 2.0 %collective-permute-start.16 = (bf16[2,64,2048]{2,1,0:T(8,128)(2,1)S(1)}, bf16[2,64,2048]{2,1,0:T(8,128)(2,1)S(1)}, u32[]{:S(2)}, u32[]{:S(2)}) collective-permute-start(bf16[2,64,2048]{2,1,0:T(8,128)(2,1)S(1)} %bitcast.70), channel_id=1, source_target_pairs={{0,32},{32,64},{64,96},{96,128},{128,160},{160,192},{192,224},{224... | collective-permute-start | bytes 1572872 | tf_op jit(solution)/shard_map/ppermute | solution.py:22
  62.7 12.3 %collective-permute-done.17.refs_2_ = bf16[2,64,2048]{2,1,0:T(8,128)(2,1)S(1)} collective-permute-done((bf16[2,64,2048]{2,1,0:T(8,128)(2,1)S(1)}, bf16[2,64,2048]{2,1,0:T(8,128)(2,1)S(1)}, u32[]{:S(2)}, u32[]{:S(2)}) %collective-permute-start.17) | collective-permute-done | bytes 524320 | tf_op jit(solution)/shard_map/ppermute | solution.py:22
  75.0 1.5 %collective-permute-start.19 = (bf16[2,64,2048]{2,1,0:T(8,128)(2,1)S(1)}, bf16[2,64,2048]{2,1,0:T(8,128)(2,1)S(1)}, u32[]{:S(2)}, u32[]{:S(2)}) collective-permute-start(bf16[2,64,2048]{2,1,0:T(8,128)(2,1)S(1)} %collective-permute-done.17.refs_2_), channel_id=1, source_target_pairs={{0,224},{32,0},{64,32},{96,64},{128,96},{160,128},{192,160},{224,1... | collective-permute-start | bytes 1572872 | tf_op jit(solution)/shard_map/ppermute | solution.py:22
  77.9 1.4 %collective-permute-start.7 = (bf16[72,512]{1,0:T(8,128)(2,1)S(1)}, bf16[72,512]{1,0:T(8,128)(2,1)S(1)}, u32[]{:S(2)}, u32[]{:S(2)}) collective-permute-start(bf16[72,512]{1,0:T(8,128)(2,1)S(1)} %get-tuple-element.30), channel_id=1, source_target_pairs={{0,2},{2,0},{1,3},{3,1},{4,6},{6,4},{5,7},{7,5},{8,10},{10,8},{9,1... | collective-permute-start | bytes 221192 | tf_op jit(solution)/shard_map/ppermute | solution.py:22
  79.3 11.1 %collective-permute-done.7.given_ref = bf16[72,512]{1,0:T(8,128)(2,1)S(1)} collective-permute-done((bf16[72,512]{1,0:T(8,128)(2,1)S(1)}, bf16[72,512]{1,0:T(8,128)(2,1)S(1)}, u32[]{:S(2)}, u32[]{:S(2)}) %collective-permute-start.7) | collective-permute-done | bytes 73760 | tf_op jit(solution)/shard_map/ppermute | solution.py:22
  90.4 2.0 %collective-permute-start.10 = (bf16[64,512]{1,0:T(8,128)(2,1)S(1)}, bf16[64,512]{1,0:T(8,128)(2,1)S(1)}, u32[]{:S(2)}, u32[]{:S(2)}) collective-permute-start(bf16[64,512]{1,0:T(8,128)(2,1)S(1)} %get-tuple-element.32.refs_0_), channel_id=1, source_target_pairs={{0,16},{8,24},{16,0},{24,8},{1,17},{9,25},{17,1},{25,9},{2,18},{10... | collective-permute-start | bytes 196616 | tf_op jit(solution)/shard_map/ppermute | solution.py:22
  92.5 3.0 %collective-permute-start.21 = (bf16[2,64,2048]{2,1,0:T(8,128)(2,1)S(1)}, bf16[2,64,2048]{2,1,0:T(8,128)(2,1)S(1)}, u32[]{:S(2)}, u32[]{:S(2)}) collective-permute-start(bf16[2,64,2048]{2,1,0:T(8,128)(2,1)S(1)} %collective-permute-done.19.refs_4_), channel_id=1, source_target_pairs={{0,224},{32,0},{64,32},{96,64},{128,96},{160,128},{192,160},{224,1... | collective-permute-start | bytes 1572872 | tf_op jit(solution)/shard_map/ppermute | solution.py:22
  95.4 1.4 %collective-permute-start.9 = (bf16[64,512]{1,0:T(8,128)(2,1)S(1)}, bf16[64,512]{1,0:T(8,128)(2,1)S(1)}, u32[]{:S(2)}, u32[]{:S(2)}) collective-permute-start(bf16[64,512]{1,0:T(8,128)(2,1)S(1)} %get-tuple-element.32.refs_0_), channel_id=1, source_target_pairs={{0,24},{8,0},{16,8},{24,16},{1,25},{9,1},{17,9},{25,17},{2,26},{10... | collective-permute-start | bytes 196616 | tf_op jit(solution)/shard_map/ppermute | solution.py:22
  96.8 1.5 %collective-permute-start.8 = (bf16[64,512]{1,0:T(8,128)(2,1)S(1)}, bf16[64,512]{1,0:T(8,128)(2,1)S(1)}, u32[]{:S(2)}, u32[]{:S(2)}) collective-permute-start(bf16[64,512]{1,0:T(8,128)(2,1)S(1)} %get-tuple-element.32.refs_0_), channel_id=1, source_target_pairs={{0,8},{8,16},{16,24},{24,0},{1,9},{9,17},{17,25},{25,1},{2,10},{10... | collective-permute-start | bytes 196616 | tf_op jit(solution)/shard_map/ppermute | solution.py:22
  98.3 2.1 %collective-permute-done.9.refs_2_ = bf16[64,512]{1,0:T(8,128)(2,1)S(1)} collective-permute-done((bf16[64,512]{1,0:T(8,128)(2,1)S(1)}, bf16[64,512]{1,0:T(8,128)(2,1)S(1)}, u32[]{:S(2)}, u32[]{:S(2)}) %collective-permute-start.9) | collective-permute-done | bytes 65568 | tf_op jit(solution)/shard_map/ppermute | solution.py:22
  100.4 1.3 %collective-permute-done.8.refs_1_ = bf16[64,512]{1,0:T(8,128)(2,1)S(1)} collective-permute-done((bf16[64,512]{1,0:T(8,128)(2,1)S(1)}, bf16[64,512]{1,0:T(8,128)(2,1)S(1)}, u32[]{:S(2)}, u32[]{:S(2)}) %collective-permute-start.8) | collective-permute-done | bytes 65568 | tf_op jit(solution)/shard_map/ppermute | solution.py:22
  102.0 3.0 %collective-permute-done.21.refs_6_.behind_ref = bf16[2,64,2048]{2,1,0:T(8,128)(2,1)S(1)} collective-permute-done((bf16[2,64,2048]{2,1,0:T(8,128)(2,1)S(1)}, bf16[2,64,2048]{2,1,0:T(8,128)(2,1)S(1)}, u32[]{:S(2)}, u32[]{:S(2)}) %collective-permute-start.21) | collective-permute-done | bytes 524320 | tf_op jit(solution)/shard_map/ppermute | solution.py:22
  105.0 3.4 %collective-permute-done.20.refs_5_.ahead_ref = bf16[2,64,2048]{2,1,0:T(8,128)(2,1)S(1)} collective-permute-done((bf16[2,64,2048]{2,1,0:T(8,128)(2,1)S(1)}, bf16[2,64,2048]{2,1,0:T(8,128)(2,1)S(1)}, u32[]{:S(2)}, u32[]{:S(2)}) %collective-permute-start.20) | collective-permute-done | bytes 524320 | tf_op jit(solution)/shard_map/ppermute | solution.py:22
  108.5 3.2 %collective-permute-start.23 = (bf16[1,64,2048]{2,1,0:T(8,128)(2,1)S(1)}, bf16[1,64,2048]{2,1,0:T(8,128)(2,1)S(1)}, u32[]{:S(2)}, u32[]{:S(2)}) collective-permute-start(bf16[1,64,2048]{2,1,0:T(8,128)(2,1)S(1)} %get-tuple-element.41), channel_id=1, source_target_pairs={{0,224},{32,0},{64,32},{96,64},{128,96},{160,128},{192,160},{224,1... | collective-permute-start | bytes 786440 | tf_op jit(solution)/shard_map/ppermute | solution.py:22
  112.6 3.5 %collective-permute-done.22.ahead_ref = bf16[1,64,2048]{2,1,0:T(8,128)(2,1)S(1)} collective-permute-done((bf16[1,64,2048]{2,1,0:T(8,128)(2,1)S(1)}, bf16[1,64,2048]{2,1,0:T(8,128)(2,1)S(1)}, u32[]{:S(2)}, u32[]{:S(2)}) %collective-permute-start.22) | collective-permute-done | bytes 262176 | tf_op jit(solution)/shard_map/ppermute | solution.py:22
  116.1 5.9 %tail.1 = (bf16[448,2048]{1,0:T(8,128)(2,1)}, bf16[2,512,2048]{2,1,0:T(8,128)(2,1)S(1)}) custom-call(s32[2]{0:T(128)S(1)} %pad_add_fusion.at_ref, s32[16]{0:T(128)S(1)} %sub.26.mine_ref, bf16[704,512]{1,0:T(8,128)(2,1)S(1)} %join.1.keep_ref, bf16[704,512]{1,0:T(8,128)(2,1)S(1)} %collective-permute-done.11.given_ref, ...), custom_call_target="tpu_custom_call", output_to_operand_aliasing={{1}: (7, {})} | custom-call | tf_op jit(solution)/shard_map/tail/pallas_call | solution.py:316
  (57 shorter events, 11.4 us)
Async XLA Ops:
  1.6 3.0 %copy-start = (bf16[448,2048]{1,0:T(8,128)(2,1)S(1)}, bf16[448,2048]{1,0:T(8,128)(2,1)}, u32[]{:S(2)}) copy-start(bf16[448,2048]{1,0:T(8,128)(2,1)} %old_ref.1) | copy-start | bytes 5505028
  5.5 14.4 %collective-permute-start.12 = (bf16[2,8,2048]{2,1,0:T(8,128)(2,1)S(1)}, bf16[2,8,2048]{2,1,0:T(8,128)(2,1)S(1)}, u32[]{:S(2)}, u32[]{:S(2)}) collective-permute-start(bf16[2,8,2048]{2,1,0:T(8,128)(2,1)S(1)} %bitcast.75), channel_id=1, source_target_pairs={{0,4},{4,0},{1,5},{5,1},{2,6},{6,2},{3,7},{7,3},{8,12},{12,8},{9,1... | collective-permute-start | bytes 196616 | tf_op jit(solution)/shard_map/ppermute | solution.py:22
  9.3 20.1 %all-to-all-start = ((bf16[8,16,1024]{2,1,0:T(8,128)(2,1)}), bf16[8,16,1024]{2,1,0:T(8,128)(2,1)S(1)}, u32[]{:S(2)}, u32[]{:S(2)}) async-start(bf16[8,16,1024]{2,1,0:T(8,128)(2,1)} %broadcast_in_dim.55), calls=%async_computation | async-start | bytes 524288 | tf_op jit(solution)/shard_map/all_to_all | solution.py:27
  20.6 9.3 %collective-permute-start.15 = (bf16[2,2,8,2048]{3,2,1,0:T(8,128)(2,1)}, bf16[2,2,8,2048]{3,2,1,0:T(8,128)(2,1)}, u32[]{:S(2)}, u32[]{:S(2)}) collective-permute-start(bf16[2,2,8,2048]{3,2,1,0:T(8,128)(2,1)} %bitcast_dynamic-update-slice_fusion.10), channel_id=1, source_target_pairs={{0,16},{8,24},{16,0},{24,8},{1,17},{9,25},{17,1},{25,9},{2,18},{10... | collective-permute-start | bytes 393224 | tf_op jit(solution)/shard_map/ppermute | solution.py:22
  22.9 7.0 %collective-permute-start.14 = (bf16[2,2,8,2048]{3,2,1,0:T(8,128)(2,1)}, bf16[2,2,8,2048]{3,2,1,0:T(8,128)(2,1)}, u32[]{:S(2)}, u32[]{:S(2)}) collective-permute-start(bf16[2,2,8,2048]{3,2,1,0:T(8,128)(2,1)} %bitcast_dynamic-update-slice_fusion.10), channel_id=1, source_target_pairs={{0,24},{8,0},{16,8},{24,16},{1,25},{9,1},{17,9},{25,17},{2,26},{10... | collective-permute-start | bytes 393224 | tf_op jit(solution)/shard_map/ppermute | solution.py:22
  24.2 5.8 %collective-permute-start.13 = (bf16[2,2,8,2048]{3,2,1,0:T(8,128)(2,1)}, bf16[2,2,8,2048]{3,2,1,0:T(8,128)(2,1)}, u32[]{:S(2)}, u32[]{:S(2)}) collective-permute-start(bf16[2,2,8,2048]{3,2,1,0:T(8,128)(2,1)} %bitcast_dynamic-update-slice_fusion.10), channel_id=1, source_target_pairs={{0,8},{8,16},{16,24},{24,0},{1,9},{9,17},{17,25},{25,1},{2,10},{10... | collective-permute-start | bytes 393224 | tf_op jit(solution)/shard_map/ppermute | solution.py:22
  29.3 7.9 %collective-permute-start = (bf16[128,1024]{1,0:T(8,128)(2,1)S(1)}, bf16[128,1024]{1,0:T(8,128)(2,1)S(1)}, u32[]{:S(2)}, u32[]{:S(2)}) collective-permute-start(bf16[128,1024]{1,0:T(8,128)(2,1)S(1)} %bitcast.73), channel_id=1, source_target_pairs={{0,4},{4,0},{1,5},{5,1},{2,6},{6,2},{3,7},{7,3},{8,12},{12,8},{9,1... | collective-permute-start | bytes 786440 | tf_op jit(solution)/shard_map/ppermute | solution.py:22
  37.2 12.1 %collective-permute-start.2 = (bf16[2,128,1024]{2,1,0:T(8,128)(2,1)S(1)}, bf16[2,128,1024]{2,1,0:T(8,128)(2,1)S(1)}, u32[]{:S(2)}, u32[]{:S(2)}) collective-permute-start(bf16[2,128,1024]{2,1,0:T(8,128)(2,1)S(1)} %bitcast_dynamic-update-slice_fusion.3), channel_id=1, source_target_pairs={{0,24},{8,0},{16,8},{24,16},{1,25},{9,1},{17,9},{25,17},{2,26},{10... | collective-permute-start | bytes 1572872 | tf_op jit(solution)/shard_map/ppermute | solution.py:22
  37.8 11.7 %collective-permute-start.1 = (bf16[2,128,1024]{2,1,0:T(8,128)(2,1)S(1)}, bf16[2,128,1024]{2,1,0:T(8,128)(2,1)S(1)}, u32[]{:S(2)}, u32[]{:S(2)}) collective-permute-start(bf16[2,128,1024]{2,1,0:T(8,128)(2,1)S(1)} %bitcast_dynamic-update-slice_fusion.3), channel_id=1, source_target_pairs={{0,8},{8,16},{16,24},{24,0},{1,9},{9,17},{17,25},{25,1},{2,10},{10... | collective-permute-start | bytes 1572872 | tf_op jit(solution)/shard_map/ppermute | solution.py:22
  49.3 6.4 %collective-permute-start.4 = (bf16[1,128,1024]{2,1,0:T(8,128)(2,1)S(1)}, bf16[1,128,1024]{2,1,0:T(8,128)(2,1)S(1)}, u32[]{:S(2)}, u32[]{:S(2)}) collective-permute-start(bf16[1,128,1024]{2,1,0:T(8,128)(2,1)S(1)} %slice.17), channel_id=1, source_target_pairs={{0,24},{8,0},{16,8},{24,16},{1,25},{9,1},{17,9},{25,17},{2,26},{10... | collective-permute-start | bytes 786440 | tf_op jit(solution)/shard_map/ppermute | solution.py:22
  49.5 7.9 %collective-permute-start.3 = (bf16[1,128,1024]{2,1,0:T(8,128)(2,1)S(1)}, bf16[1,128,1024]{2,1,0:T(8,128)(2,1)S(1)}, u32[]{:S(2)}, u32[]{:S(2)}) collective-permute-start(bf16[1,128,1024]{2,1,0:T(8,128)(2,1)S(1)} %slice.16), channel_id=1, source_target_pairs={{0,8},{8,16},{16,24},{24,0},{1,9},{9,17},{17,25},{25,1},{2,10},{10... | collective-permute-start | bytes 786440 | tf_op jit(solution)/shard_map/ppermute | solution.py:22
  59.6 17.5 %collective-permute-start.5 = (bf16[712,512]{1,0:T(8,128)(2,1)S(1)}, bf16[712,512]{1,0:T(8,128)(2,1)S(1)}, u32[]{:S(2)}, u32[]{:S(2)}) collective-permute-start(bf16[712,512]{1,0:T(8,128)(2,1)S(1)} %get-tuple-element.26), channel_id=1, source_target_pairs={{0,1},{1,0},{2,3},{3,2},{4,5},{5,4},{6,7},{7,6},{8,9},{9,8},{10,11... | collective-permute-start | bytes 2187272 | tf_op jit(solution)/shard_map/ppermute | solution.py:22
  60.6 14.4 %collective-permute-start.17 = (bf16[2,64,2048]{2,1,0:T(8,128)(2,1)S(1)}, bf16[2,64,2048]{2,1,0:T(8,128)(2,1)S(1)}, u32[]{:S(2)}, u32[]{:S(2)}) collective-permute-start(bf16[2,64,2048]{2,1,0:T(8,128)(2,1)S(1)} %bitcast.69), channel_id=1, source_target_pairs={{0,224},{32,0},{64,32},{96,64},{128,96},{160,128},{192,160},{224,1... | collective-permute-start | bytes 1572872 | tf_op jit(solution)/shard_map/ppermute | solution.py:22
  60.8 15.7 %collective-permute-start.16 = (bf16[2,64,2048]{2,1,0:T(8,128)(2,1)S(1)}, bf16[2,64,2048]{2,1,0:T(8,128)(2,1)S(1)}, u32[]{:S(2)}, u32[]{:S(2)}) collective-permute-start(bf16[2,64,2048]{2,1,0:T(8,128)(2,1)S(1)} %bitcast.70), channel_id=1, source_target_pairs={{0,32},{32,64},{64,96},{96,128},{128,160},{160,192},{192,224},{224... | collective-permute-start | bytes 1572872 | tf_op jit(solution)/shard_map/ppermute | solution.py:22
  75.0 17.5 %collective-permute-start.19 = (bf16[2,64,2048]{2,1,0:T(8,128)(2,1)S(1)}, bf16[2,64,2048]{2,1,0:T(8,128)(2,1)S(1)}, u32[]{:S(2)}, u32[]{:S(2)}) collective-permute-start(bf16[2,64,2048]{2,1,0:T(8,128)(2,1)S(1)} %collective-permute-done.17.refs_2_), channel_id=1, source_target_pairs={{0,224},{32,0},{64,32},{96,64},{128,96},{160,128},{192,160},{224,1... | collective-permute-start | bytes 1572872 | tf_op jit(solution)/shard_map/ppermute | solution.py:22
  76.5 18.9 %collective-permute-start.18 = (bf16[2,64,2048]{2,1,0:T(8,128)(2,1)S(1)}, bf16[2,64,2048]{2,1,0:T(8,128)(2,1)S(1)}, u32[]{:S(2)}, u32[]{:S(2)}) collective-permute-start(bf16[2,64,2048]{2,1,0:T(8,128)(2,1)S(1)} %collective-permute-done.16.refs_1_), channel_id=1, source_target_pairs={{0,32},{32,64},{64,96},{96,128},{128,160},{160,192},{192,224},{224... | collective-permute-start | bytes 1572872 | tf_op jit(solution)/shard_map/ppermute | solution.py:22
  77.2 34.6 %copy-start.1 = (f32[2,512,512]{2,1,0:T(8,128)S(1)}, f32[2,512,512]{2,1,0:T(8,128)}, u32[]{:S(2)}) copy-start(f32[2,512,512]{2,1,0:T(8,128)} %x_ref) | copy-start | bytes 6291460
  77.2 24.5 %collective-permute-start.6 = (bf16[448,512]{1,0:T(8,128)(2,1)S(1)}, bf16[448,512]{1,0:T(8,128)(2,1)S(1)}, u32[]{:S(2)}, u32[]{:S(2)}) collective-permute-start(bf16[448,512]{1,0:T(8,128)(2,1)S(1)} %get-tuple-element.28), channel_id=1, source_target_pairs={{0,2},{2,0},{1,3},{3,1},{4,6},{6,4},{5,7},{7,5},{8,10},{10,8},{9,1... | collective-permute-start | bytes 1376264 | tf_op jit(solution)/shard_map/ppermute | solution.py:22
  77.9 12.5 %collective-permute-start.7 = (bf16[72,512]{1,0:T(8,128)(2,1)S(1)}, bf16[72,512]{1,0:T(8,128)(2,1)S(1)}, u32[]{:S(2)}, u32[]{:S(2)}) collective-permute-start(bf16[72,512]{1,0:T(8,128)(2,1)S(1)} %get-tuple-element.30), channel_id=1, source_target_pairs={{0,2},{2,0},{1,3},{3,1},{4,6},{6,4},{5,7},{7,5},{8,10},{10,8},{9,1... | collective-permute-start | bytes 221192 | tf_op jit(solution)/shard_map/ppermute | solution.py:22
  90.4 6.4 %collective-permute-start.10 = (bf16[64,512]{1,0:T(8,128)(2,1)S(1)}, bf16[64,512]{1,0:T(8,128)(2,1)S(1)}, u32[]{:S(2)}, u32[]{:S(2)}) collective-permute-start(bf16[64,512]{1,0:T(8,128)(2,1)S(1)} %get-tuple-element.32.refs_0_), channel_id=1, source_target_pairs={{0,16},{8,24},{16,0},{24,8},{1,17},{9,25},{17,1},{25,9},{2,18},{10... | collective-permute-start | bytes 196616 | tf_op jit(solution)/shard_map/ppermute | solution.py:22
  92.5 12.5 %collective-permute-start.21 = (bf16[2,64,2048]{2,1,0:T(8,128)(2,1)S(1)}, bf16[2,64,2048]{2,1,0:T(8,128)(2,1)S(1)}, u32[]{:S(2)}, u32[]{:S(2)}) collective-permute-start(bf16[2,64,2048]{2,1,0:T(8,128)(2,1)S(1)} %collective-permute-done.19.refs_4_), channel_id=1, source_target_pairs={{0,224},{32,0},{64,32},{96,64},{128,96},{160,128},{192,160},{224,1... | collective-permute-start | bytes 1572872 | tf_op jit(solution)/shard_map/ppermute | solution.py:22
  95.4 13.0 %collective-permute-start.20 = (bf16[2,64,2048]{2,1,0:T(8,128)(2,1)S(1)}, bf16[2,64,2048]{2,1,0:T(8,128)(2,1)S(1)}, u32[]{:S(2)}, u32[]{:S(2)}) collective-permute-start(bf16[2,64,2048]{2,1,0:T(8,128)(2,1)S(1)} %collective-permute-done.18.refs_3_), channel_id=1, source_target_pairs={{0,32},{32,64},{64,96},{96,128},{128,160},{160,192},{192,224},{224... | collective-permute-start | bytes 1572872 | tf_op jit(solution)/shard_map/ppermute | solution.py:22
  95.4 5.0 %collective-permute-start.9 = (bf16[64,512]{1,0:T(8,128)(2,1)S(1)}, bf16[64,512]{1,0:T(8,128)(2,1)S(1)}, u32[]{:S(2)}, u32[]{:S(2)}) collective-permute-start(bf16[64,512]{1,0:T(8,128)(2,1)S(1)} %get-tuple-element.32.refs_0_), channel_id=1, source_target_pairs={{0,24},{8,0},{16,8},{24,16},{1,25},{9,1},{17,9},{25,17},{2,26},{10... | collective-permute-start | bytes 196616 | tf_op jit(solution)/shard_map/ppermute | solution.py:22
  96.8 5.0 %collective-permute-start.8 = (bf16[64,512]{1,0:T(8,128)(2,1)S(1)}, bf16[64,512]{1,0:T(8,128)(2,1)S(1)}, u32[]{:S(2)}, u32[]{:S(2)}) collective-permute-start(bf16[64,512]{1,0:T(8,128)(2,1)S(1)} %get-tuple-element.32.refs_0_), channel_id=1, source_target_pairs={{0,8},{8,16},{16,24},{24,0},{1,9},{9,17},{17,25},{25,1},{2,10},{10... | collective-permute-start | bytes 196616 | tf_op jit(solution)/shard_map/ppermute | solution.py:22
  101.9 14.2 %collective-permute-start.11 = (bf16[704,512]{1,0:T(8,128)(2,1)S(1)}, bf16[704,512]{1,0:T(8,128)(2,1)S(1)}, u32[]{:S(2)}, u32[]{:S(2)}) collective-permute-start(bf16[704,512]{1,0:T(8,128)(2,1)S(1)} %join.1.keep_ref), channel_id=1, source_target_pairs={{0,1},{1,0},{2,3},{3,2},{4,5},{5,4},{6,7},{7,6},{8,9},{9,8},{10,11... | collective-permute-start | bytes 2162696 | tf_op jit(solution)/shard_map/ppermute | solution.py:22
  108.4 7.7 %collective-permute-start.22 = (bf16[1,64,2048]{2,1,0:T(8,128)(2,1)S(1)}, bf16[1,64,2048]{2,1,0:T(8,128)(2,1)S(1)}, u32[]{:S(2)}, u32[]{:S(2)}) collective-permute-start(bf16[1,64,2048]{2,1,0:T(8,128)(2,1)S(1)} %get-tuple-element.40), channel_id=1, source_target_pairs={{0,32},{32,64},{64,96},{96,128},{128,160},{160,192},{192,224},{224... | collective-permute-start | bytes 786440 | tf_op jit(solution)/shard_map/ppermute | solution.py:22
  108.5 7.6 %collective-permute-start.23 = (bf16[1,64,2048]{2,1,0:T(8,128)(2,1)S(1)}, bf16[1,64,2048]{2,1,0:T(8,128)(2,1)S(1)}, u32[]{:S(2)}, u32[]{:S(2)}) collective-permute-start(bf16[1,64,2048]{2,1,0:T(8,128)(2,1)S(1)} %get-tuple-element.41), channel_id=1, source_target_pairs={{0,224},{32,0},{64,32},{96,64},{128,96},{160,128},{192,160},{224,1... | collective-permute-start | bytes 786440 | tf_op jit(solution)/shard_map/ppermute | solution.py:22

commit v8 on v7

--- a/solution.py
+++ b/solution.py
@@ -51,12 +51,19 @@
 
 
 def spread_acts(block):
-    other = shift(block, "xh", 1)
-    block = place([(0, block), (1, other)], "xh", 0)
-    ahead, behind = shift(block, "y", 1), shift(block, "y", -1)
+    half = block.shape[1] // 2
+    one, two = block[:, :half], block[:, half:]
+    other = shift(one, "xh", 1)
+    others = [(k, shift(two, "y", k)) for k in (1, 3, 2)]
+    one = place([(0, one), (1, other)], "xh", 0)
+    ahead, behind = shift(one, "y", 1), shift(one, "y", -1)
+    two = place([(0, two)] + others, "y", 0)
+    other = shift(two, "xh", 1)
     left, right = shift(ahead[:1], "y", 1), shift(behind[1:], "y", -1)
     far_block = jnp.concatenate([left, right], axis=0)
-    return place([(0, block), (1, ahead), (3, behind), (2, far_block)], "y", 0)
+    one = place([(0, one), (1, ahead), (3, behind), (2, far_block)], "y", 0)
+    two = place([(0, two), (1, other)], "xh", 1)
+    return jnp.concatenate([one, two], axis=-1)
 
 
 def halve_kernel(ahead_ref, behind_ref, first_ref, second_ref, sems):

time: 124 us -> 121 us (0.976)
  waiting for transfers between devices: 61 us -> 52.3 us
  starting transfers between devices: 38.1 us -> 44.3 us
    ppermute x24 -> x28, waiting for transfers between devices: 57.6 us -> 48.8 us  [shift(): return lax.ppermute(x, axis, [(i, (i + by) % n) for i in range(n)])]
    ppermute x24 -> x28, starting transfers between devices: 29.7 us -> 35.9 us  [shift(): return lax.ppermute(x, axis, [(i, (i + by) % n) for i in range(n)])]
    dynamic_update_slice x10 -> x15, local copies, waits for them, and re-layouts: 4.49 us -> 4.55 us  [place(): out = lax.dynamic_update_slice(out, jnp.expand_dims(piece, dim), at)]
  transfers between devices with their start and end apart: 25 -> 29, of which waited for: 13 -> 12; matrix products, arithmetic and copies ran while one was open for 6% -> 6% of each run, Pallas kernels for 1% -> 1%
where the time goes in v8:
time: 121 us; the launch traced here: 120 us
  waiting for transfers between devices  52.3 us (43%)
  starting transfers between devices  44.3 us (37%)
  Pallas kernels  8.92 us (7%)
  local copies, waits for them, and re-layouts  6.56 us (5%)
  other arithmetic  3.28 us (3%)
  matrix products  3.28 us (3%)
  between operations  1.22 us (1%)
    ppermute x28, waiting for transfers between devices, shift(): return lax.ppermute(x, axis, [(i, (i + by) % n) for i in range(n)])  48.8 us
    ppermute x28, starting transfers between devices, shift(): return lax.ppermute(x, axis, [(i, (i + by) % n) for i in range(n)])  35.9 us
    all_to_all x1, starting transfers between devices, to_all(): lax.all_to_all(jnp.broadcast_to(x, (n, *x.shape)), axes, split_axis=0, co...  8.47 us
    pallas_call x1, Pallas kernels, compute(): pl.pallas_call(tail_kernel, out_shape=(jax.ShapeDtypeStruct((local, colum...  5.85 us
    dynamic_update_slice x15, local copies, waits for them, and re-layouts, place(): out = lax.dynamic_update_slice(out, jnp.expand_dims(piece, dim), at)  4.55 us
    all_to_all x1, waiting for transfers between devices, to_all(): lax.all_to_all(jnp.broadcast_to(x, (n, *x.shape)), axes, split_axis=0, co...  3.46 us
  transfers between devices with their start and end apart: 29, of which 12 were waited for; matrix products, arithmetic and copies ran while one was open for 6% of the time, Pallas kernels for 1%

profile of v8, /device:TPU:8, one launch (start us, length us, event | category | flops | bytes accessed | tf_op | source)
XLA Modules:
  0.0 119.9 jit_solution(4341763966274648428)
XLA Ops:
  1.6 2.3 %convolution_convert_fusion.1 = bf16[16,1024]{1,0:T(8,128)(2,1)S(1)} fusion(s32[16]{0:T(128)S(1)} %sub.30.mine_ref, f32[1024]{0:T(1024)S(1)} %fusion.9, bf16[1024,2,448]{0,2,1:T(8,128)(2,1)} %param.5), kind=kOutput, calls=%fused_computation.10 | convolution fusion | flops 18832384 | bytes 1871936 | tf_op jit(solution)/shard_map/dot_general | solution.py:245
  4.5 1.0 bitcast_dynamic-update-slice_fusion.15
  5.5 3.0 %collective-permute-start.16 = (bf16[2,8,2048]{2,1,0:T(8,128)(2,1)S(1)}, bf16[2,8,2048]{2,1,0:T(8,128)(2,1)S(1)}, u32[]{:S(2)}, u32[]{:S(2)}) collective-permute-start(bf16[2,8,2048]{2,1,0:T(8,128)(2,1)S(1)} %bitcast.88), channel_id=1, source_target_pairs={{0,4},{4,0},{1,5},{5,1},{2,6},{6,2},{3,7},{7,3},{8,12},{12,8},{9,1... | collective-permute-start | bytes 196616 | tf_op jit(solution)/shard_map/ppermute | solution.py:22
  9.3 8.5 %all-to-all-start = ((bf16[8,16,1024]{2,1,0:T(8,128)(2,1)}), bf16[8,16,1024]{2,1,0:T(8,128)(2,1)S(1)}, u32[]{:S(2)}, u32[]{:S(2)}) async-start(bf16[8,16,1024]{2,1,0:T(8,128)(2,1)} %broadcast_in_dim.75), calls=%async_computation | async-start | bytes 524288 | tf_op jit(solution)/shard_map/all_to_all | solution.py:27
  17.7 2.1 %fusion.15.hidden_ref = bf16[448,1024]{1,0:T(8,128)(2,1)S(1)} fusion(f32[1024]{0:T(1024)S(1)} %fusion.9, bf16[1024,2,448]{0,2,1:T(8,128)(2,1)} %param.5), kind=kLoop, calls=%fused_computation.39 | loop fusion | flops 4128768 | bytes 2756608 | tf_op jit(solution)/shard_map/transpose | solution.py:276
  20.6 2.3 %collective-permute-start.19 = (bf16[2,2,8,2048]{3,2,1,0:T(8,128)(2,1)}, bf16[2,2,8,2048]{3,2,1,0:T(8,128)(2,1)}, u32[]{:S(2)}, u32[]{:S(2)}) collective-permute-start(bf16[2,2,8,2048]{3,2,1,0:T(8,128)(2,1)} %bitcast_dynamic-update-slice_fusion.16), channel_id=1, source_target_pairs={{0,16},{8,24},{16,0},{24,8},{1,17},{9,25},{17,1},{25,9},{2,18},{10... | collective-permute-start | bytes 393224 | tf_op jit(solution)/shard_map/ppermute | solution.py:22
  22.9 1.3 %collective-permute-start.18 = (bf16[2,2,8,2048]{3,2,1,0:T(8,128)(2,1)}, bf16[2,2,8,2048]{3,2,1,0:T(8,128)(2,1)}, u32[]{:S(2)}, u32[]{:S(2)}) collective-permute-start(bf16[2,2,8,2048]{3,2,1,0:T(8,128)(2,1)} %bitcast_dynamic-update-slice_fusion.16), channel_id=1, source_target_pairs={{0,24},{8,0},{16,8},{24,16},{1,25},{9,1},{17,9},{25,17},{2,26},{10... | collective-permute-start | bytes 393224 | tf_op jit(solution)/shard_map/ppermute | solution.py:22
  24.9 0.9 bitcast_dynamic-update-slice_fusion.7
  25.9 3.5 %all-to-all-done = bf16[8,16,1024]{2,1,0:T(8,128)(2,1)S(1)} async-done(((bf16[8,16,1024]{2,1,0:T(8,128)(2,1)}), bf16[8,16,1024]{2,1,0:T(8,128)(2,1)S(1)}, u32[]{:S(2)}, u32[]{:S(2)}) %all-to-all-start) | async-done | bytes 262176 | tf_op jit(solution)/shard_map/all_to_all | solution.py:27
  29.9 1.6 %collective-permute-start.5 = (bf16[128,512]{1,0:T(8,128)(2,1)S(1)}, bf16[128,512]{1,0:T(8,128)(2,1)S(1)}, u32[]{:S(2)}, u32[]{:S(2)}) collective-permute-start(bf16[128,512]{1,0:T(8,128)(2,1)S(1)} %get-tuple-element.44), channel_id=1, source_target_pairs={{0,8},{8,16},{16,24},{24,0},{1,9},{9,17},{17,25},{25,1},{2,10},{10... | collective-permute-start | bytes 393224 | tf_op jit(solution)/shard_map/ppermute | solution.py:22
  31.5 3.5 %collective-permute-start.7 = (bf16[128,512]{1,0:T(8,128)(2,1)S(1)}, bf16[128,512]{1,0:T(8,128)(2,1)S(1)}, u32[]{:S(2)}, u32[]{:S(2)}) collective-permute-start(bf16[128,512]{1,0:T(8,128)(2,1)S(1)} %get-tuple-element.44), channel_id=1, source_target_pairs={{0,16},{8,24},{16,0},{24,8},{1,17},{9,25},{17,1},{25,9},{2,18},{10... | collective-permute-start | bytes 393224 | tf_op jit(solution)/shard_map/ppermute | solution.py:22
  37.4 4.0 %collective-permute-done = bf16[128,512]{1,0:T(8,128)(2,1)S(1)} collective-permute-done((bf16[128,512]{1,0:T(8,128)(2,1)S(1)}, bf16[128,512]{1,0:T(8,128)(2,1)S(1)}, u32[]{:S(2)}, u32[]{:S(2)}) %collective-permute-start) | collective-permute-done | bytes 131104 | tf_op jit(solution)/shard_map/ppermute | solution.py:22
  41.7 1.9 %collective-permute-start.1 = (bf16[2,128,512]{2,1,0:T(8,128)(2,1)S(1)}, bf16[2,128,512]{2,1,0:T(8,128)(2,1)S(1)}, u32[]{:S(2)}, u32[]{:S(2)}) collective-permute-start(bf16[2,128,512]{2,1,0:T(8,128)(2,1)S(1)} %bitcast_dynamic-update-slice_fusion.13), channel_id=1, source_target_pairs={{0,8},{8,16},{16,24},{24,0},{1,9},{9,17},{17,25},{25,1},{2,10},{10... | collective-permute-start | bytes 786440 | tf_op jit(solution)/shard_map/ppermute | solution.py:22
  44.5 4.8 %collective-permute-done.2 = bf16[2,128,512]{2,1,0:T(8,128)(2,1)S(1)} collective-permute-done((bf16[2,128,512]{2,1,0:T(8,128)(2,1)S(1)}, bf16[2,128,512]{2,1,0:T(8,128)(2,1)S(1)}, u32[]{:S(2)}, u32[]{:S(2)}) %collective-permute-start.2) | collective-permute-done | bytes 262176 | tf_op jit(solution)/shard_map/ppermute | solution.py:22
  49.6 2.1 %collective-permute-start.3 = (bf16[1,128,512]{2,1,0:T(8,128)(2,1)S(1)}, bf16[1,128,512]{2,1,0:T(8,128)(2,1)S(1)}, u32[]{:S(2)}, u32[]{:S(2)}) collective-permute-start(bf16[1,128,512]{2,1,0:T(8,128)(2,1)S(1)} %slice.25), channel_id=1, source_target_pairs={{0,8},{8,16},{16,24},{24,0},{1,9},{9,17},{17,25},{25,1},{2,10},{10... | collective-permute-start | bytes 393224 | tf_op jit(solution)/shard_map/ppermute | solution.py:22
  51.8 2.6 %collective-permute-done.4 = bf16[1,128,512]{2,1,0:T(8,128)(2,1)S(1)} collective-permute-done((bf16[1,128,512]{2,1,0:T(8,128)(2,1)S(1)}, bf16[1,128,512]{2,1,0:T(8,128)(2,1)S(1)}, u32[]{:S(2)}, u32[]{:S(2)}) %collective-permute-start.4) | collective-permute-done | bytes 131104 | tf_op jit(solution)/shard_map/ppermute | solution.py:22
  55.4 2.0 %partial.1 = (f32[712,512]{1,0:T(8,128)S(1)}, bf16[712,512]{1,0:T(8,128)(2,1)S(1)}) custom-call(s32[1]{0:T(128)} %bitcast.core_ref, s32[1]{0:T(128)} %copy.37.count_ref, bf16[448,1024]{1,0:T(8,128)(2,1)S(1)} %fusion.15.hidden_ref, bf16[2,512,1024]{2,1,0:T(8,128)(2,1)S(1)} %bitcast.81), custom_call_target="tpu_custom_call" | custom-call | tf_op jit(solution)/shard_map/partial/pallas_call | solution.py:266
  58.4 1.2 %collective-permute-start.21 = (bf16[2,64,2048]{2,1,0:T(8,128)(2,1)S(1)}, bf16[2,64,2048]{2,1,0:T(8,128)(2,1)S(1)}, u32[]{:S(2)}, u32[]{:S(2)}) collective-permute-start(bf16[2,64,2048]{2,1,0:T(8,128)(2,1)S(1)} %bitcast.82), channel_id=1, source_target_pairs={{0,224},{32,0},{64,32},{96,64},{128,96},{160,128},{192,160},{224,1... | collective-permute-start | bytes 1572872 | tf_op jit(solution)/shard_map/ppermute | solution.py:22
  60.5 12.3 %collective-permute-done.21.refs_2_ = bf16[2,64,2048]{2,1,0:T(8,128)(2,1)S(1)} collective-permute-done((bf16[2,64,2048]{2,1,0:T(8,128)(2,1)S(1)}, bf16[2,64,2048]{2,1,0:T(8,128)(2,1)S(1)}, u32[]{:S(2)}, u32[]{:S(2)}) %collective-permute-start.21) | collective-permute-done | bytes 524320 | tf_op jit(solution)/shard_map/ppermute | solution.py:22
  72.8 2.3 %collective-permute-start.23 = (bf16[2,64,2048]{2,1,0:T(8,128)(2,1)S(1)}, bf16[2,64,2048]{2,1,0:T(8,128)(2,1)S(1)}, u32[]{:S(2)}, u32[]{:S(2)}) collective-permute-start(bf16[2,64,2048]{2,1,0:T(8,128)(2,1)S(1)} %collective-permute-done.21.refs_2_), channel_id=1, source_target_pairs={{0,224},{32,0},{64,32},{96,64},{128,96},{160,128},{192,160},{224,1... | collective-permute-start | bytes 1572872 | tf_op jit(solution)/shard_map/ppermute | solution.py:22
  76.0 1.4 %collective-permute-start.11 = (bf16[72,512]{1,0:T(8,128)(2,1)S(1)}, bf16[72,512]{1,0:T(8,128)(2,1)S(1)}, u32[]{:S(2)}, u32[]{:S(2)}) collective-permute-start(bf16[72,512]{1,0:T(8,128)(2,1)S(1)} %get-tuple-element.30), channel_id=1, source_target_pairs={{0,2},{2,0},{1,3},{3,1},{4,6},{6,4},{5,7},{7,5},{8,10},{10,8},{9,1... | collective-permute-start | bytes 221192 | tf_op jit(solution)/shard_map/ppermute | solution.py:22
  77.4 11.3 %collective-permute-done.11.given_ref = bf16[72,512]{1,0:T(8,128)(2,1)S(1)} collective-permute-done((bf16[72,512]{1,0:T(8,128)(2,1)S(1)}, bf16[72,512]{1,0:T(8,128)(2,1)S(1)}, u32[]{:S(2)}, u32[]{:S(2)}) %collective-permute-start.11) | collective-permute-done | bytes 73760 | tf_op jit(solution)/shard_map/ppermute | solution.py:22
  88.8 1.7 %collective-permute-start.14 = (bf16[64,512]{1,0:T(8,128)(2,1)S(1)}, bf16[64,512]{1,0:T(8,128)(2,1)S(1)}, u32[]{:S(2)}, u32[]{:S(2)}) collective-permute-start(bf16[64,512]{1,0:T(8,128)(2,1)S(1)} %get-tuple-element.32.refs_0_), channel_id=1, source_target_pairs={{0,16},{8,24},{16,0},{24,8},{1,17},{9,25},{17,1},{25,9},{2,18},{10... | collective-permute-start | bytes 196616 | tf_op jit(solution)/shard_map/ppermute | solution.py:22
  90.5 2.9 %collective-permute-start.25 = (bf16[2,64,2048]{2,1,0:T(8,128)(2,1)S(1)}, bf16[2,64,2048]{2,1,0:T(8,128)(2,1)S(1)}, u32[]{:S(2)}, u32[]{:S(2)}) collective-permute-start(bf16[2,64,2048]{2,1,0:T(8,128)(2,1)S(1)} %collective-permute-done.23.refs_4_), channel_id=1, source_target_pairs={{0,224},{32,0},{64,32},{96,64},{128,96},{160,128},{192,160},{224,1... | collective-permute-start | bytes 1572872 | tf_op jit(solution)/shard_map/ppermute | solution.py:22
  93.4 1.8 %collective-permute-start.13 = (bf16[64,512]{1,0:T(8,128)(2,1)S(1)}, bf16[64,512]{1,0:T(8,128)(2,1)S(1)}, u32[]{:S(2)}, u32[]{:S(2)}) collective-permute-start(bf16[64,512]{1,0:T(8,128)(2,1)S(1)} %get-tuple-element.32.refs_0_), channel_id=1, source_target_pairs={{0,24},{8,0},{16,8},{24,16},{1,25},{9,1},{17,9},{25,17},{2,26},{10... | collective-permute-start | bytes 196616 | tf_op jit(solution)/shard_map/ppermute | solution.py:22
  96.0 2.1 %collective-permute-done.13.refs_2_ = bf16[64,512]{1,0:T(8,128)(2,1)S(1)} collective-permute-done((bf16[64,512]{1,0:T(8,128)(2,1)S(1)}, bf16[64,512]{1,0:T(8,128)(2,1)S(1)}, u32[]{:S(2)}, u32[]{:S(2)}) %collective-permute-start.13) | collective-permute-done | bytes 65568 | tf_op jit(solution)/shard_map/ppermute | solution.py:22
  98.2 1.3 %collective-permute-done.12.refs_1_ = bf16[64,512]{1,0:T(8,128)(2,1)S(1)} collective-permute-done((bf16[64,512]{1,0:T(8,128)(2,1)S(1)}, bf16[64,512]{1,0:T(8,128)(2,1)S(1)}, u32[]{:S(2)}, u32[]{:S(2)}) %collective-permute-start.12) | collective-permute-done | bytes 65568 | tf_op jit(solution)/shard_map/ppermute | solution.py:22
  99.8 2.9 %collective-permute-done.25.refs_6_.behind_ref = bf16[2,64,2048]{2,1,0:T(8,128)(2,1)S(1)} collective-permute-done((bf16[2,64,2048]{2,1,0:T(8,128)(2,1)S(1)}, bf16[2,64,2048]{2,1,0:T(8,128)(2,1)S(1)}, u32[]{:S(2)}, u32[]{:S(2)}) %collective-permute-start.25) | collective-permute-done | bytes 524320 | tf_op jit(solution)/shard_map/ppermute | solution.py:22
  102.7 3.4 %collective-permute-done.24.refs_5_.ahead_ref = bf16[2,64,2048]{2,1,0:T(8,128)(2,1)S(1)} collective-permute-done((bf16[2,64,2048]{2,1,0:T(8,128)(2,1)S(1)}, bf16[2,64,2048]{2,1,0:T(8,128)(2,1)S(1)}, u32[]{:S(2)}, u32[]{:S(2)}) %collective-permute-start.24) | collective-permute-done | bytes 524320 | tf_op jit(solution)/shard_map/ppermute | solution.py:22
  106.3 3.2 %collective-permute-start.27 = (bf16[1,64,2048]{2,1,0:T(8,128)(2,1)S(1)}, bf16[1,64,2048]{2,1,0:T(8,128)(2,1)S(1)}, u32[]{:S(2)}, u32[]{:S(2)}) collective-permute-start(bf16[1,64,2048]{2,1,0:T(8,128)(2,1)S(1)} %get-tuple-element.41), channel_id=1, source_target_pairs={{0,224},{32,0},{64,32},{96,64},{128,96},{160,128},{192,160},{224,1... | collective-permute-start | bytes 786440 | tf_op jit(solution)/shard_map/ppermute | solution.py:22
  110.3 3.5 %collective-permute-done.26.ahead_ref = bf16[1,64,2048]{2,1,0:T(8,128)(2,1)S(1)} collective-permute-done((bf16[1,64,2048]{2,1,0:T(8,128)(2,1)S(1)}, bf16[1,64,2048]{2,1,0:T(8,128)(2,1)S(1)}, u32[]{:S(2)}, u32[]{:S(2)}) %collective-permute-start.26) | collective-permute-done | bytes 262176 | tf_op jit(solution)/shard_map/ppermute | solution.py:22
  113.9 5.9 %tail.1 = (bf16[448,2048]{1,0:T(8,128)(2,1)}, bf16[2,512,2048]{2,1,0:T(8,128)(2,1)S(1)}) custom-call(s32[2]{0:T(128)S(1)} %pad_add_fusion.at_ref, s32[16]{0:T(128)S(1)} %sub.30.mine_ref, bf16[704,512]{1,0:T(8,128)(2,1)S(1)} %join.1.keep_ref, bf16[704,512]{1,0:T(8,128)(2,1)S(1)} %collective-permute-done.15.given_ref, ...), custom_call_target="tpu_custom_call", output_to_operand_aliasing={{1}: (7, {})} | custom-call | tf_op jit(solution)/shard_map/tail/pallas_call | solution.py:323
  (74 shorter events, 13.8 us)
Async XLA Ops:
  1.6 3.0 %copy-start = (bf16[448,2048]{1,0:T(8,128)(2,1)S(1)}, bf16[448,2048]{1,0:T(8,128)(2,1)}, u32[]{:S(2)}) copy-start(bf16[448,2048]{1,0:T(8,128)(2,1)} %old_ref.1) | copy-start | bytes 5505028
  5.5 14.4 %collective-permute-start.16 = (bf16[2,8,2048]{2,1,0:T(8,128)(2,1)S(1)}, bf16[2,8,2048]{2,1,0:T(8,128)(2,1)S(1)}, u32[]{:S(2)}, u32[]{:S(2)}) collective-permute-start(bf16[2,8,2048]{2,1,0:T(8,128)(2,1)S(1)} %bitcast.88), channel_id=1, source_target_pairs={{0,4},{4,0},{1,5},{5,1},{2,6},{6,2},{3,7},{7,3},{8,12},{12,8},{9,1... | collective-permute-start | bytes 196616 | tf_op jit(solution)/shard_map/ppermute | solution.py:22
  9.3 20.1 %all-to-all-start = ((bf16[8,16,1024]{2,1,0:T(8,128)(2,1)}), bf16[8,16,1024]{2,1,0:T(8,128)(2,1)S(1)}, u32[]{:S(2)}, u32[]{:S(2)}) async-start(bf16[8,16,1024]{2,1,0:T(8,128)(2,1)} %broadcast_in_dim.75), calls=%async_computation | async-start | bytes 524288 | tf_op jit(solution)/shard_map/all_to_all | solution.py:27
  20.6 10.9 %collective-permute-start.19 = (bf16[2,2,8,2048]{3,2,1,0:T(8,128)(2,1)}, bf16[2,2,8,2048]{3,2,1,0:T(8,128)(2,1)}, u32[]{:S(2)}, u32[]{:S(2)}) collective-permute-start(bf16[2,2,8,2048]{3,2,1,0:T(8,128)(2,1)} %bitcast_dynamic-update-slice_fusion.16), channel_id=1, source_target_pairs={{0,16},{8,24},{16,0},{24,8},{1,17},{9,25},{17,1},{25,9},{2,18},{10... | collective-permute-start | bytes 393224 | tf_op jit(solution)/shard_map/ppermute | solution.py:22
  22.9 12.1 %collective-permute-start.18 = (bf16[2,2,8,2048]{3,2,1,0:T(8,128)(2,1)}, bf16[2,2,8,2048]{3,2,1,0:T(8,128)(2,1)}, u32[]{:S(2)}, u32[]{:S(2)}) collective-permute-start(bf16[2,2,8,2048]{3,2,1,0:T(8,128)(2,1)} %bitcast_dynamic-update-slice_fusion.16), channel_id=1, source_target_pairs={{0,24},{8,0},{16,8},{24,16},{1,25},{9,1},{17,9},{25,17},{2,26},{10... | collective-permute-start | bytes 393224 | tf_op jit(solution)/shard_map/ppermute | solution.py:22
  24.2 10.8 %collective-permute-start.17 = (bf16[2,2,8,2048]{3,2,1,0:T(8,128)(2,1)}, bf16[2,2,8,2048]{3,2,1,0:T(8,128)(2,1)}, u32[]{:S(2)}, u32[]{:S(2)}) collective-permute-start(bf16[2,2,8,2048]{3,2,1,0:T(8,128)(2,1)} %bitcast_dynamic-update-slice_fusion.16), channel_id=1, source_target_pairs={{0,8},{8,16},{16,24},{24,0},{1,9},{9,17},{17,25},{25,1},{2,10},{10... | collective-permute-start | bytes 393224 | tf_op jit(solution)/shard_map/ppermute | solution.py:22
  29.4 14.2 %collective-permute-start.6 = (bf16[128,512]{1,0:T(8,128)(2,1)S(1)}, bf16[128,512]{1,0:T(8,128)(2,1)S(1)}, u32[]{:S(2)}, u32[]{:S(2)}) collective-permute-start(bf16[128,512]{1,0:T(8,128)(2,1)S(1)} %get-tuple-element.44), channel_id=1, source_target_pairs={{0,24},{8,0},{16,8},{24,16},{1,25},{9,1},{17,9},{25,17},{2,26},{10... | collective-permute-start | bytes 393224 | tf_op jit(solution)/shard_map/ppermute | solution.py:22
  29.9 13.7 %collective-permute-start.5 = (bf16[128,512]{1,0:T(8,128)(2,1)S(1)}, bf16[128,512]{1,0:T(8,128)(2,1)S(1)}, u32[]{:S(2)}, u32[]{:S(2)}) collective-permute-start(bf16[128,512]{1,0:T(8,128)(2,1)S(1)} %get-tuple-element.44), channel_id=1, source_target_pairs={{0,8},{8,16},{16,24},{24,0},{1,9},{9,17},{17,25},{25,1},{2,10},{10... | collective-permute-start | bytes 393224 | tf_op jit(solution)/shard_map/ppermute | solution.py:22
  31.5 12.2 %collective-permute-start.7 = (bf16[128,512]{1,0:T(8,128)(2,1)S(1)}, bf16[128,512]{1,0:T(8,128)(2,1)S(1)}, u32[]{:S(2)}, u32[]{:S(2)}) collective-permute-start(bf16[128,512]{1,0:T(8,128)(2,1)S(1)} %get-tuple-element.44), channel_id=1, source_target_pairs={{0,16},{8,24},{16,0},{24,8},{1,17},{9,25},{17,1},{25,9},{2,18},{10... | collective-permute-start | bytes 393224 | tf_op jit(solution)/shard_map/ppermute | solution.py:22
  35.0 6.5 %collective-permute-start = (bf16[128,512]{1,0:T(8,128)(2,1)S(1)}, bf16[128,512]{1,0:T(8,128)(2,1)S(1)}, u32[]{:S(2)}, u32[]{:S(2)}) collective-permute-start(bf16[128,512]{1,0:T(8,128)(2,1)S(1)} %get-tuple-element.43), channel_id=1, source_target_pairs={{0,4},{4,0},{1,5},{5,1},{2,6},{6,2},{3,7},{7,3},{8,12},{12,8},{9,1... | collective-permute-start | bytes 393224 | tf_op jit(solution)/shard_map/ppermute | solution.py:22
  41.5 7.9 %collective-permute-start.2 = (bf16[2,128,512]{2,1,0:T(8,128)(2,1)S(1)}, bf16[2,128,512]{2,1,0:T(8,128)(2,1)S(1)}, u32[]{:S(2)}, u32[]{:S(2)}) collective-permute-start(bf16[2,128,512]{2,1,0:T(8,128)(2,1)S(1)} %bitcast_dynamic-update-slice_fusion.13), channel_id=1, source_target_pairs={{0,24},{8,0},{16,8},{24,16},{1,25},{9,1},{17,9},{25,17},{2,26},{10... | collective-permute-start | bytes 786440 | tf_op jit(solution)/shard_map/ppermute | solution.py:22
  41.7 7.9 %collective-permute-start.1 = (bf16[2,128,512]{2,1,0:T(8,128)(2,1)S(1)}, bf16[2,128,512]{2,1,0:T(8,128)(2,1)S(1)}, u32[]{:S(2)}, u32[]{:S(2)}) collective-permute-start(bf16[2,128,512]{2,1,0:T(8,128)(2,1)S(1)} %bitcast_dynamic-update-slice_fusion.13), channel_id=1, source_target_pairs={{0,8},{8,16},{16,24},{24,0},{1,9},{9,17},{17,25},{25,1},{2,10},{10... | collective-permute-start | bytes 786440 | tf_op jit(solution)/shard_map/ppermute | solution.py:22
  43.7 11.2 %collective-permute-start.8 = (bf16[4,128,512]{2,1,0:T(8,128)(2,1)S(1)}, bf16[4,128,512]{2,1,0:T(8,128)(2,1)S(1)}, u32[]{:S(2)}, u32[]{:S(2)}) collective-permute-start(bf16[4,128,512]{2,1,0:T(8,128)(2,1)S(1)} %bitcast_dynamic-update-slice_fusion.9), channel_id=1, source_target_pairs={{0,4},{4,0},{1,5},{5,1},{2,6},{6,2},{3,7},{7,3},{8,12},{12,8},{9,1... | collective-permute-start | bytes 1572872 | tf_op jit(solution)/shard_map/ppermute | solution.py:22
  49.3 5.0 %collective-permute-start.4 = (bf16[1,128,512]{2,1,0:T(8,128)(2,1)S(1)}, bf16[1,128,512]{2,1,0:T(8,128)(2,1)S(1)}, u32[]{:S(2)}, u32[]{:S(2)}) collective-permute-start(bf16[1,128,512]{2,1,0:T(8,128)(2,1)S(1)} %slice.26), channel_id=1, source_target_pairs={{0,24},{8,0},{16,8},{24,16},{1,25},{9,1},{17,9},{25,17},{2,26},{10... | collective-permute-start | bytes 393224 | tf_op jit(solution)/shard_map/ppermute | solution.py:22
  49.6 5.2 %collective-permute-start.3 = (bf16[1,128,512]{2,1,0:T(8,128)(2,1)S(1)}, bf16[1,128,512]{2,1,0:T(8,128)(2,1)S(1)}, u32[]{:S(2)}, u32[]{:S(2)}) collective-permute-start(bf16[1,128,512]{2,1,0:T(8,128)(2,1)S(1)} %slice.25), channel_id=1, source_target_pairs={{0,8},{8,16},{16,24},{24,0},{1,9},{9,17},{17,25},{25,1},{2,10},{10... | collective-permute-start | bytes 393224 | tf_op jit(solution)/shard_map/ppermute | solution.py:22
  57.3 17.8 %collective-permute-start.9 = (bf16[712,512]{1,0:T(8,128)(2,1)S(1)}, bf16[712,512]{1,0:T(8,128)(2,1)S(1)}, u32[]{:S(2)}, u32[]{:S(2)}) collective-permute-start(bf16[712,512]{1,0:T(8,128)(2,1)S(1)} %get-tuple-element.26), channel_id=1, source_target_pairs={{0,1},{1,0},{2,3},{3,2},{4,5},{5,4},{6,7},{7,6},{8,9},{9,8},{10,11... | collective-permute-start | bytes 2187272 | tf_op jit(solution)/shard_map/ppermute | solution.py:22
  58.4 14.4 %collective-permute-start.21 = (bf16[2,64,2048]{2,1,0:T(8,128)(2,1)S(1)}, bf16[2,64,2048]{2,1,0:T(8,128)(2,1)S(1)}, u32[]{:S(2)}, u32[]{:S(2)}) collective-permute-start(bf16[2,64,2048]{2,1,0:T(8,128)(2,1)S(1)} %bitcast.82), channel_id=1, source_target_pairs={{0,224},{32,0},{64,32},{96,64},{128,96},{160,128},{192,160},{224,1... | collective-permute-start | bytes 1572872 | tf_op jit(solution)/shard_map/ppermute | solution.py:22
  59.6 15.5 %collective-permute-start.20 = (bf16[2,64,2048]{2,1,0:T(8,128)(2,1)S(1)}, bf16[2,64,2048]{2,1,0:T(8,128)(2,1)S(1)}, u32[]{:S(2)}, u32[]{:S(2)}) collective-permute-start(bf16[2,64,2048]{2,1,0:T(8,128)(2,1)S(1)} %bitcast.83), channel_id=1, source_target_pairs={{0,32},{32,64},{64,96},{96,128},{128,160},{160,192},{192,224},{224... | collective-permute-start | bytes 1572872 | tf_op jit(solution)/shard_map/ppermute | solution.py:22
  72.8 17.7 %collective-permute-start.23 = (bf16[2,64,2048]{2,1,0:T(8,128)(2,1)S(1)}, bf16[2,64,2048]{2,1,0:T(8,128)(2,1)S(1)}, u32[]{:S(2)}, u32[]{:S(2)}) collective-permute-start(bf16[2,64,2048]{2,1,0:T(8,128)(2,1)S(1)} %collective-permute-done.21.refs_2_), channel_id=1, source_target_pairs={{0,224},{32,0},{64,32},{96,64},{128,96},{160,128},{192,160},{224,1... | collective-permute-start | bytes 1572872 | tf_op jit(solution)/shard_map/ppermute | solution.py:22
  75.1 18.3 %collective-permute-start.22 = (bf16[2,64,2048]{2,1,0:T(8,128)(2,1)S(1)}, bf16[2,64,2048]{2,1,0:T(8,128)(2,1)S(1)}, u32[]{:S(2)}, u32[]{:S(2)}) collective-permute-start(bf16[2,64,2048]{2,1,0:T(8,128)(2,1)S(1)} %collective-permute-done.20.refs_1_), channel_id=1, source_target_pairs={{0,32},{32,64},{64,96},{96,128},{128,160},{160,192},{192,224},{224... | collective-permute-start | bytes 1572872 | tf_op jit(solution)/shard_map/ppermute | solution.py:22
  75.3 34.3 %copy-start.1 = (f32[2,512,512]{2,1,0:T(8,128)S(1)}, f32[2,512,512]{2,1,0:T(8,128)}, u32[]{:S(2)}) copy-start(f32[2,512,512]{2,1,0:T(8,128)} %x_ref) | copy-start | bytes 6291460
  75.3 24.3 %collective-permute-start.10 = (bf16[448,512]{1,0:T(8,128)(2,1)S(1)}, bf16[448,512]{1,0:T(8,128)(2,1)S(1)}, u32[]{:S(2)}, u32[]{:S(2)}) collective-permute-start(bf16[448,512]{1,0:T(8,128)(2,1)S(1)} %get-tuple-element.28), channel_id=1, source_target_pairs={{0,2},{2,0},{1,3},{3,1},{4,6},{6,4},{5,7},{7,5},{8,10},{10,8},{9,1... | collective-permute-start | bytes 1376264 | tf_op jit(solution)/shard_map/ppermute | solution.py:22
  76.0 12.8 %collective-permute-start.11 = (bf16[72,512]{1,0:T(8,128)(2,1)S(1)}, bf16[72,512]{1,0:T(8,128)(2,1)S(1)}, u32[]{:S(2)}, u32[]{:S(2)}) collective-permute-start(bf16[72,512]{1,0:T(8,128)(2,1)S(1)} %get-tuple-element.30), channel_id=1, source_target_pairs={{0,2},{2,0},{1,3},{3,1},{4,6},{6,4},{5,7},{7,5},{8,10},{10,8},{9,1... | collective-permute-start | bytes 221192 | tf_op jit(solution)/shard_map/ppermute | solution.py:22
  88.8 6.4 %collective-permute-start.14 = (bf16[64,512]{1,0:T(8,128)(2,1)S(1)}, bf16[64,512]{1,0:T(8,128)(2,1)S(1)}, u32[]{:S(2)}, u32[]{:S(2)}) collective-permute-start(bf16[64,512]{1,0:T(8,128)(2,1)S(1)} %get-tuple-element.32.refs_0_), channel_id=1, source_target_pairs={{0,16},{8,24},{16,0},{24,8},{1,17},{9,25},{17,1},{25,9},{2,18},{10... | collective-permute-start | bytes 196616 | tf_op jit(solution)/shard_map/ppermute | solution.py:22
  90.5 12.2 %collective-permute-start.25 = (bf16[2,64,2048]{2,1,0:T(8,128)(2,1)S(1)}, bf16[2,64,2048]{2,1,0:T(8,128)(2,1)S(1)}, u32[]{:S(2)}, u32[]{:S(2)}) collective-permute-start(bf16[2,64,2048]{2,1,0:T(8,128)(2,1)S(1)} %collective-permute-done.23.refs_4_), channel_id=1, source_target_pairs={{0,224},{32,0},{64,32},{96,64},{128,96},{160,128},{192,160},{224,1... | collective-permute-start | bytes 1572872 | tf_op jit(solution)/shard_map/ppermute | solution.py:22
  93.4 12.7 %collective-permute-start.24 = (bf16[2,64,2048]{2,1,0:T(8,128)(2,1)S(1)}, bf16[2,64,2048]{2,1,0:T(8,128)(2,1)S(1)}, u32[]{:S(2)}, u32[]{:S(2)}) collective-permute-start(bf16[2,64,2048]{2,1,0:T(8,128)(2,1)S(1)} %collective-permute-done.22.refs_3_), channel_id=1, source_target_pairs={{0,32},{32,64},{64,96},{96,128},{128,160},{160,192},{192,224},{224... | collective-permute-start | bytes 1572872 | tf_op jit(solution)/shard_map/ppermute | solution.py:22
  93.4 4.8 %collective-permute-start.13 = (bf16[64,512]{1,0:T(8,128)(2,1)S(1)}, bf16[64,512]{1,0:T(8,128)(2,1)S(1)}, u32[]{:S(2)}, u32[]{:S(2)}) collective-permute-start(bf16[64,512]{1,0:T(8,128)(2,1)S(1)} %get-tuple-element.32.refs_0_), channel_id=1, source_target_pairs={{0,24},{8,0},{16,8},{24,16},{1,25},{9,1},{17,9},{25,17},{2,26},{10... | collective-permute-start | bytes 196616 | tf_op jit(solution)/shard_map/ppermute | solution.py:22
  95.2 4.3 %collective-permute-start.12 = (bf16[64,512]{1,0:T(8,128)(2,1)S(1)}, bf16[64,512]{1,0:T(8,128)(2,1)S(1)}, u32[]{:S(2)}, u32[]{:S(2)}) collective-permute-start(bf16[64,512]{1,0:T(8,128)(2,1)S(1)} %get-tuple-element.32.refs_0_), channel_id=1, source_target_pairs={{0,8},{8,16},{16,24},{24,0},{1,9},{9,17},{17,25},{25,1},{2,10},{10... | collective-permute-start | bytes 196616 | tf_op jit(solution)/shard_map/ppermute | solution.py:22
  99.7 14.2 %collective-permute-start.15 = (bf16[704,512]{1,0:T(8,128)(2,1)S(1)}, bf16[704,512]{1,0:T(8,128)(2,1)S(1)}, u32[]{:S(2)}, u32[]{:S(2)}) collective-permute-start(bf16[704,512]{1,0:T(8,128)(2,1)S(1)} %join.1.keep_ref), channel_id=1, source_target_pairs={{0,1},{1,0},{2,3},{3,2},{4,5},{5,4},{6,7},{7,6},{8,9},{9,8},{10,11... | collective-permute-start | bytes 2162696 | tf_op jit(solution)/shard_map/ppermute | solution.py:22
  106.2 7.7 %collective-permute-start.26 = (bf16[1,64,2048]{2,1,0:T(8,128)(2,1)S(1)}, bf16[1,64,2048]{2,1,0:T(8,128)(2,1)S(1)}, u32[]{:S(2)}, u32[]{:S(2)}) collective-permute-start(bf16[1,64,2048]{2,1,0:T(8,128)(2,1)S(1)} %get-tuple-element.40), channel_id=1, source_target_pairs={{0,32},{32,64},{64,96},{96,128},{128,160},{160,192},{192,224},{224... | collective-permute-start | bytes 786440 | tf_op jit(solution)/shard_map/ppermute | solution.py:22
  106.3 7.6 %collective-permute-start.27 = (bf16[1,64,2048]{2,1,0:T(8,128)(2,1)S(1)}, bf16[1,64,2048]{2,1,0:T(8,128)(2,1)S(1)}, u32[]{:S(2)}, u32[]{:S(2)}) collective-permute-start(bf16[1,64,2048]{2,1,0:T(8,128)(2,1)S(1)} %get-tuple-element.41), channel_id=1, source_target_pairs={{0,224},{32,0},{64,32},{96,64},{128,96},{160,128},{192,160},{224,1... | collective-permute-start | bytes 786440 | tf_op jit(solution)/shard_map/ppermute | solution.py:22
